TPU v7x, 32 devices: a whole 2x2x4 slice. The times are simulated.
32 devices in a mesh: sub: 4 (over z), grp: 8 (over y, x, core).
Axes of the slice: x: 2, y: 2, z: 4, core: 2. Of those that a mesh axis runs over, the one named last changes fastest.
Arguments:
- schur: bfloat16 [128, 1024, 1024], P(('sub', 'grp')), as said below
- mortar: bfloat16 [128, 8, 128, 128], P(('sub', 'grp')), may hold values from -0.5 to 0.5
- partner: int32 [128, 4], P(('sub', 'grp')), may hold values from 0 to 15, as said below
- corner_map: int32 [128, 8], P(('sub', 'grp')), may hold values from 0 to 127
- coarse_inv: float32 [4, 128, 128], P('sub'), as said below
- load: float32 [128, 1024, 384], P(('sub', 'grp')), may hold values from -6 to 6
Outputs:
- solution: float32 [128, 1024, 384], P(('sub', 'grp'))
Inputs may be any that keep to these rules, and one draw needn't show every extreme that they name: `partner`: within the 4 subdomains of one device, the entries form a permutation of 0 to 15. `schur`: each matrix is symmetric positive definite. `coarse_inv`: each matrix is symmetric positive definite.
All inputs are finite; a program needn't handle non-finite values.
Results may differ from a plain program's by a relative error of at most 0.0025.
Values may be sent and summed in bfloat16 or wider, within the bound.
No kernel may reach another device: no remote copies, remote signals or barrier semaphores. Data moves between devices by JAX's collectives and lax.ppermute only.
A program may use at most 128 MiB of HBM per device.

v0:
```python
import jax
import jax.numpy as jnp
from jax import lax
from jax.sharding import PartitionSpec as P

ITERS = 2


def shifted(block, axis, distance):
    devices = range(lax.axis_size(axis))
    route = [((i - distance) % len(devices), i) for i in devices]
    return lax.ppermute(block, axis, route)


def face_terms(direction, schur, mortar, partner):
    subdoms = direction.shape[0]
    order = direction.shape[1]
    columns = direction.shape[2]
    faces_all = mortar.shape[1]
    block = mortar.shape[2]
    half_faces = faces_all // 2
    dir_half = direction.astype(jnp.bfloat16)
    stiff = jnp.einsum("sij,sjr->sir", schur, dir_half, preferred_element_type=jnp.float32)
    face_rows = dir_half.reshape(subdoms, faces_all, block, columns)
    traces = jnp.einsum(
        "sfij,sfjr->sfir", mortar, face_rows, preferred_element_type=jnp.float32
    ).astype(jnp.bfloat16)
    upper = traces[:, :half_faces].reshape(subdoms * half_faces, block, columns)
    lower = traces[:, half_faces:].reshape(subdoms * half_faces, block, columns)
    mates = partner.reshape(-1)
    inverse = jnp.argsort(mates)
    reordered = jnp.take(upper, inverse, axis=0)
    lower_mate = shifted(reordered, "sub", 1)
    jump_lower = (lower.astype(jnp.float32) - lower_mate.astype(jnp.float32)).astype(jnp.bfloat16)
    above = shifted(lower, "sub", -1)
    upper_mate = jnp.take(above, mates, axis=0)
    jump_upper = (upper.astype(jnp.float32) - upper_mate.astype(jnp.float32)).astype(jnp.bfloat16)
    jump_all = jnp.concatenate(
        [
            jump_upper.reshape(subdoms, half_faces, block, columns),
            jump_lower.reshape(subdoms, half_faces, block, columns),
        ],
        axis=1,
    )
    pulled = jnp.einsum("sfji,sfjr->sfir", mortar, jump_all, preferred_element_type=jnp.float32)
    return stiff + pulled.reshape(subdoms, order, columns)


def squares(residual):
    return lax.psum(jnp.sum(residual * residual, axis=(0, 1)), ("sub", "grp"))


def on_device(schur, mortar, partner, corner_map, coarse_inv, load):
    order = load.shape[1]
    corner_count = corner_map.shape[1]
    coarse_count = coarse_inv.shape[1]
    stride = order // corner_count
    onehot = (corner_map[..., None] == jnp.arange(coarse_count, dtype=jnp.int32)).astype(
        jnp.float32
    )
    coarse_matrix = coarse_inv[0]
    solution = jnp.zeros_like(load)
    residual = load
    direction = load
    norm_now = squares(residual)
    for step in range(ITERS):
        partial_value = face_terms(direction, schur, mortar, partner)
        corners = direction[:, ::stride, :]
        local_sum = jnp.einsum("sco,scr->or", onehot, corners, precision=lax.Precision.HIGHEST)
        local_dot = jnp.sum(direction * partial_value, axis=(0, 1))
        coarse_sum = lax.psum(local_sum.astype(jnp.bfloat16), "grp").astype(jnp.float32)
        group_dot = lax.psum(local_dot.astype(jnp.bfloat16), "grp").astype(jnp.float32)
        coarse_val = jnp.dot(coarse_matrix, coarse_sum, precision=lax.Precision.HIGHEST)
        corner_add = jnp.einsum("sco,or->scr", onehot, coarse_val, precision=lax.Precision.HIGHEST)
        image = partial_value.at[:, ::stride, :].add(corner_add)
        curvature = lax.psum(group_dot + jnp.sum(coarse_sum * coarse_val, axis=0), "sub")
        image, curvature = (image, curvature)
        step_len = norm_now / curvature
        solution = solution + step_len * direction
        if step + 1 < ITERS:
            residual = residual - step_len * image
            norm_next = squares(residual)
            direction = residual + norm_next / norm_now * direction
            norm_now = norm_next
    return solution


def solution(mesh):
    return jax.shard_map(
        on_device,
        mesh=mesh,
        in_specs=(
            P(("sub", "grp"), None, None),
            P(("sub", "grp"), None, None, None),
            P(("sub", "grp"), None),
            P(("sub", "grp"), None),
            P("sub", None, None),
            P(("sub", "grp"), None, None),
        ),
        out_specs=P(("sub", "grp"), None, None),
        check_vma=False,
    )
```

profile of v0, /device:TPU:0, one launch (start us, length us, event | category | flops | bytes accessed | tf_op | source)
XLA Modules:
  0.0 398.2 jit_solution(7781319759656753900)
XLA Ops:
  6.5 3.2 convert_element_type.76
  9.8 1.0 convolution_convert_fusion
  10.8 1.5 fusion.33
  12.3 5.1 %collective-permute-start = (bf16[16,128,384]{2,1,0:T(8,128)(2,1)}, bf16[16,128,384]{2,1,0:T(8,128)(2,1)}, u32[]{:S(2)}, u32[]{:S(2)}) collective-permute-start(bf16[16,128,384]{2,1,0:T(8,128)(2,1)} %bitcast.2), channel_id=1, source_target_pairs={{8,0},{16,8},{24,16},{0,24},{9,1},{17,9},{25,17},{1,25},{10,2},{18... | collective-permute-start | bytes 4718600 | tf_op jit(solution)/shard_map/ppermute | solution.py:12
  17.5 1.2 sort.19
  18.8 1.9 gather_fusion.1
  20.7 2.8 broadcast_select_fusion.1
  23.5 2.8 slice.20
  26.3 1.0 fusion.17
  27.4 6.6 %copy.8 = f32[4,1024,384]{1,2,0:T(8,128)} copy(f32[4,1024,384]{2,1,0:T(8,128)} %param.13) | data formatting | bytes 12582912 | tf_op args[5]
  34.0 46.9 %all-reduce.3.cloned.1.call-done = bf16[128,384]{1,0:T(8,128)(2,1)} async-done(((bf16[128,384]{1,0:T(8,128)(2,1)}), bf16[128,384]{1,0:T(8,128)(2,1)}) %all-reduce.3.cloned.1.call-update) | async-done | bytes 98320 | tf_op jit(solution)/shard_map/psum | solution.py:71
  81.0 1.2 fusion.21
  82.4 3.3 gather_fusion
  85.8 2.1 subtract_convert_fusion.3
  87.9 2.5 subtract_convert_fusion.2
  90.4 3.7 fusion.5
  94.1 12.9 %multiply_reduce_fusion.1 = (bf16[384]{0:T(512)(128)(2,1)S(1)}, f32[384]{0:T(512)S(1)}, f32[4,1024,384]{2,1,0:T(8,128)}) fusion(f32[4,1024,384]{2,1,0:T(8,128)S(1)} %bitcast.79, f32[4,8,384,128]{2,3,1,0:T(8,128)} %fusion.5, bf16[4,1024,1024]{2,1,0:T(8,128)(2,1)} %param.8), kind=kOutput, calls=%fused_computation.13 | convolution fusion | flops 3230661632 | bytes 27265280 | tf_op jit(solution)/shard_map/sij,sjr->sir/dot_general | solution.py:23
  107.0 12.8 %psum.57 = bf16[384]{0:T(512)(128)(2,1)S(1)} all-reduce(bf16[384]{0:T(512)(128)(2,1)S(1)} %get-tuple-element.8), channel_id=1, replica_groups=mesh['sub'=4,'grp'=8] {'grp'}, use_global_device_ids=true, to_apply=%region_4.6 | all-reduce | flops 384 | bytes 1536 | tf_op jit(solution)/shard_map/psum | solution.py:72
  119.8 11.7 %psum.59 = f32[384]{0:T(512)S(1)} all-reduce(f32[384]{0:T(512)S(1)} %convert_add_fusion.1), channel_id=1, replica_groups=mesh['sub'=4,'grp'=8] {'sub'}, use_global_device_ids=true, to_apply=%region_7.9 | all-reduce | flops 384 | bytes 3072 | tf_op jit(solution)/shard_map/psum | solution.py:76
  131.5 37.0 %psum.56 = f32[384]{0:T(512)S(1)} all-reduce(f32[384]{0:T(512)S(1)} %get-tuple-element.9), channel_id=1, replica_groups=mesh['sub'=4,'grp'=8] {'sub','grp'}, use_global_device_ids=true, to_apply=%region_1.0 | all-reduce | flops 384 | bytes 3072 | tf_op jit(solution)/shard_map/psum | solution.py:50
  168.5 9.5 %copy.10 = f32[4,1024,384]{2,0,1:T(4,128)} copy(f32[4,1024,384]{2,1,0:T(8,128)} %get-tuple-element.16) | data formatting | bytes 12582912 | tf_op jit(solution)/shard_map/add | solution.py:46
  178.0 2.1 scatter_fusion
  180.0 7.6 %copy.12 = f32[4,1024,384]{1,2,0:T(8,128)} copy(f32[4,1024,384]{2,0,1:T(4,128)} %scatter_fusion) | data formatting | bytes 12582912 | tf_op jit(solution)/shard_map/scatter-add | solution.py:75
  187.7 5.6 %multiply_reduce_fusion = f32[384]{0:T(512)S(1)} fusion(f32[4,1024,384]{1,2,0:T(8,128)} %copy.8, f32[4,1024,384]{1,2,0:T(8,128)} %copy.12, f32[384]{0:T(512)S(1)} %div.9), kind=kLoop, calls=%fused_computation.11 | loop fusion | flops 6291072 | bytes 12585984 | tf_op jit(solution)/shard_map/reduce_sum | solution.py:50
  193.3 42.2 %psum.60 = f32[384]{0:T(512)S(1)} all-reduce(f32[384]{0:T(512)S(1)} %multiply_reduce_fusion), channel_id=1, replica_groups=mesh['sub'=4,'grp'=8] {'sub','grp'}, use_global_device_ids=true, to_apply=%region_10.12 | all-reduce | flops 384 | bytes 3072 | tf_op jit(solution)/shard_map/psum | solution.py:50
  235.5 7.7 %convert_bitcast_fusion.1 = (bf16[4,48,8,8,128]{4,3,2,1,0:T(8,128)(2,1)S(1)}, f32[4,1024,384]{1,2,0:T(8,128)}) fusion(f32[4,1024,384]{1,2,0:T(8,128)} %copy.8, f32[384]{0:T(512)S(1)} %div.10, f32[4,1024,384]{1,2,0:T(8,128)} %copy.12, f32[384]{0:T(512)S(1)} %div.9), kind=kLoop, calls=%fused_computation.32 | loop fusion | flops 7864320 | bytes 22023168
  243.2 1.0 convert_bitcast_fusion
  244.2 1.4 fusion.32
  245.6 1.6 collective-permute-start.2
  247.1 1.9 gather_fusion.3
  249.0 2.8 broadcast_select_fusion
  252.3 4.3 %slice.23 = f32[4,8,384]{1,2,0:T(8,128)S(1)} slice(f32[4,1024,384]{1,2,0:T(8,128)} %get-tuple-element.11), slice={[0:4:1], [0:1024:128], [0:384:1]} | slice | bytes 98304 | tf_op jit(solution)/shard_map/slice | solution.py:68
  256.6 1.2 fusion.18
  257.9 53.1 %all-reduce.5.cloned.1.call-done = bf16[128,384]{1,0:T(8,128)(2,1)} async-done(((bf16[128,384]{1,0:T(8,128)(2,1)}), bf16[128,384]{1,0:T(8,128)(2,1)}) %all-reduce.5.cloned.1.call-update) | async-done | bytes 98320 | tf_op jit(solution)/shard_map/psum | solution.py:71
  310.9 1.2 fusion.19
  312.1 2.8 collective-permute-done.2
  314.9 3.3 gather_fusion.2
  318.3 3.2 subtract_convert_fusion.1
  321.4 1.9 copy.16
  323.3 3.4 subtract_convert_fusion
  326.8 2.6 copy.17
  329.3 5.1 %fusion.9 = f32[4,8,384,128]{2,3,1,0:T(8,128)} fusion(bf16[4,8,128,128]{3,2,1,0:T(8,128)(2,1)S(1)} %copy-done, bf16[4,4,128,384]{3,2,1,0:T(8,128)(2,1)} %bitcast.87, bf16[4,4,128,384]{3,2,1,0:T(8,128)(2,1)S(1)} %bitcast.85), kind=kOutput, calls=%fused_computation.22 | convolution fusion | flops 404226048 | bytes 10485760 | tf_op jit(solution)/shard_map/sfji,sfjr->sfir/dot_general | solution.py:45
  334.4 6.5 %copy.27 = f32[4,1024,384]{1,2,0:T(8,128)} copy(f32[4,1024,384]{2,1,0:T(8,128)} %bitcast.80) | data formatting | bytes 12582912 | tf_op jit(solution)/shard_map/reshape | solution.py:46
  340.9 12.5 %fusion.1 = bf16[384]{0:T(512)(128)(2,1)S(1)} fusion(f32[4,1024,384]{1,2,0:T(8,128)} %get-tuple-element.11, f32[4,1024,384]{1,2,0:T(8,128)} %copy.27, bf16[4,1024,1024]{2,1,0:T(8,128)(2,1)} %param.8), kind=kOutput, calls=%fused_computation.8 | convolution fusion | flops 3227516416 | bytes 20972288 | tf_op jit(solution)/shard_map/sij,sjr->sir/dot_general | solution.py:23
  353.5 11.8 %psum.61 = bf16[384]{0:T(512)(128)(2,1)S(1)} all-reduce(bf16[384]{0:T(512)(128)(2,1)S(1)} %fusion.1), channel_id=1, replica_groups=mesh['sub'=4,'grp'=8] {'grp'}, use_global_device_ids=true, to_apply=%region_12.14 | all-reduce | flops 384 | bytes 1536 | tf_op jit(solution)/shard_map/psum | solution.py:72
  365.3 9.9 %psum.63 = f32[384]{0:T(512)S(1)} all-reduce(f32[384]{0:T(512)S(1)} %convert_add_fusion), channel_id=1, replica_groups=mesh['sub'=4,'grp'=8] {'sub'}, use_global_device_ids=true, to_apply=%region_15.17 | all-reduce | flops 384 | bytes 3072 | tf_op jit(solution)/shard_map/psum | solution.py:76
  375.2 9.6 %multiply_add_fusion = f32[4,1024,384]{1,2,0:T(8,128)} fusion(f32[4,1024,384]{1,2,0:T(8,128)} %get-tuple-element.11, f32[4,1024,384]{1,2,0:T(8,128)} %copy.8, f32[384]{0:T(512)S(1)} %div.11, f32[384]{0:T(512)S(1)} %div.9), kind=kLoop, calls=%fused_computation.9 | loop fusion | flops 4718592 | bytes 18877440 | tf_op jit(solution)/shard_map/add | solution.py:79
  384.8 6.6 %copy.21 = f32[4,1024,384]{2,1,0:T(8,128)} copy(f32[4,1024,384]{1,2,0:T(8,128)} %multiply_add_fusion) | data formatting | bytes 12582912 | tf_op jit(solution)/shard_map/add | solution.py:79
  (38 shorter events, 1.0 us)
Async XLA Ops:
  6.5 3.2 copy-start
  6.5 74.4 %all-reduce.3.cloned.1.call-start = ((), (), s32[]{:S(2)}) async-start(), calls=%async_computation | async-start | bytes 196608 | tf_op jit(solution)/shard_map/psum | solution.py:71
  10.8 6.6 %copy-start.3 = (s32[4,4]{1,0:T(4,128)S(1)}, s32[4,4]{1,0:T(4,128)}, u32[]{:S(2)}) copy-start(s32[4,4]{1,0:T(4,128)} %param.10) | copy-start | bytes 196
  12.3 70.1 %collective-permute-start = (bf16[16,128,384]{2,1,0:T(8,128)(2,1)}, bf16[16,128,384]{2,1,0:T(8,128)(2,1)}, u32[]{:S(2)}, u32[]{:S(2)}) collective-permute-start(bf16[16,128,384]{2,1,0:T(8,128)(2,1)} %bitcast.2), channel_id=1, source_target_pairs={{8,0},{16,8},{24,16},{0,24},{9,1},{17,9},{25,17},{1,25},{10,2},{18... | collective-permute-start | bytes 4718600 | tf_op jit(solution)/shard_map/ppermute | solution.py:12
  18.8 7.5 %copy-start.2 = (s32[4,8]{1,0:T(4,128)S(1)}, s32[4,8]{1,0:T(4,128)}, u32[]{:S(2)}) copy-start(s32[4,8]{1,0:T(4,128)} %param.11) | copy-start | bytes 388
  23.5 64.4 %collective-permute-start.1 = (bf16[16,128,384]{2,1,0:T(8,128)(2,1)}, bf16[16,128,384]{2,1,0:T(8,128)(2,1)}, u32[]{:S(2)}, u32[]{:S(2)}) collective-permute-start(bf16[16,128,384]{2,1,0:T(8,128)(2,1)} %broadcast_select_fusion.1), channel_id=1, source_target_pairs={{24,0},{0,8},{8,16},{16,24},{25,1},{1,9},{9,17},{17,25},{26,2},{2,... | collective-permute-start | bytes 4718600 | tf_op jit(solution)/shard_map/ppermute | solution.py:12
  27.3 283.6 %all-reduce.5.cloned.1.call-start = ((), (), s32[]{:S(2)}) async-start(), calls=%async_computation.1 | async-start | bytes 196608 | tf_op jit(solution)/shard_map/psum | solution.py:71
  27.4 53.5 %copy-start.1 = (f32[1,128,128]{2,1,0:T(8,128)S(1)}, f32[1,128,128]{2,1,0:T(8,128)}, u32[]{:S(2)}) copy-start(f32[1,128,128]{2,1,0:T(8,128)} %param.12) | copy-start | bytes 196612
  87.9 6.2 %slice-start = ((s8[6291456]{0:T(1024)(128)(4,1)}), s8[4194304]{0:T(1024)(128)(4,1)S(1)}, s32[]{:S(2)}) async-start(s8[6291456]{0:T(1024)(128)(4,1)} %bitcast.78), calls=%async_computation.2 | async-start | bytes 8388608
  90.4 3.7 slice-start.1
  245.6 69.3 %collective-permute-start.2 = (bf16[16,128,384]{1,2,0:T(8,128)(2,1)}, bf16[16,128,384]{1,2,0:T(8,128)(2,1)}, u32[]{:S(2)}, u32[]{:S(2)}) collective-permute-start(bf16[16,128,384]{1,2,0:T(8,128)(2,1)} %bitcast.16), channel_id=1, source_target_pairs={{8,0},{16,8},{24,16},{0,24},{9,1},{17,9},{25,17},{1,25},{10,2},{18... | collective-permute-start | bytes 4718600 | tf_op jit(solution)/shard_map/ppermute | solution.py:12
  251.8 71.5 %collective-permute-start.3 = (bf16[16,128,384]{1,2,0:T(8,128)(2,1)}, bf16[16,128,384]{1,2,0:T(8,128)(2,1)}, u32[]{:S(2)}, u32[]{:S(2)}) collective-permute-start(bf16[16,128,384]{1,2,0:T(8,128)(2,1)} %broadcast_select_fusion), channel_id=1, source_target_pairs={{24,0},{0,8},{8,16},{16,24},{25,1},{1,9},{9,17},{17,25},{26,2},{2,... | collective-permute-start | bytes 4718600 | tf_op jit(solution)/shard_map/ppermute | solution.py:12
Sparse Core Ops, SparseCore 0:
  27.4 53.4 all-reduce.2
  258.0 52.8 all-reduce.4
where the time goes:
time: 399 us; the launch traced here: 398 us
  blocking collectives  125 us (31%)
  waiting for transfers between devices  103 us (26%)
  local copies, waits for them, and re-layouts  61.9 us (16%)
  other arithmetic  46.2 us (12%)
  matrix products  41.1 us (10%)
  between operations  13.6 us (3%)
  starting transfers between devices  7.15 us (2%)
    psum x2, waiting for transfers between devices, on_device(): lax.psum(local_sum.astype(jnp.bfloat16), 'grp').astype(jnp.float32)  100 us
    psum x2, blocking collectives, squares(): return lax.psum(jnp.sum(residual * residual, axis=(0, 1)), ('sub', 'grp'))  79.2 us
    dot_general x2, matrix products, face_terms(): jnp.einsum('sij,sjr->sir', schur, dir_half, preferred_element_type=jnp.fl...  25.4 us
    psum x2, blocking collectives, on_device(): lax.psum(local_dot.astype(jnp.bfloat16), 'grp').astype(jnp.float32)  24.6 us
    psum x2, blocking collectives, on_device(): lax.psum(group_dot + jnp.sum(coarse_sum * coarse_val, axis=0), 'sub')  21.6 us
    add x1, other arithmetic, on_device(): solution = solution + step_len * direction  9.61 us
    add x1, local copies, waits for them, and re-layouts, face_terms(): return stiff + pulled.reshape(subdoms, order, columns)  9.48 us
    dot_general x2, matrix products, face_terms(): jnp.einsum('sfji,sfjr->sfir', mortar, jump_all, preferred_element_type=jn...  8.78 us
  transfers between devices with their start and end apart: 6, of which 3 were waited for; matrix products, arithmetic and copies ran while one was open for 11% of the time, Pallas kernels for 0%

commit v1 on v0

v1 whole, which is shorter than its diff:
```python
import functools

import jax
import jax.numpy as jnp
from jax import lax
from jax.experimental import pallas as pl
from jax.experimental.pallas import tpu as pltpu
from jax.sharding import PartitionSpec as P

LANES = 128
F32 = jnp.float32
BF16 = jnp.bfloat16


def shifted(block, axis, distance):
    devices = range(lax.axis_size(axis))
    route = [((i - distance) % len(devices), i) for i in devices]
    return lax.ppermute(block, axis, route)


def group_sum(value, axis):
    size = lax.axis_size(axis)
    hop = 1
    while hop < size:
        value = value + lax.ppermute(value, axis, [(i ^ hop, i) for i in range(size)])
        hop *= 2
    return value


def fold_rows(x):
    return jnp.sum(x.reshape(x.shape[0] // 8, 8, x.shape[1]), axis=0)


def smem():
    return pl.BlockSpec(memory_space=pltpu.SMEM)


def whole(shape):
    return pl.BlockSpec(shape, lambda s: (0,) * len(shape))


def first_traces(bounds, partner, cmap, load, mortar, *outs):
    ups, los, norm, csum = outs[: len(bounds)], outs[len(bounds) : 2 * len(bounds)], outs[-2], outs[-1]
    s = pl.program_id(0)
    faces, block = mortar.shape[1], mortar.shape[2]
    half = faces // 2
    corners = cmap.shape[1]
    stride = load.shape[1] // corners

    @pl.when(s == 0)
    def _():
        norm[...] = jnp.zeros_like(norm)
        csum[...] = jnp.zeros_like(csum)

    for f in range(faces):
        rows = load[0, f * block : (f + 1) * block, :]
        norm[...] += fold_rows(rows * rows)
        trace = jnp.dot(mortar[0, f], rows.astype(BF16), preferred_element_type=F32).astype(BF16)
        for (lo, hi), up_ref, lo_ref in zip(bounds, ups, los):
            if f < half:
                up_ref[partner[s, f]] = trace[:, lo:hi]
            else:
                lo_ref[f - half] = trace[:, lo:hi]
    for c in range(corners):
        row = pl.ds(cmap[s, c], 1)
        csum[row, :] += load[0, c * stride : c * stride + 1, :]


def stiff_product(schur, load, out):
    out[0] = jnp.dot(schur[0], load[0].astype(BF16), preferred_element_type=F32)


def first_image(partner, cmap, mortar, stiff, load, up, low, above, below, csum, cinv,
                image, up_out, low_out, jump_out, curv, csum_out, cval):
    s = pl.program_id(0)
    faces, block = mortar.shape[1], mortar.shape[2]
    half = faces // 2
    corners = cmap.shape[1]
    stride = load.shape[1] // corners

    @pl.when(s == 0)
    def _():
        curv[...] = jnp.zeros_like(curv)
        csum_out[...] = jnp.zeros_like(csum_out)
        cval[...] = jnp.dot(cinv[0], csum[...], precision=lax.Precision.HIGHEST, preferred_element_type=F32)

    for f in range(faces):
        if f < half:
            slot = partner[s, f]
            jump = (up[slot].astype(F32) - above[slot].astype(F32)).astype(BF16)
        else:
            jump = (low[f - half].astype(F32) - below[f - half].astype(F32)).astype(BF16)
            jump_out[f - half] = jump
        pulled = lax.dot_general(mortar[0, f], jump, (((0,), (0,)), ((), ())), preferred_element_type=F32)
        rows = slice(f * block, (f + 1) * block)
        image[0, rows, :] = stiff[0, rows, :] + pulled
    for c in range(corners):
        row = pl.ds(cmap[s, c], 1)
        at = slice(c * stride, c * stride + 1)
        value = image[0, at, :] + cval[row, :]
        image[0, at, :] = value
        csum_out[row, :] += value
    for f in range(faces):
        rows = image[0, f * block : (f + 1) * block, :]
        curv[...] += fold_rows(load[0, f * block : (f + 1) * block, :] * rows)
        trace = jnp.dot(mortar[0, f], rows.astype(BF16), preferred_element_type=F32).astype(BF16)
        if f < half:
            up_out[partner[s, f]] = trace
        else:
            low_out[f - half] = trace


def pack_rows(norm, *rest):
    out, curvs = rest[-1], rest[:-1]
    out[...] = jnp.zeros_like(out)
    at = 0
    for ref in (norm,) + curvs:
        for j in range(ref.shape[1] // LANES):
            out[at : at + 1, :] = jnp.sum(ref[:, j * LANES : (j + 1) * LANES], axis=0, keepdims=True)
            at += 1


def step_row(sums, groups, j):
    return sums[j : j + 1, :] / sums[groups + j : groups + j + 1, :]


def residual_sums(bounds, share, sums, schur, load, csum, cinv, *rest):
    count = len(bounds)
    images, csums, norm, energy, resid = rest[:count], rest[count : 2 * count], rest[-3], rest[-2], rest[-1]
    s = pl.program_id(0)
    groups = load.shape[2] // LANES

    def step_of(j):
        return step_row(sums, groups, j)

    @pl.when(s == 0)
    def _():
        norm[...] = jnp.zeros_like(norm)
        for (lo, hi), cs in zip(bounds, csums):
            for j in range(lo // LANES, hi // LANES):
                cols = slice(j * LANES, (j + 1) * LANES)
                own = slice(j * LANES - lo, (j + 1) * LANES - lo)
                coarse = csum[:, cols] - step_of(j) * cs[:, own]
                value = jnp.dot(cinv[0], coarse, precision=lax.Precision.HIGHEST, preferred_element_type=F32)
                energy[:, cols] = share * fold_rows(coarse * value)

    for (lo, hi), image in zip(bounds, images):
        for j in range(lo // LANES, hi // LANES):
            cols = slice(j * LANES, (j + 1) * LANES)
            own = slice(j * LANES - lo, (j + 1) * LANES - lo)
            resid[:, cols] = load[0, :, cols] - step_of(j) * image[0, :, own]
    r = resid[...]
    norm[...] += fold_rows(r * r)
    energy[...] += fold_rows(r * jnp.dot(schur[0], r.astype(BF16), preferred_element_type=F32))


def jump_energy(first, groups, sums, low, recv, jump, out):
    s = pl.program_id(0)

    @pl.when(s == 0)
    def _():
        out[...] = jnp.zeros_like(out)

    for j in range(out.shape[1] // LANES):
        cols = slice(j * LANES, (j + 1) * LANES)
        step = step_row(sums, groups, first + j)
        acc = out[:, cols]
        for k in range(low.shape[0]):
            delta = low[k, :, cols].astype(F32) - recv[k, :, cols].astype(F32)
            value = jump[k, :, cols].astype(F32) - step * delta
            acc += fold_rows(value * value)
        out[:, cols] = acc


def finish(bounds, sums, gathered, load, *rest):
    images, out = rest[:-1], rest[-1]
    groups = load.shape[2] // LANES
    total = jnp.sum(gathered[...], axis=0)
    for (lo, hi), image in zip(bounds, images):
        for j in range(lo // LANES, hi // LANES):
            cols = slice(j * LANES, (j + 1) * LANES)
            own = slice(j * LANES - lo, (j + 1) * LANES - lo)
            norm0 = sums[j : j + 1, :]
            step = step_row(sums, groups, j)
            norm1 = total[j : j + 1, :]
            beta = norm1 / norm0
            curvature = total[groups + j : groups + j + 1, :] - beta * norm1 / step
            step2 = norm1 / curvature
            scale_load = step + step2 * (1.0 + beta)
            scale_image = step2 * step
            out[0, :, cols] = scale_load * load[0, :, cols] - scale_image * image[0, :, own]


def on_device(schur, mortar, partner, corner_map, coarse_inv, load):
    subs, order, columns = load.shape
    faces, block = mortar.shape[1], mortar.shape[2]
    half = faces // 2
    slots = subs * half
    coarse = coarse_inv.shape[1]
    groups = columns // LANES
    cut = columns - LANES if columns > LANES else columns
    bounds = [b for b in ((0, cut), (cut, columns)) if b[1] > b[0]]
    widths = [hi - lo for lo, hi in bounds]
    shape = jax.ShapeDtypeStruct
    params = pltpu.CompilerParams(dimension_semantics=("arbitrary",))

    per_sub = lambda width, at: pl.BlockSpec((1, order, width), lambda s: (s, 0, at))
    mortar_spec = pl.BlockSpec((1, faces, block, block), lambda s: (s, 0, 0, 0))
    schur_spec = pl.BlockSpec((1, order, order), lambda s: (s, 0, 0))
    slot_spec = lambda width: pl.BlockSpec((half, block, width), lambda s: (s, 0, 0))
    faces_of = lambda width: shape((slots, block, width), BF16)
    cinv_spec = whole((1, coarse, coarse))

    first = pl.pallas_call(
        functools.partial(first_traces, bounds),
        grid=(subs,),
        in_specs=[smem(), smem(), per_sub(columns, 0), mortar_spec],
        out_specs=[whole((slots, block, w)) for w in widths]
        + [slot_spec(w) for w in widths]
        + [whole((8, columns)), whole((coarse, columns))],
        out_shape=[faces_of(w) for w in widths] * 2 + [shape((8, columns), F32), shape((coarse, columns), F32)],
        compiler_params=params,
        name="first_traces",
    )(partner, corner_map, load, mortar)
    ups, lows = first[: len(bounds)], first[len(bounds) : 2 * len(bounds)]
    norm_part, csum_part = first[-2], first[-1]

    belows = []
    aboves = []
    for k in range(len(bounds)):
        belows.append(shifted(ups[k], "sub", 1))
        aboves.append(shifted(lows[k], "sub", -1))
    csum = group_sum(csum_part, "grp")

    stiff = pl.pallas_call(
        stiff_product,
        grid=(subs,),
        in_specs=[schur_spec, per_sub(columns, 0)],
        out_specs=per_sub(columns, 0),
        out_shape=shape((subs, order, columns), F32),
        compiler_params=params,
        name="stiff_product",
    )(schur, load)

    images, jumps, low2s, up2s, curvs, csum2s = [], [], [], [], [], []
    for k, (lo, hi) in enumerate(bounds):
        w = hi - lo
        outs = pl.pallas_call(
            first_image,
            grid=(subs,),
            in_specs=[
                smem(), smem(), mortar_spec, per_sub(w, lo // w), per_sub(w, lo // w),
                whole((slots, block, w)), slot_spec(w), whole((slots, block, w)), slot_spec(w),
                pl.BlockSpec((coarse, w), lambda s, at=lo // w: (0, at)), cinv_spec,
            ],
            out_specs=[per_sub(w, 0), whole((slots, block, w)), slot_spec(w), slot_spec(w),
                       whole((8, w)), whole((coarse, w))],
            out_shape=[shape((subs, order, w), F32), faces_of(w), faces_of(w), faces_of(w),
                       shape((8, w), F32), shape((coarse, w), F32)],
            scratch_shapes=[pltpu.VMEM((coarse, w), F32)],
            compiler_params=params,
            name=f"first_image_{k}",
        )(partner, corner_map, mortar, stiff, load, ups[k], lows[k], aboves[k], belows[k], csum, coarse_inv)
        images.append(outs[0])
        up2s.append(outs[1])
        low2s.append(outs[2])
        jumps.append(outs[3])
        curvs.append(outs[4])
        csum2s.append(group_sum(outs[5], "grp"))

    pack = lambda *parts: pl.pallas_call(
        pack_rows, out_shape=shape((8, LANES), F32), name="pack_rows"
    )(*parts)

    part = group_sum(pack(norm_part, *curvs), "grp")
    recvs = [shifted(up2s[k], "sub", 1) for k in range(len(bounds))]
    sums = part
    for d in range(1, lax.axis_size("sub")):
        sums = sums + shifted(part, "sub", d)

    share = 1.0 / lax.axis_size("grp")
    sums_spec = whole((8, LANES))
    norm1, energy = pl.pallas_call(
        functools.partial(residual_sums, bounds, share),
        grid=(subs,),
        in_specs=[sums_spec, schur_spec, per_sub(columns, 0), whole((coarse, columns)), cinv_spec]
        + [per_sub(w, 0) for w in widths]
        + [whole((coarse, w)) for w in widths],
        out_specs=[whole((8, columns)), whole((8, columns))],
        out_shape=[shape((8, columns), F32)] * 2,
        scratch_shapes=[pltpu.VMEM((order, columns), F32)],
        compiler_params=params,
        name="residual_sums",
    )(sums, schur, load, csum, coarse_inv, *images, *csum2s)

    energies = []
    for k, (lo, hi) in enumerate(bounds):
        w = hi - lo
        energies.append(pl.pallas_call(
            functools.partial(jump_energy, lo // LANES, groups),
            grid=(subs,),
            in_specs=[sums_spec, slot_spec(w), slot_spec(w), slot_spec(w)],
            out_specs=whole((8, w)),
            out_shape=shape((8, w), F32),
            compiler_params=params,
            name=f"jump_energy_{k}",
        )(sums, low2s[k], recvs[k], jumps[k]))

    packed = pack(norm1, energy + jnp.concatenate(energies, axis=1))
    devices = lax.axis_size("sub") * lax.axis_size("grp")
    spread = jnp.broadcast_to(packed[None], (devices,) + packed.shape)
    gathered = lax.all_to_all(spread, ("sub", "grp"), 0, 0, tiled=True)

    return pl.pallas_call(
        functools.partial(finish, bounds),
        grid=(subs,),
        in_specs=[sums_spec, whole((devices, 8, LANES)), per_sub(columns, 0)] + [per_sub(w, 0) for w in widths],
        out_specs=per_sub(columns, 0),
        out_shape=shape((subs, order, columns), F32),
        compiler_params=params,
        name="finish",
    )(sums, gathered, load, *images)


def solution(mesh):
    return jax.shard_map(
        on_device,
        mesh=mesh,
        in_specs=(
            P(("sub", "grp"), None, None),
            P(("sub", "grp"), None, None, None),
            P(("sub", "grp"), None),
            P(("sub", "grp"), None),
            P("sub", None, None),
            P(("sub", "grp"), None, None),
        ),
        out_specs=P(("sub", "grp"), None, None),
        check_vma=False,
    )
```

time: 399 us -> 160 us (0.40)
  blocking collectives: 125 us -> 11.4 us
  Pallas kernels: 0 us -> 59.1 us
  local copies, waits for them, and re-layouts: 61.9 us -> 4.28 us
  waiting for transfers between devices: 103 us -> 51 us
  matrix products: 41.1 us -> 0 us
  other arithmetic: 46.2 us -> 6.48 us
  starting transfers between devices: 7.15 us -> 26.5 us
  between operations: 13.6 us -> 0.09 us
    psum x6 -> x0, blocking collectives: 125 us -> none  [the longest x2 79.2 us: squares(): return lax.psum(jnp.sum(residual * residual, axis=(0, 1)), ('sub', 'grp'))]
    psum x2 -> x0, waiting for transfers between devices: 100 us -> none  [on_device(): lax.psum(local_sum.astype(jnp.bfloat16), 'grp').astype(jnp.float32)]
    pallas_call x0 -> x10, Pallas kernels: none -> 59.1 us  [the longest x2 15.6 us: on_device(): pl.pallas_call(first_image, grid=(subs,), in_specs=[smem(), smem(), morta...]
    dot_general x11 -> x0, matrix products: 41.1 us -> none  [the longest x2 25.4 us: face_terms(): jnp.einsum('sij,sjr->sir', schur, dir_half, preferred_element_type=jnp.fl...]
    ppermute x4 -> x9, waiting for transfers between devices: 2.79 us -> 34.4 us  [shifted(): return lax.ppermute(block, axis, route)]
    ppermute x0 -> x12, waiting for transfers between devices: none -> 16.7 us  [group_sum(): lax.ppermute(value, axis, [(i ^ hop, i) for i in range(size)])]
    add x2 -> x0, local copies, waits for them, and re-layouts: 16 us -> none  [the longest x1 9.48 us: face_terms(): return stiff + pulled.reshape(subdoms, order, columns)]
    convert_element_type x5 -> x0, other arithmetic: 14.4 us -> none  [the longest x2 5.93 us: face_terms(): (lower.astype(jnp.float32) - lower_mate.astype(jnp.float32)).astype(jnp.b...]
  transfers between devices with their start and end apart: 6 -> 21, of which waited for: 3 -> 12; matrix products, arithmetic and copies ran while one was open for 11% -> 3% of each run, Pallas kernels for 0% -> 26%
where the time goes in v1:
time: 160 us; the launch traced here: 159 us
  Pallas kernels  59.1 us (37%)
  waiting for transfers between devices  51 us (32%)
  starting transfers between devices  26.5 us (17%)
  blocking collectives  11.4 us (7%)
  other arithmetic  6.48 us (4%)
  local copies, waits for them, and re-layouts  4.28 us (3%)
    ppermute x9, waiting for transfers between devices, shifted(): return lax.ppermute(block, axis, route)  34.4 us
    ppermute x12, waiting for transfers between devices, group_sum(): lax.ppermute(value, axis, [(i ^ hop, i) for i in range(size)])  16.7 us
    pallas_call x2, Pallas kernels, on_device(): pl.pallas_call(first_image, grid=(subs,), in_specs=[smem(), smem(), morta...  15.6 us
    ppermute x9, starting transfers between devices, shifted(): return lax.ppermute(block, axis, route)  15.1 us
    ppermute x12, starting transfers between devices, group_sum(): lax.ppermute(value, axis, [(i ^ hop, i) for i in range(size)])  11.4 us
    all_to_all x1, blocking collectives, on_device(): gathered = lax.all_to_all(spread, ('sub', 'grp'), 0, 0, tiled=True)  11.4 us
    pallas_call x1, Pallas kernels, on_device(): pl.pallas_call(functools.partial(residual_sums, bounds, share), grid=(sub...  10.7 us
    pallas_call x1, Pallas kernels, on_device(): pl.pallas_call(stiff_product, grid=(subs,), in_specs=[schur_spec, per_sub...  10.1 us
  transfers between devices with their start and end apart: 21, of which 12 were waited for; matrix products, arithmetic and copies ran while one was open for 3% of the time, Pallas kernels for 26%

profile of v1, /device:TPU:0, one launch (start us, length us, event | category | flops | bytes accessed | tf_op | source)
XLA Modules:
  0.0 158.9 jit_solution(1283800506882821569)
XLA Ops:
  0.0 5.8 %first_traces.1 = (bf16[16,128,256]{2,1,0:T(8,128)(2,1)}, bf16[16,128,128]{2,1,0:T(8,128)(2,1)}, bf16[16,128,256]{2,1,0:T(8,128)(2,1)}, bf16[16,128,128]{2,1,0:T...) custom-call(s32[4,4]{1,0:T(4,128)} %partner.5, s32[4,8]{1,0:T(4,128)} %cmap.5, f32[4,1024,384]{2,1,0:T(8,128)} %load.11, ...), custom_call_target="tpu_custom_call" | custom-call | tf_op jit(solution)/shard_map/first_traces/pallas_call | solution.py:214
  5.8 5.1 %collective-permute-start = (bf16[16,128,256]{2,1,0:T(8,128)(2,1)}, bf16[16,128,256]{2,1,0:T(8,128)(2,1)S(1)}, u32[]{:S(2)}, u32[]{:S(2)}) collective-permute-start(bf16[16,128,256]{2,1,0:T(8,128)(2,1)} %get-tuple-element.27.low), channel_id=1, source_target_pairs={{8,0},{16,8},{24,16},{0,24},{9,1},{17,9},{25,17},{1,25},{10,2},{18... | collective-permute-start | bytes 3145736 | tf_op jit(solution)/shard_map/ppermute | solution.py:18
  10.9 1.6 %collective-permute-done.2 = f32[128,384]{1,0:T(8,128)S(1)} collective-permute-done((f32[128,384]{1,0:T(8,128)}, f32[128,384]{1,0:T(8,128)S(1)}, u32[]{:S(2)}, u32[]{:S(2)}) %collective-permute-start.2) | collective-permute-done | bytes 196640 | tf_op jit(solution)/shard_map/ppermute | solution.py:25
  12.6 0.9 add.48
  13.5 1.6 collective-permute-start.3
  15.1 5.5 %collective-permute-done.3 = f32[128,384]{1,0:T(8,128)S(1)} collective-permute-done((f32[128,384]{1,0:T(8,128)S(1)}, f32[128,384]{1,0:T(8,128)S(1)}, u32[]{:S(2)}, u32[]{:S(2)}) %collective-permute-start.3) | collective-permute-done | bytes 196640 | tf_op jit(solution)/shard_map/ppermute | solution.py:25
  20.6 1.6 collective-permute-start.4
  22.1 3.8 %collective-permute-start.5 = (bf16[16,128,128]{2,1,0:T(8,128)(2,1)}, bf16[16,128,128]{2,1,0:T(8,128)(2,1)S(1)}, u32[]{:S(2)}, u32[]{:S(2)}) collective-permute-start(bf16[16,128,128]{2,1,0:T(8,128)(2,1)} %get-tuple-element.31.low), channel_id=1, source_target_pairs={{8,0},{16,8},{24,16},{0,24},{9,1},{17,9},{25,17},{1,25},{10,2},{18... | collective-permute-start | bytes 1572872 | tf_op jit(solution)/shard_map/ppermute | solution.py:18
  26.0 10.1 %stiff_product.1.stiff = f32[4,1024,384]{2,1,0:T(8,128)} custom-call(bf16[4,1024,1024]{2,1,0:T(8,128)(2,1)} %schur.3, f32[4,1024,384]{2,1,0:T(8,128)} %load.11), custom_call_target="tpu_custom_call" | custom-call | tf_op jit(solution)/shard_map/stiff_product/pallas_call | solution.py:235
  36.1 0.7 add.50.csum
  36.8 21.3 %collective-permute-done.1.below = bf16[16,128,256]{2,1,0:T(8,128)(2,1)S(1)} collective-permute-done((bf16[16,128,256]{2,1,0:T(8,128)(2,1)}, bf16[16,128,256]{2,1,0:T(8,128)(2,1)S(1)}, u32[]{:S(2)}, u32[]{:S(2)}) %collective-permute-start.1) | collective-permute-done | bytes 1048608 | tf_op jit(solution)/shard_map/ppermute | solution.py:18
  58.1 1.0 copy-done.1
  59.1 9.3 %first_image_0.1 = (f32[4,1024,256]{2,1,0:T(8,128)}, bf16[16,128,256]{2,1,0:T(8,128)(2,1)}, bf16[16,128,256]{2,1,0:T(8,128)(2,1)}, bf16[16,128,256]{2,1,0:T(8,12...) custom-call(s32[4,4]{1,0:T(4,128)} %partner.5, s32[4,8]{1,0:T(4,128)} %cmap.5, bf16[4,8,128,128]{3,2,1,0:T(8,128)(2,1)} %mortar.5, ...), custom_call_target="tpu_custom_call" | custom-call | tf_op jit(solution)/shard_map/first_image_0/pallas_call | solution.py:248
  68.4 1.6 collective-permute-start.19
  70.0 10.5 %collective-permute-done.6.below = bf16[16,128,128]{2,1,0:T(8,128)(2,1)S(1)} collective-permute-done((bf16[16,128,128]{2,1,0:T(8,128)(2,1)}, bf16[16,128,128]{2,1,0:T(8,128)(2,1)S(1)}, u32[]{:S(2)}, u32[]{:S(2)}) %collective-permute-start.6) | collective-permute-done | bytes 524320 | tf_op jit(solution)/shard_map/ppermute | solution.py:18
  80.6 0.8 copy-done.5
  81.4 6.3 %first_image_1.1 = (f32[4,1024,128]{2,1,0:T(8,128)}, bf16[16,128,128]{2,1,0:T(8,128)(2,1)}, bf16[16,128,128]{2,1,0:T(8,128)(2,1)}, bf16[16,128,128]{2,1,0:T(8,12...) custom-call(s32[4,4]{1,0:T(4,128)} %partner.5, s32[4,8]{1,0:T(4,128)} %cmap.5, bf16[4,8,128,128]{3,2,1,0:T(8,128)(2,1)} %mortar.5, ...), custom_call_target="tpu_custom_call" | custom-call | tf_op jit(solution)/shard_map/first_image_1/pallas_call | solution.py:248
  87.7 1.6 %collective-permute-start.20 = (bf16[16,128,128]{2,1,0:T(8,128)(2,1)}, bf16[16,128,128]{2,1,0:T(8,128)(2,1)S(1)}, u32[]{:S(2)}, u32[]{:S(2)}) collective-permute-start(bf16[16,128,128]{2,1,0:T(8,128)(2,1)} %get-tuple-element.43), channel_id=1, source_target_pairs={{24,0},{0,8},{8,16},{16,24},{25,1},{1,9},{9,17},{17,25},{26,2},{2,... | collective-permute-start | bytes 1572872 | tf_op jit(solution)/shard_map/ppermute | solution.py:18
  89.9 1.1 collective-permute-done.16
  91.0 0.8 add.60
  91.8 1.5 collective-permute-start.17
  93.4 0.6 collective-permute-start.14
  94.0 2.3 %collective-permute-done.17 = f32[128,128]{1,0:T(8,128)S(1)} collective-permute-done((f32[128,128]{1,0:T(8,128)S(1)}, f32[128,128]{1,0:T(8,128)S(1)}, u32[]{:S(2)}, u32[]{:S(2)}) %collective-permute-start.17) | collective-permute-done | bytes 65568 | tf_op jit(solution)/shard_map/ppermute | solution.py:25
  96.4 1.6 collective-permute-start.18
  97.9 1.3 pack_rows.2
  99.3 1.4 collective-permute-done.7
  100.6 0.7 add.51
  101.3 2.0 %collective-permute-start.8 = (f32[8,128]{1,0:T(8,128)S(1)}, f32[8,128]{1,0:T(8,128)S(1)}, u32[]{:S(2)}, u32[]{:S(2)}) collective-permute-start(f32[8,128]{1,0:T(8,128)S(1)} %add.51), channel_id=1, source_target_pairs={{2,0},{3,1},{0,2},{1,3},{6,4},{7,5},{4,6},{5,7},{10,8},{11,9},{8,1... | collective-permute-start | bytes 12296 | tf_op jit(solution)/shard_map/ppermute | solution.py:25
  103.3 1.6 %collective-permute-done.8 = f32[8,128]{1,0:T(8,128)S(1)} collective-permute-done((f32[8,128]{1,0:T(8,128)S(1)}, f32[8,128]{1,0:T(8,128)S(1)}, u32[]{:S(2)}, u32[]{:S(2)}) %collective-permute-start.8) | collective-permute-done | bytes 4128 | tf_op jit(solution)/shard_map/ppermute | solution.py:25
  105.5 3.1 %collective-permute-done.9 = f32[8,128]{1,0:T(8,128)S(1)} collective-permute-done((f32[8,128]{1,0:T(8,128)S(1)}, f32[8,128]{1,0:T(8,128)S(1)}, u32[]{:S(2)}, u32[]{:S(2)}) %collective-permute-start.9) | collective-permute-done | bytes 4128 | tf_op jit(solution)/shard_map/ppermute | solution.py:25
  108.6 2.2 %collective-permute-start.12 = (f32[8,128]{1,0:T(8,128)S(1)}, f32[8,128]{1,0:T(8,128)S(1)}, u32[]{:S(2)}, u32[]{:S(2)}) collective-permute-start(f32[8,128]{1,0:T(8,128)S(1)} %add.53), channel_id=1, source_target_pairs={{8,0},{16,8},{24,16},{0,24},{9,1},{17,9},{25,17},{1,25},{10,2},{18... | collective-permute-start | bytes 12296 | tf_op jit(solution)/shard_map/ppermute | solution.py:18
  110.8 0.7 collective-permute-start.10
  111.6 0.6 add.62.rest_3_
  112.5 1.5 collective-permute-start.15
  114.0 1.3 collective-permute-done.11
  115.3 1.0 collective-permute-done.10
  116.3 0.6 add_add_fusion.sums
  116.9 0.8 copy-done.3
  117.7 3.0 %jump_energy_1.1 = f32[8,128]{1,0:T(8,128)} custom-call(f32[8,128]{1,0:T(8,128)} %add_add_fusion.sums, bf16[16,128,128]{2,1,0:T(8,128)(2,1)} %get-tuple-element.42.low, bf16[16,128,128]{2,1,0:T(8,128)(2,1)} %copy-done.3, bf16[16,128,128]{2,1,0:T(8,128)(2,1)} %get-tuple-element.44.jump), custom_call_target="tpu_custom_call" | custom-call | tf_op jit(solution)/shard_map/jump_energy_1/pallas_call | solution.py:299
  120.7 0.7 add.59.rest_2_
  121.3 10.7 %residual_sums.1 = (f32[8,384]{1,0:T(8,128)}, f32[8,384]{1,0:T(8,128)}) custom-call(f32[8,128]{1,0:T(8,128)} %add_add_fusion.sums, bf16[4,1024,1024]{2,1,0:T(8,128)(2,1)} %schur.3, f32[4,1024,384]{2,1,0:T(8,128)} %load.11, f32[128,384]{1,0:T(8,128)} %add.50.csum, f32[1,128,128]{2,1,0:T(8,128)} %cinv.5, f32[4,1024,256]{2,1,0:T(8,128)} %get-tuple-element.33.rest_0_, ...), custom_call_target="tpu_custom_call" | custom-call | tf_op jit(solution)/shard_map/residual_sums/pallas_call | solution.py:283
  132.0 1.0 copy-done.2
  133.0 3.4 %jump_energy_0.1 = f32[8,256]{1,0:T(8,128)} custom-call(f32[8,128]{1,0:T(8,128)} %add_add_fusion.sums, bf16[16,128,256]{2,1,0:T(8,128)(2,1)} %get-tuple-element.39.low, bf16[16,128,256]{2,1,0:T(8,128)(2,1)} %copy-done.2, bf16[16,128,256]{2,1,0:T(8,128)(2,1)} %get-tuple-element.41.jump), custom_call_target="tpu_custom_call" | custom-call | tf_op jit(solution)/shard_map/jump_energy_0/pallas_call | solution.py:299
  136.4 1.3 maximum_add_fusion.rest_0_
  137.7 1.3 pack_rows.3
  139.0 0.7 broadcast_in_dim.2
  139.7 11.4 %all_to_all.5.gathered = f32[32,8,128]{2,1,0:T(8,128)} all-to-all(f32[32,8,128]{2,1,0:T(8,128)S(1)} %broadcast_in_dim.2), channel_id=1, replica_groups=mesh['sub'=4,'grp'=8] {'sub','grp'}, dimensions={0} | all-to-all | bytes 262144 | tf_op jit(solution)/shard_map/all_to_all | solution.py:312
  151.1 7.8 %finish.1 = f32[4,1024,384]{2,1,0:T(8,128)} custom-call(f32[8,128]{1,0:T(8,128)} %add_add_fusion.sums, f32[32,8,128]{2,1,0:T(8,128)} %all_to_all.5.gathered, f32[4,1024,384]{2,1,0:T(8,128)} %load.11, f32[4,1024,256]{2,1,0:T(8,128)} %get-tuple-element.33.rest_0_, f32[4,1024,128]{2,1,0:T(8,128)} %get-tuple-element.34.rest_1_), custom_call_target="tpu_custom_call" | custom-call | tf_op jit(solution)/shard_map/finish/pallas_call | solution.py:314
  (36 shorter events, 1.4 us)
Async XLA Ops:
  5.8 31.0 %collective-permute-start = (bf16[16,128,256]{2,1,0:T(8,128)(2,1)}, bf16[16,128,256]{2,1,0:T(8,128)(2,1)S(1)}, u32[]{:S(2)}, u32[]{:S(2)}) collective-permute-start(bf16[16,128,256]{2,1,0:T(8,128)(2,1)} %get-tuple-element.27.low), channel_id=1, source_target_pairs={{8,0},{16,8},{24,16},{0,24},{9,1},{17,9},{25,17},{1,25},{10,2},{18... | collective-permute-start | bytes 3145736 | tf_op jit(solution)/shard_map/ppermute | solution.py:18
  10.9 47.2 %collective-permute-start.1 = (bf16[16,128,256]{2,1,0:T(8,128)(2,1)}, bf16[16,128,256]{2,1,0:T(8,128)(2,1)S(1)}, u32[]{:S(2)}, u32[]{:S(2)}) collective-permute-start(bf16[16,128,256]{2,1,0:T(8,128)(2,1)} %get-tuple-element.26.up), channel_id=1, source_target_pairs={{24,0},{0,8},{8,16},{16,24},{25,1},{1,9},{9,17},{17,25},{26,2},{2,... | collective-permute-start | bytes 3145736 | tf_op jit(solution)/shard_map/ppermute | solution.py:18
  10.9 1.7 %collective-permute-start.2 = (f32[128,384]{1,0:T(8,128)}, f32[128,384]{1,0:T(8,128)S(1)}, u32[]{:S(2)}, u32[]{:S(2)}) collective-permute-start(f32[128,384]{1,0:T(8,128)} %get-tuple-element.28), channel_id=1, source_target_pairs={{1,0},{0,1},{3,2},{2,3},{5,4},{4,5},{7,6},{6,7},{9,8},{8,9},{11,10... | collective-permute-start | bytes 589832 | tf_op jit(solution)/shard_map/ppermute | solution.py:25
  13.5 7.0 %collective-permute-start.3 = (f32[128,384]{1,0:T(8,128)S(1)}, f32[128,384]{1,0:T(8,128)S(1)}, u32[]{:S(2)}, u32[]{:S(2)}) collective-permute-start(f32[128,384]{1,0:T(8,128)S(1)} %add.48), channel_id=1, source_target_pairs={{2,0},{3,1},{0,2},{1,3},{6,4},{7,5},{4,6},{5,7},{10,8},{11,9},{8,1... | collective-permute-start | bytes 589832 | tf_op jit(solution)/shard_map/ppermute | solution.py:25
  20.6 15.5 %collective-permute-start.4 = (f32[128,384]{1,0:T(8,128)S(1)}, f32[128,384]{1,0:T(8,128)S(1)}, u32[]{:S(2)}, u32[]{:S(2)}) collective-permute-start(f32[128,384]{1,0:T(8,128)S(1)} %add.49), channel_id=1, source_target_pairs={{4,0},{5,1},{6,2},{7,3},{0,4},{1,5},{2,6},{3,7},{12,8},{13,9},{14,... | collective-permute-start | bytes 589832 | tf_op jit(solution)/shard_map/ppermute | solution.py:25
  22.1 47.9 %collective-permute-start.5 = (bf16[16,128,128]{2,1,0:T(8,128)(2,1)}, bf16[16,128,128]{2,1,0:T(8,128)(2,1)S(1)}, u32[]{:S(2)}, u32[]{:S(2)}) collective-permute-start(bf16[16,128,128]{2,1,0:T(8,128)(2,1)} %get-tuple-element.31.low), channel_id=1, source_target_pairs={{8,0},{16,8},{24,16},{0,24},{9,1},{17,9},{25,17},{1,25},{10,2},{18... | collective-permute-start | bytes 1572872 | tf_op jit(solution)/shard_map/ppermute | solution.py:18
  26.0 54.6 %collective-permute-start.6 = (bf16[16,128,128]{2,1,0:T(8,128)(2,1)}, bf16[16,128,128]{2,1,0:T(8,128)(2,1)S(1)}, u32[]{:S(2)}, u32[]{:S(2)}) collective-permute-start(bf16[16,128,128]{2,1,0:T(8,128)(2,1)} %get-tuple-element.30.up), channel_id=1, source_target_pairs={{24,0},{0,8},{8,16},{16,24},{25,1},{1,9},{9,17},{17,25},{26,2},{2,... | collective-permute-start | bytes 1572872 | tf_op jit(solution)/shard_map/ppermute | solution.py:18
  36.8 21.3 %copy-start = (bf16[16,128,256]{2,1,0:T(8,128)(2,1)}, bf16[16,128,256]{2,1,0:T(8,128)(2,1)S(1)}, u32[]{:S(2)}) copy-start(bf16[16,128,256]{2,1,0:T(8,128)(2,1)S(1)} %collective-permute-done.above) | copy-start | bytes 3145732
  58.1 1.0 copy-start.1
  68.4 20.9 %copy-start.6 = (f32[128,256]{1,0:T(8,128)S(1)}, f32[128,256]{1,0:T(8,128)}, u32[]{:S(2)}) copy-start(f32[128,256]{1,0:T(8,128)} %get-tuple-element.35) | copy-start | bytes 393220
  68.4 63.6 %collective-permute-start.19 = (bf16[16,128,256]{2,1,0:T(8,128)(2,1)}, bf16[16,128,256]{2,1,0:T(8,128)(2,1)S(1)}, u32[]{:S(2)}, u32[]{:S(2)}) collective-permute-start(bf16[16,128,256]{2,1,0:T(8,128)(2,1)} %get-tuple-element.40), channel_id=1, source_target_pairs={{24,0},{0,8},{8,16},{16,24},{25,1},{1,9},{9,17},{17,25},{26,2},{2,... | collective-permute-start | bytes 3145736 | tf_op jit(solution)/shard_map/ppermute | solution.py:18
  70.0 10.5 %copy-start.4 = (bf16[16,128,128]{2,1,0:T(8,128)(2,1)}, bf16[16,128,128]{2,1,0:T(8,128)(2,1)S(1)}, u32[]{:S(2)}) copy-start(bf16[16,128,128]{2,1,0:T(8,128)(2,1)S(1)} %collective-permute-done.5.above) | copy-start | bytes 1572868
  80.6 0.8 copy-start.5
  87.7 29.1 %collective-permute-start.20 = (bf16[16,128,128]{2,1,0:T(8,128)(2,1)}, bf16[16,128,128]{2,1,0:T(8,128)(2,1)S(1)}, u32[]{:S(2)}, u32[]{:S(2)}) collective-permute-start(bf16[16,128,128]{2,1,0:T(8,128)(2,1)} %get-tuple-element.43), channel_id=1, source_target_pairs={{24,0},{0,8},{8,16},{16,24},{25,1},{1,9},{9,17},{17,25},{26,2},{2,... | collective-permute-start | bytes 1572872 | tf_op jit(solution)/shard_map/ppermute | solution.py:18
  89.4 4.0 %collective-permute-start.13 = (f32[128,256]{1,0:T(8,128)S(1)}, f32[128,256]{1,0:T(8,128)S(1)}, u32[]{:S(2)}, u32[]{:S(2)}) collective-permute-start(f32[128,256]{1,0:T(8,128)S(1)} %copy-done.6), channel_id=1, source_target_pairs={{1,0},{0,1},{3,2},{2,3},{5,4},{4,5},{7,6},{6,7},{9,8},{8,9},{11,10... | collective-permute-start | bytes 393224 | tf_op jit(solution)/shard_map/ppermute | solution.py:25
  89.4 1.6 %collective-permute-start.16 = (f32[128,128]{1,0:T(8,128)}, f32[128,128]{1,0:T(8,128)S(1)}, u32[]{:S(2)}, u32[]{:S(2)}) collective-permute-start(f32[128,128]{1,0:T(8,128)} %get-tuple-element.36), channel_id=1, source_target_pairs={{1,0},{0,1},{3,2},{2,3},{5,4},{4,5},{7,6},{6,7},{9,8},{8,9},{11,10... | collective-permute-start | bytes 196616 | tf_op jit(solution)/shard_map/ppermute | solution.py:25
  91.8 4.5 %collective-permute-start.17 = (f32[128,128]{1,0:T(8,128)S(1)}, f32[128,128]{1,0:T(8,128)S(1)}, u32[]{:S(2)}, u32[]{:S(2)}) collective-permute-start(f32[128,128]{1,0:T(8,128)S(1)} %add.60), channel_id=1, source_target_pairs={{2,0},{3,1},{0,2},{1,3},{6,4},{7,5},{4,6},{5,7},{10,8},{11,9},{8,1... | collective-permute-start | bytes 196616 | tf_op jit(solution)/shard_map/ppermute | solution.py:25
  93.4 17.4 %collective-permute-start.14 = (f32[128,256]{1,0:T(8,128)S(1)}, f32[128,256]{1,0:T(8,128)S(1)}, u32[]{:S(2)}, u32[]{:S(2)}) collective-permute-start(f32[128,256]{1,0:T(8,128)S(1)} %add.57), channel_id=1, source_target_pairs={{2,0},{3,1},{0,2},{1,3},{6,4},{7,5},{4,6},{5,7},{10,8},{11,9},{8,1... | collective-permute-start | bytes 393224 | tf_op jit(solution)/shard_map/ppermute | solution.py:25
  96.4 14.4 %collective-permute-start.18 = (f32[128,128]{1,0:T(8,128)S(1)}, f32[128,128]{1,0:T(8,128)S(1)}, u32[]{:S(2)}, u32[]{:S(2)}) collective-permute-start(f32[128,128]{1,0:T(8,128)S(1)} %add.61), channel_id=1, source_target_pairs={{4,0},{5,1},{6,2},{7,3},{0,4},{1,5},{2,6},{3,7},{12,8},{13,9},{14,... | collective-permute-start | bytes 196616 | tf_op jit(solution)/shard_map/ppermute | solution.py:25
  99.3 1.4 collective-permute-start.7
  101.3 3.6 %collective-permute-start.8 = (f32[8,128]{1,0:T(8,128)S(1)}, f32[8,128]{1,0:T(8,128)S(1)}, u32[]{:S(2)}, u32[]{:S(2)}) collective-permute-start(f32[8,128]{1,0:T(8,128)S(1)} %add.51), channel_id=1, source_target_pairs={{2,0},{3,1},{0,2},{1,3},{6,4},{7,5},{4,6},{5,7},{10,8},{11,9},{8,1... | collective-permute-start | bytes 12296 | tf_op jit(solution)/shard_map/ppermute | solution.py:25
  104.9 3.6 %collective-permute-start.9 = (f32[8,128]{1,0:T(8,128)S(1)}, f32[8,128]{1,0:T(8,128)S(1)}, u32[]{:S(2)}, u32[]{:S(2)}) collective-permute-start(f32[8,128]{1,0:T(8,128)S(1)} %add.52), channel_id=1, source_target_pairs={{4,0},{5,1},{6,2},{7,3},{0,4},{1,5},{2,6},{3,7},{12,8},{13,9},{14,... | collective-permute-start | bytes 12296 | tf_op jit(solution)/shard_map/ppermute | solution.py:25
  108.6 4.0 %collective-permute-start.12 = (f32[8,128]{1,0:T(8,128)S(1)}, f32[8,128]{1,0:T(8,128)S(1)}, u32[]{:S(2)}, u32[]{:S(2)}) collective-permute-start(f32[8,128]{1,0:T(8,128)S(1)} %add.53), channel_id=1, source_target_pairs={{8,0},{16,8},{24,16},{0,24},{9,1},{17,9},{25,17},{1,25},{10,2},{18... | collective-permute-start | bytes 12296 | tf_op jit(solution)/shard_map/ppermute | solution.py:18
  110.8 4.5 %collective-permute-start.11 = (f32[8,128]{1,0:T(8,128)S(1)}, f32[8,128]{1,0:T(8,128)S(1)}, u32[]{:S(2)}, u32[]{:S(2)}) collective-permute-start(f32[8,128]{1,0:T(8,128)S(1)} %add.53), channel_id=1, source_target_pairs={{16,0},{24,8},{0,16},{8,24},{17,1},{25,9},{1,17},{9,25},{18,2},{26... | collective-permute-start | bytes 12296 | tf_op jit(solution)/shard_map/ppermute | solution.py:18
  110.8 5.5 %collective-permute-start.10 = (f32[8,128]{1,0:T(8,128)S(1)}, f32[8,128]{1,0:T(8,128)S(1)}, u32[]{:S(2)}, u32[]{:S(2)}) collective-permute-start(f32[8,128]{1,0:T(8,128)S(1)} %add.53), channel_id=1, source_target_pairs={{24,0},{0,8},{8,16},{16,24},{25,1},{1,9},{9,17},{17,25},{26,2},{2,... | collective-permute-start | bytes 12296 | tf_op jit(solution)/shard_map/ppermute | solution.py:18
  112.5 8.2 %collective-permute-start.15 = (f32[128,256]{1,0:T(8,128)S(1)}, f32[128,256]{1,0:T(8,128)S(1)}, u32[]{:S(2)}, u32[]{:S(2)}) collective-permute-start(f32[128,256]{1,0:T(8,128)S(1)} %add.58), channel_id=1, source_target_pairs={{4,0},{5,1},{6,2},{7,3},{0,4},{1,5},{2,6},{3,7},{12,8},{13,9},{14,... | collective-permute-start | bytes 393224 | tf_op jit(solution)/shard_map/ppermute | solution.py:25
  116.9 0.8 copy-start.3
  121.3 15.0 %copy-start.7 = (f32[8,128]{1,0:T(8,128)S(1)}, f32[8,128]{1,0:T(8,128)}, u32[]{:S(2)}) copy-start(f32[8,128]{1,0:T(8,128)} %jump_energy_1.1) | copy-start | bytes 12292
  132.0 1.0 copy-start.2

commit v2 on v0

v2 whole, which is shorter than its diff:
```python
import functools

import jax
import jax.numpy as jnp
from jax import lax
from jax.experimental import pallas as pl
from jax.experimental.pallas import tpu as pltpu
from jax.sharding import PartitionSpec as P


LANES = 128
F32 = jnp.float32
BF16 = jnp.bfloat16


def shifted(block, axis, distance):
    devices = range(lax.axis_size(axis))
    route = [((i - distance) % len(devices), i) for i in devices]
    return lax.ppermute(block, axis, route)


def group_sum(value, axis):
    size = lax.axis_size(axis)
    hop = 1
    while hop < size:
        value = value + lax.ppermute(value, axis, [(i ^ hop, i) for i in range(size)])
        hop *= 2
    return value


def hub_sum(value, axis):
    size = lax.axis_size(axis)
    hub = size - 1
    total = value
    for i in range(hub):
        total = total + lax.ppermute(value, axis, [(i, hub)])
    others = [lax.ppermute(total, axis, [(hub, i)]) for i in range(hub)]
    return [total] + others


def fold_rows(x):
    return jnp.sum(x.reshape(x.shape[0] // 8, 8, x.shape[1]), axis=0)


def vmem(x):
    return pltpu.with_memory_space_constraint(x, pltpu.VMEM)


def hbm(x):
    return pltpu.with_memory_space_constraint(x, pltpu.HBM)


VMEM = pl.BlockSpec(memory_space=pltpu.VMEM)
ANY = pl.BlockSpec(memory_space=pl.ANY)


def row_sum(x):
    return jnp.sum(x, axis=0, keepdims=True)


def group_cols(j):
    return slice(j * LANES, (j + 1) * LANES)


def fetch_tables(partner_hbm, cmap_hbm, partner, cmap, sems):
    return [
        pltpu.make_async_copy(partner_hbm, partner, sems.at[0]),
        pltpu.make_async_copy(cmap_hbm, cmap, sems.at[1]),
    ]


def first_traces(lo, copies, partner_hbm, cmap_hbm, load_hbm, mortar_in, *refs):
    if copies:
        load, mortar, up, low, norm, csum, partner, cmap, sems = refs
    else:
        load, up, low, norm, csum, partner, cmap, sems = refs
        mortar = mortar_in
    subs, order, width = load.shape
    faces, block = mortar.shape[1], mortar.shape[2]
    half = faces // 2
    corners = cmap.shape[1]
    stride = order // corners

    def fetch(s):
        moves = [pltpu.make_async_copy(load_hbm.at[s, :, pl.ds(lo, width)], load.at[s], sems.at[0, s])]
        if copies:
            moves.append(pltpu.make_async_copy(mortar_in.at[s], mortar.at[s], sems.at[1, s]))
        return moves

    tables = fetch_tables(partner_hbm, cmap_hbm, partner, cmap, sems.at[2])
    for move in tables:
        move.start()
    for s in range(subs):
        for move in fetch(s):
            move.start()
    norm[...] = jnp.zeros_like(norm)
    csum[...] = jnp.zeros_like(csum)
    for move in tables:
        move.wait()
    for s in range(subs):
        for move in fetch(s):
            move.wait()
        for f in range(faces):
            rows = load[s, f * block : (f + 1) * block, :]
            norm[...] += fold_rows(rows * rows)
            trace = jnp.dot(mortar[s, f], rows.astype(BF16), preferred_element_type=F32).astype(BF16)
            if f < half:
                up[partner[s, f]] = trace
            else:
                low[s * half + f - half] = trace
        for c in range(corners):
            row = pl.ds(cmap[s, c], 1)
            csum[row, :] += load[s, c * stride : c * stride + 1, :]


def stiff_product(schur_hbm, mortar, *refs):
    loads, (out_a, out_b, schur, flipped, sems) = refs[:-5], refs[-5:]
    subs = schur.shape[0]

    def fetch(s):
        return pltpu.make_async_copy(schur_hbm.at[s], schur.at[s], sems.at[s])

    for s in range(subs):
        fetch(s).start()

    def work(s, _):
        fetch(s).wait()
        value = jnp.concatenate([load[s].astype(BF16) for load in loads], axis=1)
        product = jnp.dot(schur[s], value, preferred_element_type=F32)
        out_a[s] = product[:, : out_a.shape[2]]
        out_b[s] = product[:, out_a.shape[2] :]
        for f in range(mortar.shape[1]):
            flipped[s, f] = mortar[s, f].T
        return 0

    lax.fori_loop(0, subs, work, 0)


def first_image(lo, pieces, groups, share, partner_hbm, cmap_hbm, mortar, flipped, stiff, csum, cinv, *refs):
    ins, earlier, refs = refs[: 6 * pieces], refs[6 * pieces], refs[6 * pieces + 1 :]
    loads, norms, ups, lows, aboves, belows = (ins[i * pieces : (i + 1) * pieces] for i in range(6))
    up_cuts, refs = refs[1:-8], refs[:1] + refs[-8:]
    image, low_out, jump_out, sums, cval, up_out, partner, cmap, sems = refs
    subs, order, width = image.shape
    faces, block = mortar.shape[1], mortar.shape[2]
    half = faces // 2
    corners = cmap.shape[1]
    coarse = csum.shape[0]
    stride = order // corners
    cols = slice(lo, lo + width)
    tables = fetch_tables(partner_hbm, cmap_hbm, partner, cmap, sems)
    for move in tables:
        move.start()
    sums[...] = jnp.zeros_like(sums)
    cval[...] = jnp.dot(cinv[0], csum[:, cols], precision=lax.Precision.HIGHEST, preferred_element_type=F32)
    for move in tables:
        move.wait()

    def difference(own, other, slot):
        return jnp.concatenate(
            [(a[slot].astype(F32) - b[slot].astype(F32)).astype(BF16) for a, b in zip(own, other)], axis=1
        )

    def work(s, curv):
        for f in range(faces):
            if f < half:
                jump = difference(ups, aboves, partner[s, f])
            else:
                jump = difference(lows, belows, s * half + f - half)
                jump_out[s * half + f - half] = jump
            pulled = jnp.dot(flipped[s, f], jump, preferred_element_type=F32)
            rows = slice(f * block, (f + 1) * block)
            image[s, rows, :] = stiff[s, rows, :] + pulled
        for c in range(corners):
            row = pl.ds(cmap[s, c], 1)
            at = slice(c * stride, c * stride + 1)
            value = image[s, at, :] + cval[row, :]
            image[s, at, :] = value
            sums[row, :] += value
        for f in range(faces):
            at = slice(f * block, (f + 1) * block)
            rows = image[s, at, :]
            curv = tuple(
                acc + fold_rows(load[s, at, :] * rows[:, group_cols(j)])
                for j, (acc, load) in enumerate(zip(curv, loads))
            )
            trace = jnp.dot(mortar[s, f], rows.astype(BF16), preferred_element_type=F32).astype(BF16)
            if f < half:
                up_out[partner[s, f]] = trace
            else:
                low_out[s * half + f - half] = trace
        return curv

    curv = lax.fori_loop(0, subs, work, tuple(jnp.zeros((8, LANES), F32) for _ in loads))
    at = 0
    for cut in up_cuts:
        cut[...] = up_out[at : at + cut.shape[0]]
        at += cut.shape[0]
    first = lo // LANES
    for j in range(pieces):
        for row, value in ((first + j, norms[j][...]), (groups + first + j, curv[j])):
            sums[coarse + row : coarse + row + 1, :LANES] = row_sum(value)
    for j in range(first):
        for row in (j, groups + j):
            at = slice(coarse + row, coarse + row + 1)
            sums[at, :] = share * earlier[at, :LANES]


def residual_sums(share, hops, groups, *refs):
    parts, refs = refs[:hops], refs[hops:]
    schur, csum, cinv, csum_a, csum_b, image_a, image_b = refs[:7]
    loads, (total, norm, energy, resid) = refs[7 : 7 + groups], refs[7 + groups :]
    coarse = csum.shape[0]
    value = jnp.where(lax.axis_index("sub") == hops - 1, parts[0][...], 0.0)
    for ref in parts[1:]:
        value += ref[...]
    for j in range(groups):
        total[0:1, group_cols(j)] = value[j : j + 1, :]
        total[1:2, group_cols(j)] = value[groups + j : groups + j + 1, :]
    step = total[0:1, :] / total[1:2, :]
    inner = jnp.concatenate([csum_a[:coarse, :], csum_b[:coarse, :]], axis=1)
    change = csum[...] - step * inner
    field = jnp.dot(cinv[0], change, precision=lax.Precision.HIGHEST, preferred_element_type=F32)
    norm[...] = jnp.zeros_like(norm)
    energy[...] = share * fold_rows(change * field)

    def work(s, _):
        for j, load in enumerate(loads):
            cols = group_cols(j)
            image, own = (image_a, cols) if j + 1 < groups else (image_b, group_cols(0))
            resid[:, cols] = load[s] - step[:, cols] * image[s, :, own]
        r = resid[...]
        norm[...] += fold_rows(r * r)
        energy[...] += fold_rows(r * jnp.dot(schur[s], r.astype(BF16), preferred_element_type=F32))
        return 0

    lax.fori_loop(0, schur.shape[0], work, 0)


def jump_squares(step, low, jump, recvs, cols):
    start, acc = 0, jnp.zeros((8, LANES), F32)
    for recv in recvs:

        def one(k, acc, recv=recv, start=start):
            delta = low[start + k, :, cols].astype(F32) - recv[k, :, cols].astype(F32)
            value = jump[start + k, :, cols].astype(F32) - step * delta
            return acc + fold_rows(value * value)

        acc = lax.fori_loop(0, recv.shape[0], one, acc, unroll=2)
        start += recv.shape[0]
    return acc


def add_jumps(total, energy, low, jump, *refs):
    recvs, out = refs[:-1], refs[-1]
    wide = low.shape[2]
    out[:, wide:] = energy[:, wide:]
    for j in range(wide // LANES):
        cols = group_cols(j)
        step = total[0:1, cols] / total[1:2, cols]
        out[:, cols] = energy[:, cols] + jump_squares(step, low, jump, recvs, cols)


def last_sums(total, norm, energy, low, jump, *refs):
    recvs, out = refs[:-1], refs[-1]
    groups = norm.shape[1] // LANES
    last = group_cols(groups - 1)
    rows = [row_sum(norm[:, group_cols(j)]) for j in range(groups)]
    rows += [row_sum(energy[:, group_cols(j)]) for j in range(groups - 1)]
    step = total[0:1, last] / total[1:2, last]
    rows.append(row_sum(energy[:, last] + jump_squares(step, low, jump, recvs, group_cols(0))))
    rows.append(jnp.zeros((8 - len(rows), LANES), F32))
    out[...] = jnp.broadcast_to(jnp.concatenate(rows, axis=0)[None], out.shape)


def finish(total, gathered, *refs):
    loads, (image_a, image_b, out_hbm, stage, sems) = refs[:-5], refs[-5:]
    groups = len(loads)
    subs = stage.shape[0]
    second = jnp.sum(gathered[...], axis=0)

    def send(s):
        return pltpu.make_async_copy(stage.at[s], out_hbm.at[s], sems.at[s])

    scales = []
    for j in range(groups):
        norm0 = total[0:1, group_cols(j)]
        step = norm0 / total[1:2, group_cols(j)]
        norm1 = second[j : j + 1, :]
        beta = norm1 / norm0
        step2 = norm1 / (second[groups + j : groups + j + 1, :] - beta * norm1 / step)
        scales.append((step + step2 * (1.0 + beta), step2 * step))
    for s in range(subs):
        for j in range(groups):
            image, cols = (image_a, group_cols(j)) if j + 1 < groups else (image_b, group_cols(0))
            stage[s, :, group_cols(j)] = scales[j][0] * loads[j][s] - scales[j][1] * image[s, :, cols]
        send(s).start()
    for s in range(subs):
        send(s).wait()


def call(kernel, in_specs, outs, scratch=(), limit=5, in_hbm=(), alias=None):
    return pl.pallas_call(
        kernel,
        in_specs=in_specs,
        out_specs=[ANY if i in in_hbm else VMEM for i in range(len(outs))],
        out_shape=outs,
        scratch_shapes=list(scratch),
        input_output_aliases=alias or {},
        compiler_params=pltpu.CompilerParams(vmem_limit_bytes=limit * 2**20),
    )


def iterate(schur, mortar, partner, corner_map, coarse_inv, load):
    subs, order, columns = load.shape
    faces, block = mortar.shape[1], mortar.shape[2]
    half = faces // 2
    slots = subs * half
    coarse = coarse_inv.shape[1]
    groups = columns // LANES
    dma = pltpu.SemaphoreType.DMA
    table_scratch = [pltpu.SMEM(partner.shape, partner.dtype), pltpu.SMEM(corner_map.shape, corner_map.dtype)]
    tables = (hbm(partner), hbm(corner_map))

    def traces_of(width):
        return pltpu.VMEM((slots, block, width), BF16)

    loads, norms, ups, lows, csums, aboves, belows = [], [], [], [], [], [], []
    held_mortar = hbm(mortar)
    for j in range(groups):
        outs = [pltpu.VMEM((subs, order, LANES), F32)]
        if j == 0:
            outs.append(pltpu.VMEM(mortar.shape, BF16))
        outs += [traces_of(LANES)] * 2 + [pltpu.VMEM((8, LANES), F32), pltpu.VMEM((coarse, LANES), F32)]
        got = list(call(
            functools.partial(first_traces, j * LANES, j == 0),
            [ANY, ANY, ANY, ANY if j == 0 else VMEM], outs, table_scratch + [dma((3, max(subs, 2)))],
        )(*tables, hbm(load), held_mortar))
        loads.append(vmem(got.pop(0)))
        if j == 0:
            held_mortar = vmem(got.pop(0))
        belows.append(vmem(shifted(got[0], "sub", 1)))
        aboves.append(vmem(shifted(got[1], "sub", -1)))
        ups.append(vmem(got[0]))
        lows.append(vmem(got[1]))
        norms.append(vmem(got[2]))
        csums.append(got[3])
    csum = vmem(group_sum(jnp.concatenate(csums, axis=1), "grp"))

    *stiff, held_schur, flipped = call(
        stiff_product, [ANY] + [VMEM] * (1 + groups),
        [pltpu.VMEM((subs, order, w), F32) for w in (columns - LANES, LANES)]
        + [pltpu.VMEM(schur.shape, BF16), pltpu.VMEM(mortar.shape, BF16)], [dma((subs,))],
    )(hbm(schur), held_mortar, *loads)
    held_schur, flipped = vmem(held_schur), vmem(flipped)

    bounds = ((0, groups - 1), (groups - 1, groups))
    share = 1.0 / lax.axis_size("grp")
    images, jumps, low2s, recvs, csum2s = [], [], [], [], []
    cuts = ((slots - slots // 8, slots // 8), (5 * slots // 16, slots - 5 * slots // 16))
    for k, (lo, hi) in enumerate(bounds):
        n, w = hi - lo, (hi - lo) * LANES
        pick = [x[lo:hi] for x in (loads, norms, ups, lows, aboves, belows)]
        got = call(
            functools.partial(first_image, lo * LANES, n, groups, share),
            [ANY, ANY] + [VMEM] * (6 + 6 * n),
            [pltpu.VMEM((subs, order, w), F32)]
            + [pltpu.VMEM((size, block, w), BF16) for size in cuts[k]]
            + [traces_of(w)] * 2 + [pltpu.VMEM((coarse + 8, w), F32)],
            [pltpu.VMEM((coarse, w), F32), traces_of(w)] + table_scratch + [dma((2,))], alias={4: 0},
        )(*tables, held_mortar, flipped, vmem(stiff[k]), csum, coarse_inv, *sum(pick, []), csum2s[0] if k else csum)
        image, *up2, low2, jump, sums = got
        images.append(vmem(image))
        low2s.append(vmem(low2))
        jumps.append(vmem(jump))
        sums = group_sum(sums, "grp")
        if not k:
            csum, sums = lax.optimization_barrier((csum, sums))
            csum = vmem(csum)
        csum2s.append(vmem(sums))
        recvs.append([])
        for piece in up2:
            recvs[-1].append(vmem(shifted(piece, "sub", 1)))

    totals = [vmem(x) for x in hub_sum(sums[coarse:], "sub")]
    hops = len(totals)
    total, norm1, energy = call(
        functools.partial(residual_sums, share, hops, groups),
        [VMEM] * (hops + 7 + groups), [pltpu.VMEM((8, columns), F32)] * 3, [pltpu.VMEM((order, columns), F32)],
    )(*totals, held_schur, csum, coarse_inv, *csum2s, *images, *loads)
    total, norm1 = vmem(total), vmem(norm1)
    energy = vmem(call(
        add_jumps, [VMEM] * (4 + len(recvs[0])), [pltpu.VMEM(energy.shape, F32)],
    )(total, vmem(energy), low2s[0], jumps[0], *recvs[0])[0])

    devices = lax.axis_size("sub") * lax.axis_size("grp")
    spread = call(
        last_sums, [VMEM] * (5 + len(recvs[1])), [pltpu.VMEM((devices, 8, LANES), F32)],
    )(total, norm1, energy, low2s[1], jumps[1], *recvs[1])[0]
    gathered = lax.all_to_all(spread, ("sub", "grp"), 0, 0, tiled=True)

    return call(
        finish, [VMEM] * (4 + groups),
        [jax.ShapeDtypeStruct((subs, order, columns), F32)],
        [pltpu.VMEM((subs, order, columns), F32), dma((subs,))], limit=9, in_hbm=(0,),
    )(total, vmem(gathered), *loads, *images)[0]


def solution(mesh):
    return jax.shard_map(
        iterate,
        mesh=mesh,
        in_specs=(
            P(("sub", "grp"), None, None),
            P(("sub", "grp"), None, None, None),
            P(("sub", "grp"), None),
            P(("sub", "grp"), None),
            P("sub", None, None),
            P(("sub", "grp"), None, None),
        ),
        out_specs=P(("sub", "grp"), None, None),
        check_vma=False,
    )
```

time: 399 us -> 144 us (0.36)
  blocking collectives: 125 us -> 14.4 us
  local copies, waits for them, and re-layouts: 61.9 us -> 0.03 us
  other arithmetic: 46.2 us -> 0.18 us
  matrix products: 41.1 us -> 0 us
  waiting for transfers between devices: 103 us -> 65.2 us
  Pallas kernels: 0 us -> 29 us
  starting transfers between devices: 7.15 us -> 34.2 us
  between operations: 13.6 us -> 0.25 us
    psum x6 -> x0, blocking collectives: 125 us -> none  [the longest x2 79.2 us: squares(): return lax.psum(jnp.sum(residual * residual, axis=(0, 1)), ('sub', 'grp'))]
    psum x2 -> x0, waiting for transfers between devices: 100 us -> none  [on_device(): lax.psum(local_sum.astype(jnp.bfloat16), 'grp').astype(jnp.float32)]
    dot_general x11 -> x0, matrix products: 41.1 us -> none  [the longest x2 25.4 us: face_terms(): jnp.einsum('sij,sjr->sir', schur, dir_half, preferred_element_type=jnp.fl...]
    ppermute x0 -> x15, waiting for transfers between devices: none -> 36.5 us  [the longest x9 19.3 us: group_sum(): lax.ppermute(value, axis, [(i ^ hop, i) for i in range(size)])]
    pallas_call x0 -> x10, Pallas kernels: none -> 29 us  [the longest x1 6.66 us: iterate(): call(stiff_product, [ANY] + [VMEM] * (1 + groups), [pltpu.VMEM((subs, ord...]
    ppermute x4 -> x10, waiting for transfers between devices: 2.79 us -> 28.7 us  [shifted(): return lax.ppermute(block, axis, route)]
    ppermute x0 -> x15, starting transfers between devices: none -> 17.8 us  [the longest x9 10.1 us: group_sum(): lax.ppermute(value, axis, [(i ^ hop, i) for i in range(size)])]
    add x2 -> x0, local copies, waits for them, and re-layouts: 16 us -> none  [the longest x1 9.48 us: face_terms(): return stiff + pulled.reshape(subdoms, order, columns)]
  transfers between devices with their start and end apart: 6 -> 25, of which waited for: 3 -> 14; matrix products, arithmetic and copies ran while one was open for 11% -> 0% of each run, Pallas kernels for 0% -> 14%
where the time goes in v2:
time: 144 us; the launch traced here: 143 us
  waiting for transfers between devices  65.2 us (45%)
  starting transfers between devices  34.2 us (24%)
  Pallas kernels  29 us (20%)
  blocking collectives  14.4 us (10%)
    ppermute x10, waiting for transfers between devices, shifted(): return lax.ppermute(block, axis, route)  28.7 us
    ppermute x9, waiting for transfers between devices, group_sum(): lax.ppermute(value, axis, [(i ^ hop, i) for i in range(size)])  19.3 us
    ppermute x10, starting transfers between devices, shifted(): return lax.ppermute(block, axis, route)  16.4 us
    all_to_all x1, blocking collectives, iterate(): gathered = lax.all_to_all(spread, ('sub', 'grp'), 0, 0, tiled=True)  14.4 us
    ppermute x9, starting transfers between devices, group_sum(): lax.ppermute(value, axis, [(i ^ hop, i) for i in range(size)])  10.1 us
    ppermute x3, waiting for transfers between devices, hub_sum(): others = [lax.ppermute(total, axis, [(hub, i)]) for i in range(hub)]  9.15 us
    ppermute x3, waiting for transfers between devices, hub_sum(): total = total + lax.ppermute(value, axis, [(i, hub)])  8.04 us
    pallas_call x1, Pallas kernels, iterate(): call(stiff_product, [ANY] + [VMEM] * (1 + groups), [pltpu.VMEM((subs, ord...  6.66 us
  transfers between devices with their start and end apart: 25, of which 14 were waited for; matrix products, arithmetic and copies ran while one was open for 0% of the time, Pallas kernels for 14%

profile of v2, /device:TPU:0, one launch (start us, length us, event | category | flops | bytes accessed | tf_op | source)
XLA Modules:
  0.0 143.3 jit_solution(2078542264681515792)
XLA Ops:
  0.0 2.2 %shard_map.64 = (f32[4,1024,128]{2,1,0:T(8,128)S(1)}, bf16[4,8,128,128]{3,2,1,0:T(8,128)(2,1)S(1)}, bf16[16,128,128]{2,1,0:T(8,128)(2,1)S(1)}, bf16[16,128,128]{...) custom-call(s32[4,4]{1,0:T(4,128)} %partner_hbm.9, s32[4,8]{1,0:T(4,128)} %cmap_hbm.9, ...), custom_call_target="tpu_custom_call" | custom-call | tf_op jit(solution)/shard_map/pallas_call | solution.py:335
  2.2 2.1 %shard_map.65 = (f32[4,1024,128]{2,1,0:T(8,128)S(1)}, bf16[16,128,128]{2,1,0:T(8,128)(2,1)S(1)}, bf16[16,128,128]{2,1,0:T(8,128)(2,1)S(1)}, f32[8,128]{1,0:T(8,128)S(1)}, f32[128,128]{1,0:T(8,128)S(1)}) custom-call(s32[4,4]{1,0:T(4,128)} %partner_hbm.9, s32[4,8]{1,0:T(4,128)} %cmap_hbm.9, f32[4,1024,384]{2,1,0:T(8,128)} %load_hbm.5, ...), custom_call_target="tpu_custom_call" | custom-call | tf_op jit(solution)/shard_map/pallas_call | solution.py:335
  4.3 2.0 %shard_map.66 = (f32[4,1024,128]{2,1,0:T(8,128)S(1)}, bf16[16,128,128]{2,1,0:T(8,128)(2,1)S(1)}, bf16[16,128,128]{2,1,0:T(8,128)(2,1)S(1)}, f32[8,128]{1,0:T(8,128)S(1)}, f32[128,128]{1,0:T(8,128)S(1)}) custom-call(s32[4,4]{1,0:T(4,128)} %partner_hbm.9, s32[4,8]{1,0:T(4,128)} %cmap_hbm.9, f32[4,1024,384]{2,1,0:T(8,128)} %load_hbm.5, ...), custom_call_target="tpu_custom_call" | custom-call | tf_op jit(solution)/shard_map/pallas_call | solution.py:335
  6.4 0.6 collective-permute-start
  6.9 4.7 %collective-permute-start.4 = (bf16[16,128,128]{2,1,0:T(8,128)(2,1)S(1)}, bf16[16,128,128]{2,1,0:T(8,128)(2,1)S(1)}, u32[]{:S(2)}, u32[]{:S(2)}) collective-permute-start(bf16[16,128,128]{2,1,0:T(8,128)(2,1)S(1)} %get-tuple-element.57.refs_7_), channel_id=1, source_target_pairs={{8,0},{16,8},{24,16},{0,24},{9,1},{17,9},{25,17},{1,25},{10,2},{18... | collective-permute-start | bytes 1572872 | tf_op jit(solution)/shard_map/ppermute | solution.py:19
  11.6 0.0 collective-permute-start.6
  11.6 3.8 %collective-permute-start.3 = (bf16[16,128,128]{2,1,0:T(8,128)(2,1)S(1)}, bf16[16,128,128]{2,1,0:T(8,128)(2,1)S(1)}, u32[]{:S(2)}, u32[]{:S(2)}) collective-permute-start(bf16[16,128,128]{2,1,0:T(8,128)(2,1)S(1)} %get-tuple-element.56.refs_6_), channel_id=1, source_target_pairs={{8,0},{16,8},{24,16},{0,24},{9,1},{17,9},{25,17},{1,25},{10,2},{18... | collective-permute-start | bytes 1572872 | tf_op jit(solution)/shard_map/ppermute | solution.py:19
  15.4 1.6 %collective-permute-start.1 = (f32[128,384]{1,0:T(8,128)S(1)}, f32[128,384]{1,0:T(8,128)S(1)}, u32[]{:S(2)}, u32[]{:S(2)}) collective-permute-start(f32[128,384]{1,0:T(8,128)S(1)} %add.36), channel_id=1, source_target_pairs={{2,0},{3,1},{0,2},{1,3},{6,4},{7,5},{4,6},{5,7},{10,8},{11,9},{8,1... | collective-permute-start | bytes 589832 | tf_op jit(solution)/shard_map/ppermute | solution.py:26
  17.0 4.9 %collective-permute-done.1 = f32[128,384]{1,0:T(8,128)S(1)} collective-permute-done((f32[128,384]{1,0:T(8,128)S(1)}, f32[128,384]{1,0:T(8,128)S(1)}, u32[]{:S(2)}, u32[]{:S(2)}) %collective-permute-start.1) | collective-permute-done | bytes 196640 | tf_op jit(solution)/shard_map/ppermute | solution.py:26
  21.9 1.6 %collective-permute-start.2 = (f32[128,384]{1,0:T(8,128)S(1)}, f32[128,384]{1,0:T(8,128)S(1)}, u32[]{:S(2)}, u32[]{:S(2)}) collective-permute-start(f32[128,384]{1,0:T(8,128)S(1)} %add.37), channel_id=1, source_target_pairs={{4,0},{5,1},{6,2},{7,3},{0,4},{1,5},{2,6},{3,7},{12,8},{13,9},{14,... | collective-permute-start | bytes 589832 | tf_op jit(solution)/shard_map/ppermute | solution.py:26
  23.5 0.4 collective-permute-done.4.refs_9_
  23.9 4.3 %collective-permute-start.10 = (bf16[16,128,128]{2,1,0:T(8,128)(2,1)S(1)}, bf16[16,128,128]{2,1,0:T(8,128)(2,1)S(1)}, u32[]{:S(2)}, u32[]{:S(2)}) collective-permute-start(bf16[16,128,128]{2,1,0:T(8,128)(2,1)S(1)} %get-tuple-element.62.refs_3_), channel_id=1, source_target_pairs={{8,0},{16,8},{24,16},{0,24},{9,1},{17,9},{25,17},{1,25},{10,2},{18... | collective-permute-start | bytes 1572872 | tf_op jit(solution)/shard_map/ppermute | solution.py:19
  28.2 0.0 collective-permute-done.2
  28.2 0.0 collective-permute-start.11
  28.2 6.7 %shard_map.67 = (f32[4,1024,256]{2,1,0:T(8,128)S(1)}, f32[4,1024,128]{2,1,0:T(8,128)S(1)}, bf16[4,1024,1024]{2,1,0:T(8,128)(2,1)S(1)}, bf16[4,8,128,128]{3,2,1,0:T(8,128)(2,1)S(1)}) custom-call(bf16[4,1024,1024]{2,1,0:T(8,128)(2,1)} %schur_hbm.1, bf16[4,8,128,128]{3,2,1,0:T(8,128)(2,1)S(1)} %get-tuple-element.42.mortar_in.mortar, ...), custom_call_target="tpu_custom_call" | custom-call | tf_op jit(solution)/shard_map/pallas_call | solution.py:350
  34.9 1.1 collective-permute-done.6.refs_11_
  36.1 10.4 %collective-permute-done.3.refs_8_ = bf16[16,128,128]{2,1,0:T(8,128)(2,1)S(1)} collective-permute-done((bf16[16,128,128]{2,1,0:T(8,128)(2,1)S(1)}, bf16[16,128,128]{2,1,0:T(8,128)(2,1)S(1)}, u32[]{:S(2)}, u32[]{:S(2)}) %collective-permute-start.3) | collective-permute-done | bytes 524320 | tf_op jit(solution)/shard_map/ppermute | solution.py:19
  46.4 12.1 %collective-permute-done.5.refs_10_ = bf16[16,128,128]{2,1,0:T(8,128)(2,1)S(1)} collective-permute-done((bf16[16,128,128]{2,1,0:T(8,128)(2,1)S(1)}, bf16[16,128,128]{2,1,0:T(8,128)(2,1)S(1)}, u32[]{:S(2)}, u32[]{:S(2)}) %collective-permute-start.5) | collective-permute-done | bytes 524320 | tf_op jit(solution)/shard_map/ppermute | solution.py:19
  58.6 3.8 %shard_map.68 = (f32[4,1024,256]{2,1,0:T(8,128)S(1)}, bf16[14,128,256]{2,1,0:T(8,128)(2,1)S(1)}, bf16[2,128,256]{2,1,0:T(8,128)(2,1)S(1)}, bf16[16,128,256]{2,1,...) custom-call(s32[4,4]{1,0:T(4,128)} %partner_hbm.9, ...), custom_call_target="tpu_custom_call", output_to_operand_aliasing={{0}: (4, {})} | custom-call | tf_op jit(solution)/shard_map/pallas_call | solution.py:364
  62.4 1.6 %collective-permute-start.21 = (bf16[14,128,256]{2,1,0:T(8,128)(2,1)S(1)}, bf16[14,128,256]{2,1,0:T(8,128)(2,1)S(1)}, u32[]{:S(2)}, u32[]{:S(2)}) collective-permute-start(bf16[14,128,256]{2,1,0:T(8,128)(2,1)S(1)} %get-tuple-element.73), channel_id=1, source_target_pairs={{24,0},{0,8},{8,16},{16,24},{25,1},{1,9},{9,17},{17,25},{26,2},{2,... | collective-permute-start | bytes 2752520 | tf_op jit(solution)/shard_map/ppermute | solution.py:19
  64.1 1.4 collective-permute-done.7
  65.4 1.5 %collective-permute-start.8 = (f32[136,256]{1,0:T(8,128)S(1)}, f32[136,256]{1,0:T(8,128)S(1)}, u32[]{:S(2)}, u32[]{:S(2)}) collective-permute-start(f32[136,256]{1,0:T(8,128)S(1)} %add.39), channel_id=1, source_target_pairs={{2,0},{3,1},{0,2},{1,3},{6,4},{7,5},{4,6},{5,7},{10,8},{11,9},{8,1... | collective-permute-start | bytes 417800 | tf_op jit(solution)/shard_map/ppermute | solution.py:26
  67.0 4.2 %collective-permute-done.8 = f32[136,256]{1,0:T(8,128)S(1)} collective-permute-done((f32[136,256]{1,0:T(8,128)S(1)}, f32[136,256]{1,0:T(8,128)S(1)}, u32[]{:S(2)}, u32[]{:S(2)}) %collective-permute-start.8) | collective-permute-done | bytes 139296 | tf_op jit(solution)/shard_map/ppermute | solution.py:26
  71.3 1.6 %collective-permute-start.9 = (f32[136,256]{1,0:T(8,128)S(1)}, f32[136,256]{1,0:T(8,128)S(1)}, u32[]{:S(2)}, u32[]{:S(2)}) collective-permute-start(f32[136,256]{1,0:T(8,128)S(1)} %add.40), channel_id=1, source_target_pairs={{4,0},{5,1},{6,2},{7,3},{0,4},{1,5},{2,6},{3,7},{12,8},{13,9},{14,... | collective-permute-start | bytes 417800 | tf_op jit(solution)/shard_map/ppermute | solution.py:26
  72.9 3.5 %collective-permute-done.9 = f32[136,256]{1,0:T(8,128)S(1)} collective-permute-done((f32[136,256]{1,0:T(8,128)S(1)}, f32[136,256]{1,0:T(8,128)S(1)}, u32[]{:S(2)}, u32[]{:S(2)}) %collective-permute-start.9) | collective-permute-done | bytes 139296 | tf_op jit(solution)/shard_map/ppermute | solution.py:26
  76.4 4.6 %collective-permute-done.11.refs_5_ = bf16[16,128,128]{2,1,0:T(8,128)(2,1)S(1)} collective-permute-done((bf16[16,128,128]{2,1,0:T(8,128)(2,1)S(1)}, bf16[16,128,128]{2,1,0:T(8,128)(2,1)S(1)}, u32[]{:S(2)}, u32[]{:S(2)}) %collective-permute-start.11) | collective-permute-done | bytes 524320 | tf_op jit(solution)/shard_map/ppermute | solution.py:19
  81.0 2.7 %shard_map.69 = (f32[4,1024,128]{2,1,0:T(8,128)S(1)}, bf16[5,128,128]{2,1,0:T(8,128)(2,1)S(1)}, bf16[11,128,128]{2,1,0:T(8,128)(2,1)S(1)}, bf16[16,128,128]{2,1,...) custom-call(s32[4,4]{1,0:T(4,128)} %partner_hbm.9, ...), custom_call_target="tpu_custom_call", output_to_operand_aliasing={{0}: (4, {})} | custom-call | tf_op jit(solution)/shard_map/pallas_call | solution.py:364
  83.8 0.1 collective-permute-start.12
  83.9 1.2 collective-permute-done.12
  85.1 1.6 %collective-permute-start.13 = (f32[136,128]{1,0:T(8,128)S(1)}, f32[136,128]{1,0:T(8,128)S(1)}, u32[]{:S(2)}, u32[]{:S(2)}) collective-permute-start(f32[136,128]{1,0:T(8,128)S(1)} %add.42), channel_id=1, source_target_pairs={{2,0},{3,1},{0,2},{1,3},{6,4},{7,5},{4,6},{5,7},{10,8},{11,9},{8,1... | collective-permute-start | bytes 208904 | tf_op jit(solution)/shard_map/ppermute | solution.py:26
  86.7 1.6 %collective-permute-start.24 = (bf16[11,128,128]{2,1,0:T(8,128)(2,1)S(1)}, bf16[11,128,128]{2,1,0:T(8,128)(2,1)S(1)}, u32[]{:S(2)}, u32[]{:S(2)}) collective-permute-start(bf16[11,128,128]{2,1,0:T(8,128)(2,1)S(1)} %get-tuple-element.78), channel_id=1, source_target_pairs={{24,0},{0,8},{8,16},{16,24},{25,1},{1,9},{9,17},{17,25},{26,2},{2,... | collective-permute-start | bytes 1081352 | tf_op jit(solution)/shard_map/ppermute | solution.py:19
  88.3 1.2 collective-permute-done.13
  89.5 1.6 %collective-permute-start.14 = (f32[136,128]{1,0:T(8,128)S(1)}, f32[136,128]{1,0:T(8,128)S(1)}, u32[]{:S(2)}, u32[]{:S(2)}) collective-permute-start(f32[136,128]{1,0:T(8,128)S(1)} %add.43), channel_id=1, source_target_pairs={{4,0},{5,1},{6,2},{7,3},{0,4},{1,5},{2,6},{3,7},{12,8},{13,9},{14,... | collective-permute-start | bytes 208904 | tf_op jit(solution)/shard_map/ppermute | solution.py:26
  91.1 2.8 %collective-permute-done.14 = f32[136,128]{1,0:T(8,128)S(1)} collective-permute-done((f32[136,128]{1,0:T(8,128)S(1)}, f32[136,128]{1,0:T(8,128)S(1)}, u32[]{:S(2)}, u32[]{:S(2)}) %collective-permute-start.14) | collective-permute-done | bytes 69664 | tf_op jit(solution)/shard_map/ppermute | solution.py:26
  93.9 3.8 %collective-permute-start.15 = (f32[8,128]{1,0:T(8,128)S(1)}, f32[8,128]{1,0:T(8,128)S(1)}, u32[]{:S(2)}, u32[]{:S(2)}) collective-permute-start(f32[8,128]{1,0:T(8,128)S(1)} %slice.4), channel_id=1, source_target_pairs={{0,24},{1,25},{2,26},{3,27},{4,28},{5,29},{6,30},{7,31}} | collective-permute-start | bytes 12296 | tf_op jit(solution)/shard_map/ppermute | solution.py:36
  97.8 0.7 collective-permute-start.16
  98.4 0.7 collective-permute-start.17
  99.1 8.0 %collective-permute-done.15 = f32[8,128]{1,0:T(8,128)S(1)} collective-permute-done((f32[8,128]{1,0:T(8,128)S(1)}, f32[8,128]{1,0:T(8,128)S(1)}, u32[]{:S(2)}, u32[]{:S(2)}) %collective-permute-start.15) | collective-permute-done | bytes 4128 | tf_op jit(solution)/shard_map/ppermute | solution.py:36
  107.1 0.4 collective-permute-start.23
  107.5 1.3 collective-permute-start.18
  108.8 9.1 %collective-permute-done.18.refs_1_ = f32[8,128]{1,0:T(8,128)S(1)} collective-permute-done((f32[8,128]{1,0:T(8,128)S(1)}, f32[8,128]{1,0:T(8,128)S(1)}, u32[]{:S(2)}, u32[]{:S(2)}) %collective-permute-start.18) | collective-permute-done | bytes 4128 | tf_op jit(solution)/shard_map/ppermute | solution.py:37
  118.0 0.7 collective-permute-start.19
  118.6 0.7 collective-permute-start.20
  119.3 5.4 %shard_map.70 = (f32[8,384]{1,0:T(8,128)S(1)}, f32[8,384]{1,0:T(8,128)S(1)}, f32[8,384]{1,0:T(8,128)S(1)}) custom-call(f32[8,128]{1,0:T(8,128)S(1)} %add_add_fusion.refs_0_, f32[8,128]{1,0:T(8,128)S(1)} %collective-permute-done.18.refs_1_, f32[8,128]{1,0:T(8,128)S(1)} %collective-permute-done.19.refs_2_, f32[8,128]{1,0:T(8,128)S(1)} %collective-permute-done.20.refs_3_, ...), custom_call_target="tpu_custom_call" | custom-call | tf_op jit(solution)/shard_map/pallas_call | solution.py:387
  124.8 0.7 shard_map.71.energy
  125.5 0.4 shard_map.72
  125.9 14.4 %all_to_all.5.gathered = f32[32,8,128]{2,1,0:T(8,128)S(1)} all-to-all(f32[32,8,128]{2,1,0:T(8,128)S(1)} %shard_map.72), channel_id=1, replica_groups=mesh['sub'=4,'grp'=8] {'sub','grp'}, dimensions={0} | all-to-all | bytes 262144 | tf_op jit(solution)/shard_map/all_to_all | solution.py:400
  140.3 3.0 %shard_map.73 = f32[4,1024,384]{2,1,0:T(8,128)} custom-call(f32[8,384]{1,0:T(8,128)S(1)} %get-tuple-element.68.total, f32[32,8,128]{2,1,0:T(8,128)S(1)} %all_to_all.5.gathered, f32[4,1024,128]{2,1,0:T(8,128)S(1)} %get-tuple-element.43.refs_0_.refs_11_, f32[4,1024,128]{2,1,0:T(8,128)S(1)} %get-tuple-element.44.refs_1_.refs_12_, ...), custom_call_target="tpu_custom_call" | custom-call | tf_op jit(solution)/shard_map/pallas_call | solution.py:402
  (29 shorter events, 0.2 us)
Async XLA Ops:
  6.4 9.0 %collective-permute-start = (f32[128,384]{1,0:T(8,128)S(1)}, f32[128,384]{1,0:T(8,128)S(1)}, u32[]{:S(2)}, u32[]{:S(2)}) collective-permute-start(f32[128,384]{1,0:T(8,128)S(1)} %constant_dynamic-update-slice_fusion), channel_id=1, source_target_pairs={{1,0},{0,1},{3,2},{2,3},{5,4},{4,5},{7,6},{6,7},{9,8},{8,9},{11,10... | collective-permute-start | bytes 589832 | tf_op jit(solution)/shard_map/ppermute | solution.py:26
  6.9 17.0 %collective-permute-start.4 = (bf16[16,128,128]{2,1,0:T(8,128)(2,1)S(1)}, bf16[16,128,128]{2,1,0:T(8,128)(2,1)S(1)}, u32[]{:S(2)}, u32[]{:S(2)}) collective-permute-start(bf16[16,128,128]{2,1,0:T(8,128)(2,1)S(1)} %get-tuple-element.57.refs_7_), channel_id=1, source_target_pairs={{8,0},{16,8},{24,16},{0,24},{9,1},{17,9},{25,17},{1,25},{10,2},{18... | collective-permute-start | bytes 1572872 | tf_op jit(solution)/shard_map/ppermute | solution.py:19
  11.6 24.5 %collective-permute-start.6 = (bf16[16,128,128]{2,1,0:T(8,128)(2,1)S(1)}, bf16[16,128,128]{2,1,0:T(8,128)(2,1)S(1)}, u32[]{:S(2)}, u32[]{:S(2)}) collective-permute-start(bf16[16,128,128]{2,1,0:T(8,128)(2,1)S(1)} %get-tuple-element.55.refs_5_), channel_id=1, source_target_pairs={{24,0},{0,8},{8,16},{16,24},{25,1},{1,9},{9,17},{17,25},{26,2},{2,... | collective-permute-start | bytes 1572872 | tf_op jit(solution)/shard_map/ppermute | solution.py:19
  11.6 34.9 %collective-permute-start.3 = (bf16[16,128,128]{2,1,0:T(8,128)(2,1)S(1)}, bf16[16,128,128]{2,1,0:T(8,128)(2,1)S(1)}, u32[]{:S(2)}, u32[]{:S(2)}) collective-permute-start(bf16[16,128,128]{2,1,0:T(8,128)(2,1)S(1)} %get-tuple-element.56.refs_6_), channel_id=1, source_target_pairs={{8,0},{16,8},{24,16},{0,24},{9,1},{17,9},{25,17},{1,25},{10,2},{18... | collective-permute-start | bytes 1572872 | tf_op jit(solution)/shard_map/ppermute | solution.py:19
  15.4 43.2 %collective-permute-start.5 = (bf16[16,128,128]{2,1,0:T(8,128)(2,1)S(1)}, bf16[16,128,128]{2,1,0:T(8,128)(2,1)S(1)}, u32[]{:S(2)}, u32[]{:S(2)}) collective-permute-start(bf16[16,128,128]{2,1,0:T(8,128)(2,1)S(1)} %get-tuple-element.54.refs_4_), channel_id=1, source_target_pairs={{24,0},{0,8},{8,16},{16,24},{25,1},{1,9},{9,17},{17,25},{26,2},{2,... | collective-permute-start | bytes 1572872 | tf_op jit(solution)/shard_map/ppermute | solution.py:19
  15.4 6.5 %collective-permute-start.1 = (f32[128,384]{1,0:T(8,128)S(1)}, f32[128,384]{1,0:T(8,128)S(1)}, u32[]{:S(2)}, u32[]{:S(2)}) collective-permute-start(f32[128,384]{1,0:T(8,128)S(1)} %add.36), channel_id=1, source_target_pairs={{2,0},{3,1},{0,2},{1,3},{6,4},{7,5},{4,6},{5,7},{10,8},{11,9},{8,1... | collective-permute-start | bytes 589832 | tf_op jit(solution)/shard_map/ppermute | solution.py:26
  21.9 6.3 %collective-permute-start.2 = (f32[128,384]{1,0:T(8,128)S(1)}, f32[128,384]{1,0:T(8,128)S(1)}, u32[]{:S(2)}, u32[]{:S(2)}) collective-permute-start(f32[128,384]{1,0:T(8,128)S(1)} %add.37), channel_id=1, source_target_pairs={{4,0},{5,1},{6,2},{7,3},{0,4},{1,5},{2,6},{3,7},{12,8},{13,9},{14,... | collective-permute-start | bytes 589832 | tf_op jit(solution)/shard_map/ppermute | solution.py:26
  23.9 52.5 %collective-permute-start.10 = (bf16[16,128,128]{2,1,0:T(8,128)(2,1)S(1)}, bf16[16,128,128]{2,1,0:T(8,128)(2,1)S(1)}, u32[]{:S(2)}, u32[]{:S(2)}) collective-permute-start(bf16[16,128,128]{2,1,0:T(8,128)(2,1)S(1)} %get-tuple-element.62.refs_3_), channel_id=1, source_target_pairs={{8,0},{16,8},{24,16},{0,24},{9,1},{17,9},{25,17},{1,25},{10,2},{18... | collective-permute-start | bytes 1572872 | tf_op jit(solution)/shard_map/ppermute | solution.py:19
  28.2 52.8 %collective-permute-start.11 = (bf16[16,128,128]{2,1,0:T(8,128)(2,1)S(1)}, bf16[16,128,128]{2,1,0:T(8,128)(2,1)S(1)}, u32[]{:S(2)}, u32[]{:S(2)}) collective-permute-start(bf16[16,128,128]{2,1,0:T(8,128)(2,1)S(1)} %get-tuple-element.61.refs_2_), channel_id=1, source_target_pairs={{24,0},{0,8},{8,16},{16,24},{25,1},{1,9},{9,17},{17,25},{26,2},{2,... | collective-permute-start | bytes 1572872 | tf_op jit(solution)/shard_map/ppermute | solution.py:19
  28.2 30.4 %copy-start = (f32[1,128,128]{2,1,0:T(8,128)S(1)}, f32[1,128,128]{2,1,0:T(8,128)}, u32[]{:S(2)}) copy-start(f32[1,128,128]{2,1,0:T(8,128)} %refs_6_.1) | copy-start | bytes 196612
  62.4 62.3 %collective-permute-start.21 = (bf16[14,128,256]{2,1,0:T(8,128)(2,1)S(1)}, bf16[14,128,256]{2,1,0:T(8,128)(2,1)S(1)}, u32[]{:S(2)}, u32[]{:S(2)}) collective-permute-start(bf16[14,128,256]{2,1,0:T(8,128)(2,1)S(1)} %get-tuple-element.73), channel_id=1, source_target_pairs={{24,0},{0,8},{8,16},{16,24},{25,1},{1,9},{9,17},{17,25},{26,2},{2,... | collective-permute-start | bytes 2752520 | tf_op jit(solution)/shard_map/ppermute | solution.py:19
  64.1 1.4 collective-permute-start.7
  65.4 5.8 %collective-permute-start.8 = (f32[136,256]{1,0:T(8,128)S(1)}, f32[136,256]{1,0:T(8,128)S(1)}, u32[]{:S(2)}, u32[]{:S(2)}) collective-permute-start(f32[136,256]{1,0:T(8,128)S(1)} %add.39), channel_id=1, source_target_pairs={{2,0},{3,1},{0,2},{1,3},{6,4},{7,5},{4,6},{5,7},{10,8},{11,9},{8,1... | collective-permute-start | bytes 417800 | tf_op jit(solution)/shard_map/ppermute | solution.py:26
  71.3 5.1 %collective-permute-start.9 = (f32[136,256]{1,0:T(8,128)S(1)}, f32[136,256]{1,0:T(8,128)S(1)}, u32[]{:S(2)}, u32[]{:S(2)}) collective-permute-start(f32[136,256]{1,0:T(8,128)S(1)} %add.40), channel_id=1, source_target_pairs={{4,0},{5,1},{6,2},{7,3},{0,4},{1,5},{2,6},{3,7},{12,8},{13,9},{14,... | collective-permute-start | bytes 417800 | tf_op jit(solution)/shard_map/ppermute | solution.py:26
  83.8 1.3 collective-permute-start.12
  85.1 4.4 %collective-permute-start.13 = (f32[136,128]{1,0:T(8,128)S(1)}, f32[136,128]{1,0:T(8,128)S(1)}, u32[]{:S(2)}, u32[]{:S(2)}) collective-permute-start(f32[136,128]{1,0:T(8,128)S(1)} %add.42), channel_id=1, source_target_pairs={{2,0},{3,1},{0,2},{1,3},{6,4},{7,5},{4,6},{5,7},{10,8},{11,9},{8,1... | collective-permute-start | bytes 208904 | tf_op jit(solution)/shard_map/ppermute | solution.py:26
  86.7 38.8 %collective-permute-start.24 = (bf16[11,128,128]{2,1,0:T(8,128)(2,1)S(1)}, bf16[11,128,128]{2,1,0:T(8,128)(2,1)S(1)}, u32[]{:S(2)}, u32[]{:S(2)}) collective-permute-start(bf16[11,128,128]{2,1,0:T(8,128)(2,1)S(1)} %get-tuple-element.78), channel_id=1, source_target_pairs={{24,0},{0,8},{8,16},{16,24},{25,1},{1,9},{9,17},{17,25},{26,2},{2,... | collective-permute-start | bytes 1081352 | tf_op jit(solution)/shard_map/ppermute | solution.py:19
  89.5 4.4 %collective-permute-start.14 = (f32[136,128]{1,0:T(8,128)S(1)}, f32[136,128]{1,0:T(8,128)S(1)}, u32[]{:S(2)}, u32[]{:S(2)}) collective-permute-start(f32[136,128]{1,0:T(8,128)S(1)} %add.43), channel_id=1, source_target_pairs={{4,0},{5,1},{6,2},{7,3},{0,4},{1,5},{2,6},{3,7},{12,8},{13,9},{14,... | collective-permute-start | bytes 208904 | tf_op jit(solution)/shard_map/ppermute | solution.py:26
  93.9 13.2 %collective-permute-start.15 = (f32[8,128]{1,0:T(8,128)S(1)}, f32[8,128]{1,0:T(8,128)S(1)}, u32[]{:S(2)}, u32[]{:S(2)}) collective-permute-start(f32[8,128]{1,0:T(8,128)S(1)} %slice.4), channel_id=1, source_target_pairs={{0,24},{1,25},{2,26},{3,27},{4,28},{5,29},{6,30},{7,31}} | collective-permute-start | bytes 12296 | tf_op jit(solution)/shard_map/ppermute | solution.py:36
  97.8 9.4 %collective-permute-start.16 = (f32[8,128]{1,0:T(8,128)S(1)}, f32[8,128]{1,0:T(8,128)S(1)}, u32[]{:S(2)}, u32[]{:S(2)}) collective-permute-start(f32[8,128]{1,0:T(8,128)S(1)} %slice.4), channel_id=1, source_target_pairs={{8,24},{9,25},{10,26},{11,27},{12,28},{13,29},{14,30},{15,31}} | collective-permute-start | bytes 12296 | tf_op jit(solution)/shard_map/ppermute | solution.py:36
  98.4 9.1 %collective-permute-start.17 = (f32[8,128]{1,0:T(8,128)S(1)}, f32[8,128]{1,0:T(8,128)S(1)}, u32[]{:S(2)}, u32[]{:S(2)}) collective-permute-start(f32[8,128]{1,0:T(8,128)S(1)} %slice.4), channel_id=1, source_target_pairs={{16,24},{17,25},{18,26},{19,27},{20,28},{21,29},{22,30},{23,31}} | collective-permute-start | bytes 12296 | tf_op jit(solution)/shard_map/ppermute | solution.py:36
  107.1 17.6 %collective-permute-start.22 = (bf16[2,128,256]{2,1,0:T(8,128)(2,1)S(1)}, bf16[2,128,256]{2,1,0:T(8,128)(2,1)S(1)}, u32[]{:S(2)}, u32[]{:S(2)}) collective-permute-start(bf16[2,128,256]{2,1,0:T(8,128)(2,1)S(1)} %get-tuple-element.74), channel_id=1, source_target_pairs={{24,0},{0,8},{8,16},{16,24},{25,1},{1,9},{9,17},{17,25},{26,2},{2,... | collective-permute-start | bytes 393224 | tf_op jit(solution)/shard_map/ppermute | solution.py:19
  107.1 18.3 %collective-permute-start.23 = (bf16[5,128,128]{2,1,0:T(8,128)(2,1)S(1)}, bf16[5,128,128]{2,1,0:T(8,128)(2,1)S(1)}, u32[]{:S(2)}, u32[]{:S(2)}) collective-permute-start(bf16[5,128,128]{2,1,0:T(8,128)(2,1)S(1)} %get-tuple-element.77), channel_id=1, source_target_pairs={{24,0},{0,8},{8,16},{16,24},{25,1},{1,9},{9,17},{17,25},{26,2},{2,... | collective-permute-start | bytes 491528 | tf_op jit(solution)/shard_map/ppermute | solution.py:19
  107.5 10.4 %collective-permute-start.18 = (f32[8,128]{1,0:T(8,128)S(1)}, f32[8,128]{1,0:T(8,128)S(1)}, u32[]{:S(2)}, u32[]{:S(2)}) collective-permute-start(f32[8,128]{1,0:T(8,128)S(1)} %add_add_fusion.refs_0_), channel_id=1, source_target_pairs={{24,0},{25,1},{26,2},{27,3},{28,4},{29,5},{30,6},{31,7}} | collective-permute-start | bytes 12296 | tf_op jit(solution)/shard_map/ppermute | solution.py:37
  118.0 0.7 collective-permute-start.19
  118.6 0.7 collective-permute-start.20

commit v3 on v2

--- a/solution.py
+++ b/solution.py
@@ -32,9 +32,10 @@
     size = lax.axis_size(axis)
     hub = size - 1
     total = value
-    for i in range(hub):
-        total = total + lax.ppermute(value, axis, [(i, hub)])
-    others = [lax.ppermute(total, axis, [(hub, i)]) for i in range(hub)]
+    for d in range(hub, 0, -1):
+        route = [(i, (i + d) % size) for i in range(size) if (i + d) % size >= hub - 1]
+        total = total + lax.ppermute(value, axis, route)
+    others = [lax.ppermute(total, axis, [(hub, i)]) for i in range(hub - 1)]
     return [total] + others
 
 
@@ -69,9 +70,31 @@
     ]
 
 
+def lead_traces(load_hbm, mortar_hbm, low, load, mortar, sems):
+    subs, half, block = mortar.shape[:3]
+    width = load.shape[2]
+
+    def fetch(s):
+        rows = pl.ds(half * block, half * block)
+        return [
+            pltpu.make_async_copy(load_hbm.at[s, rows, pl.ds(0, width)], load.at[s], sems.at[0, s]),
+            pltpu.make_async_copy(mortar_hbm.at[s, pl.ds(half, half)], mortar.at[s], sems.at[1, s]),
+        ]
+
+    for s in range(subs):
+        for move in fetch(s):
+            move.start()
+    for s in range(subs):
+        for move in fetch(s):
+            move.wait()
+        for f in range(half):
+            rows = load[s, f * block : (f + 1) * block, :].astype(BF16)
+            low[s * half + f] = jnp.dot(mortar[s, f], rows, preferred_element_type=F32).astype(BF16)
+
+
 def first_traces(lo, copies, partner_hbm, cmap_hbm, load_hbm, mortar_in, *refs):
     if copies:
-        load, mortar, up, low, norm, csum, partner, cmap, sems = refs
+        load, mortar, up, norm, csum, partner, cmap, sems = refs
     else:
         load, up, low, norm, csum, partner, cmap, sems = refs
         mortar = mortar_in
@@ -103,6 +126,8 @@
         for f in range(faces):
             rows = load[s, f * block : (f + 1) * block, :]
             norm[...] += fold_rows(rows * rows)
+            if copies and f >= half:
+                continue
             trace = jnp.dot(mortar[s, f], rows.astype(BF16), preferred_element_type=F32).astype(BF16)
             if f < half:
                 up[partner[s, f]] = trace
@@ -139,7 +164,7 @@
 def first_image(lo, pieces, groups, share, partner_hbm, cmap_hbm, mortar, flipped, stiff, csum, cinv, *refs):
     ins, earlier, refs = refs[: 6 * pieces], refs[6 * pieces], refs[6 * pieces + 1 :]
     loads, norms, ups, lows, aboves, belows = (ins[i * pieces : (i + 1) * pieces] for i in range(6))
-    up_cuts, refs = refs[1:-8], refs[:1] + refs[-8:]
+    tail_in, (send, rest), refs = refs[:-11], refs[-10:-8], refs[-11:-10] + refs[-8:]
     image, low_out, jump_out, sums, cval, up_out, partner, cmap, sems = refs
     subs, order, width = image.shape
     faces, block = mortar.shape[1], mortar.shape[2]
@@ -192,11 +217,15 @@
         return curv
 
     curv = lax.fori_loop(0, subs, work, tuple(jnp.zeros((8, LANES), F32) for _ in loads))
-    at = 0
-    for cut in up_cuts:
-        cut[...] = up_out[at : at + cut.shape[0]]
-        at += cut.shape[0]
     first = lo // LANES
+    if first:
+        kept = first * tail_in[0].shape[0]
+        for at in range(kept):
+            send[at] = tail_in[0][at // first, :, group_cols(at % first)]
+        send[kept:] = up_out[: send.shape[0] - kept]
+    else:
+        send[...] = up_out[: send.shape[0]]
+    rest[...] = up_out[up_out.shape[0] - rest.shape[0] :]
     for j in range(pieces):
         for row, value in ((first + j, norms[j][...]), (groups + first + j, curv[j])):
             sums[coarse + row : coarse + row + 1, :LANES] = row_sum(value)
@@ -209,9 +238,10 @@
 def residual_sums(share, hops, groups, *refs):
     parts, refs = refs[:hops], refs[hops:]
     schur, csum, cinv, csum_a, csum_b, image_a, image_b = refs[:7]
-    loads, (total, norm, energy, resid) = refs[7 : 7 + groups], refs[7 + groups :]
+    loads, (low, jump), refs = refs[7 : 7 + groups], refs[7 + groups : 9 + groups], refs[9 + groups :]
+    recvs, (total, norm, energy, resid) = refs[:-4], refs[-4:]
     coarse = csum.shape[0]
-    value = jnp.where(lax.axis_index("sub") == hops - 1, parts[0][...], 0.0)
+    value = jnp.where(lax.axis_index("sub") + 1 >= hops, parts[0][...], 0.0)
     for ref in parts[1:]:
         value += ref[...]
     for j in range(groups):
@@ -224,7 +254,15 @@
     norm[...] = jnp.zeros_like(norm)
     energy[...] = share * fold_rows(change * field)
 
-    def work(s, _):
+    slots, subs = low.shape[0], schur.shape[0]
+
+    def received(k, j):
+        whole, mixed = recvs
+        if k < whole.shape[0]:
+            return whole[k, :, group_cols(j)]
+        return mixed[(k - whole.shape[0]) * (groups - 1) + j]
+
+    for s in range(subs):
         for j, load in enumerate(loads):
             cols = group_cols(j)
             image, own = (image_a, cols) if j + 1 < groups else (image_b, group_cols(0))
@@ -232,13 +270,18 @@
         r = resid[...]
         norm[...] += fold_rows(r * r)
         energy[...] += fold_rows(r * jnp.dot(schur[s], r.astype(BF16), preferred_element_type=F32))
-        return 0
-
-    lax.fori_loop(0, schur.shape[0], work, 0)
+        for j in range(groups - 1):
+            cols = group_cols(j)
+            acc = energy[:, cols]
+            for k in range(s * slots // subs, (s + 1) * slots // subs):
+                delta = low[k, :, cols].astype(F32) - received(k, j).astype(F32)
+                value = jump[k, :, cols].astype(F32) - step[:, cols] * delta
+                acc += fold_rows(value * value)
+            energy[:, cols] = acc
 
 
 def jump_squares(step, low, jump, recvs, cols):
-    start, acc = 0, jnp.zeros((8, LANES), F32)
+    acc, start = jnp.zeros((8, LANES), F32), low.shape[0] - sum(recv.shape[0] for recv in recvs)
     for recv in recvs:
 
         def one(k, acc, recv=recv, start=start):
@@ -246,31 +289,21 @@
             value = jump[start + k, :, cols].astype(F32) - step * delta
             return acc + fold_rows(value * value)
 
-        acc = lax.fori_loop(0, recv.shape[0], one, acc, unroll=2)
+        acc = lax.fori_loop(max(-start, 0), recv.shape[0], one, acc, unroll=2)
         start += recv.shape[0]
     return acc
-
-
-def add_jumps(total, energy, low, jump, *refs):
-    recvs, out = refs[:-1], refs[-1]
-    wide = low.shape[2]
-    out[:, wide:] = energy[:, wide:]
-    for j in range(wide // LANES):
-        cols = group_cols(j)
-        step = total[0:1, cols] / total[1:2, cols]
-        out[:, cols] = energy[:, cols] + jump_squares(step, low, jump, recvs, cols)
 
 
 def last_sums(total, norm, energy, low, jump, *refs):
     recvs, out = refs[:-1], refs[-1]
     groups = norm.shape[1] // LANES
     last = group_cols(groups - 1)
-    rows = [row_sum(norm[:, group_cols(j)]) for j in range(groups)]
-    rows += [row_sum(energy[:, group_cols(j)]) for j in range(groups - 1)]
     step = total[0:1, last] / total[1:2, last]
-    rows.append(row_sum(energy[:, last] + jump_squares(step, low, jump, recvs, group_cols(0))))
-    rows.append(jnp.zeros((8 - len(rows), LANES), F32))
-    out[...] = jnp.broadcast_to(jnp.concatenate(rows, axis=0)[None], out.shape)
+    ending = row_sum(energy[:, last] + jump_squares(step, low, jump, recvs, group_cols(0)))
+    for d in range(out.shape[0]):
+        out[d, 0:1, :] = row_sum(norm[...])
+        out[d, 1:2, :] = row_sum(energy[...])
+        out[d, 1:2, last] = ending
 
 
 def finish(total, gathered, *refs):
@@ -279,24 +312,31 @@
     subs = stage.shape[0]
     second = jnp.sum(gathered[...], axis=0)
 
-    def send(s):
-        return pltpu.make_async_copy(stage.at[s], out_hbm.at[s], sems.at[s])
+    pieces = sems.shape[1]
+    size = stage.shape[1] // pieces
+
+    def send(s, p):
+        rows = pl.ds(p * size, size)
+        return pltpu.make_async_copy(stage.at[s, rows], out_hbm.at[s, rows], sems.at[s, p])
 
     scales = []
     for j in range(groups):
         norm0 = total[0:1, group_cols(j)]
         step = norm0 / total[1:2, group_cols(j)]
-        norm1 = second[j : j + 1, :]
+        norm1 = second[0:1, group_cols(j)]
         beta = norm1 / norm0
-        step2 = norm1 / (second[groups + j : groups + j + 1, :] - beta * norm1 / step)
+        step2 = norm1 / (second[1:2, group_cols(j)] - beta * norm1 / step)
         scales.append((step + step2 * (1.0 + beta), step2 * step))
     for s in range(subs):
-        for j in range(groups):
-            image, cols = (image_a, group_cols(j)) if j + 1 < groups else (image_b, group_cols(0))
-            stage[s, :, group_cols(j)] = scales[j][0] * loads[j][s] - scales[j][1] * image[s, :, cols]
-        send(s).start()
-    for s in range(subs):
-        send(s).wait()
+        for p in range(pieces):
+            rows = slice(p * size, (p + 1) * size)
+            for j in range(groups):
+                image, cols = (image_a, group_cols(j)) if j + 1 < groups else (image_b, group_cols(0))
+                stage[s, rows, group_cols(j)] = scales[j][0] * loads[j][s, rows] - scales[j][1] * image[s, rows, cols]
+            send(s, p).start()
+    for s in range(subs):
+        for p in range(pieces):
+            send(s, p).wait()
 
 
 def call(kernel, in_specs, outs, scratch=(), limit=5, in_hbm=(), alias=None):
@@ -327,11 +367,17 @@
 
     loads, norms, ups, lows, csums, aboves, belows = [], [], [], [], [], [], []
     held_mortar = hbm(mortar)
+    lead = call(
+        lead_traces, [ANY, ANY], [traces_of(LANES)],
+        [pltpu.VMEM((subs, half * block, LANES), F32), pltpu.VMEM((subs, half, block, block), BF16),
+         dma((2, subs))],
+    )(hbm(load), held_mortar)[0]
+    aboves.append(vmem(shifted(lead, "sub", -1)))
     for j in range(groups):
         outs = [pltpu.VMEM((subs, order, LANES), F32)]
         if j == 0:
             outs.append(pltpu.VMEM(mortar.shape, BF16))
-        outs += [traces_of(LANES)] * 2 + [pltpu.VMEM((8, LANES), F32), pltpu.VMEM((coarse, LANES), F32)]
+        outs += [traces_of(LANES)] * (1 + (j > 0)) + [pltpu.VMEM((8, LANES), F32), pltpu.VMEM((coarse, LANES), F32)]
         got = list(call(
             functools.partial(first_traces, j * LANES, j == 0),
             [ANY, ANY, ANY, ANY if j == 0 else VMEM], outs, table_scratch + [dma((3, max(subs, 2)))],
@@ -339,8 +385,11 @@
         loads.append(vmem(got.pop(0)))
         if j == 0:
             held_mortar = vmem(got.pop(0))
+        if j == 0:
+            got.insert(1, lead)
         belows.append(vmem(shifted(got[0], "sub", 1)))
-        aboves.append(vmem(shifted(got[1], "sub", -1)))
+        if j:
+            aboves.append(vmem(shifted(got[1], "sub", -1)))
         ups.append(vmem(got[0]))
         lows.append(vmem(got[1]))
         norms.append(vmem(got[2]))
@@ -356,19 +405,20 @@
 
     bounds = ((0, groups - 1), (groups - 1, groups))
     share = 1.0 / lax.axis_size("grp")
-    images, jumps, low2s, recvs, csum2s = [], [], [], [], []
-    cuts = ((slots - slots // 8, slots // 8), (5 * slots // 16, slots - 5 * slots // 16))
+    images, jumps, low2s, recvs, csum2s, tails = [], [], [], [], [], []
+    tail, lead_slots = 2 * slots // 16, 4 * slots // 16
+    cuts = ((slots - tail, tail), ((groups - 1) * tail + lead_slots, slots - lead_slots))
     for k, (lo, hi) in enumerate(bounds):
         n, w = hi - lo, (hi - lo) * LANES
         pick = [x[lo:hi] for x in (loads, norms, ups, lows, aboves, belows)]
         got = call(
             functools.partial(first_image, lo * LANES, n, groups, share),
-            [ANY, ANY] + [VMEM] * (6 + 6 * n),
+            [ANY, ANY] + [VMEM] * (6 + 6 * n + k),
             [pltpu.VMEM((subs, order, w), F32)]
             + [pltpu.VMEM((size, block, w), BF16) for size in cuts[k]]
             + [traces_of(w)] * 2 + [pltpu.VMEM((coarse + 8, w), F32)],
             [pltpu.VMEM((coarse, w), F32), traces_of(w)] + table_scratch + [dma((2,))], alias={4: 0},
-        )(*tables, held_mortar, flipped, vmem(stiff[k]), csum, coarse_inv, *sum(pick, []), csum2s[0] if k else csum)
+        )(*tables, held_mortar, flipped, vmem(stiff[k]), csum, coarse_inv, *sum(pick, []), csum2s[0] if k else csum, *tails)
         image, *up2, low2, jump, sums = got
         images.append(vmem(image))
         low2s.append(vmem(low2))
@@ -378,31 +428,29 @@
             csum, sums = lax.optimization_barrier((csum, sums))
             csum = vmem(csum)
         csum2s.append(vmem(sums))
-        recvs.append([])
+        held = up2.pop() if not k else None
+        tails = [vmem(held)] if not k else []
         for piece in up2:
-            recvs[-1].append(vmem(shifted(piece, "sub", 1)))
+            recvs.append(vmem(shifted(piece, "sub", 1)))
 
     totals = [vmem(x) for x in hub_sum(sums[coarse:], "sub")]
     hops = len(totals)
     total, norm1, energy = call(
         functools.partial(residual_sums, share, hops, groups),
-        [VMEM] * (hops + 7 + groups), [pltpu.VMEM((8, columns), F32)] * 3, [pltpu.VMEM((order, columns), F32)],
-    )(*totals, held_schur, csum, coarse_inv, *csum2s, *images, *loads)
-    total, norm1 = vmem(total), vmem(norm1)
-    energy = vmem(call(
-        add_jumps, [VMEM] * (4 + len(recvs[0])), [pltpu.VMEM(energy.shape, F32)],
-    )(total, vmem(energy), low2s[0], jumps[0], *recvs[0])[0])
+        [VMEM] * (hops + 11 + groups), [pltpu.VMEM((8, columns), F32)] * 3, [pltpu.VMEM((order, columns), F32)],
+    )(*totals, held_schur, csum, coarse_inv, *csum2s, *images, *loads, low2s[0], jumps[0], *recvs[:2])
+    total, norm1, energy = vmem(total), vmem(norm1), vmem(energy)
 
     devices = lax.axis_size("sub") * lax.axis_size("grp")
     spread = call(
-        last_sums, [VMEM] * (5 + len(recvs[1])), [pltpu.VMEM((devices, 8, LANES), F32)],
-    )(total, norm1, energy, low2s[1], jumps[1], *recvs[1])[0]
+        last_sums, [VMEM] * 7, [pltpu.VMEM((devices, 2, columns), F32)],
+    )(total, norm1, energy, low2s[1], jumps[1], *recvs[1:])[0]
     gathered = lax.all_to_all(spread, ("sub", "grp"), 0, 0, tiled=True)
 
     return call(
         finish, [VMEM] * (4 + groups),
         [jax.ShapeDtypeStruct((subs, order, columns), F32)],
-        [pltpu.VMEM((subs, order, columns), F32), dma((subs,))], limit=9, in_hbm=(0,),
+        [pltpu.VMEM((subs, order, columns), F32), dma((subs, 2))], limit=9, in_hbm=(0,),
     )(total, vmem(gathered), *loads, *images)[0]
 
 

time: 144 us -> 147 us (1.021)
  waiting for transfers between devices: 65.2 us -> 71.5 us
  blocking collectives: 14.4 us -> 11.7 us
  starting transfers between devices: 34.2 us -> 32.7 us
    ppermute x6 -> x5, waiting for transfers between devices: 17.2 us -> 23.6 us  [the longest x3 13.7 us: hub_sum(): total = total + lax.ppermute(value, axis, route)]
    all_to_all x1, blocking collectives: 14.4 us -> 11.7 us  [iterate(): gathered = lax.all_to_all(spread, ('sub', 'grp'), 0, 0, tiled=True)]
    ppermute x10 -> x9, starting transfers between devices: 16.4 us -> 14.7 us  [shifted(): return lax.ppermute(block, axis, route)]
    ppermute x10 -> x9, waiting for transfers between devices: 28.7 us -> 28.1 us  [shifted(): return lax.ppermute(block, axis, route)]
    ppermute x6 -> x5, starting transfers between devices: 7.76 us -> 8.01 us  [the longest x3 6.05 us: hub_sum(): total = total + lax.ppermute(value, axis, route)]
  transfers between devices with their start and end apart: 25 -> 23, of which waited for: 14 -> 12; matrix products, arithmetic and copies ran while one was open for 0% -> 0% of each run, Pallas kernels for 14% -> 14%
where the time goes in v3:
time: 147 us; the launch traced here: 146 us
  waiting for transfers between devices  71.5 us (49%)
  starting transfers between devices  32.7 us (22%)
  Pallas kernels  29.9 us (20%)
  blocking collectives  11.7 us (8%)
    ppermute x9, waiting for transfers between devices, shifted(): return lax.ppermute(block, axis, route)  28.1 us
    ppermute x9, waiting for transfers between devices, group_sum(): lax.ppermute(value, axis, [(i ^ hop, i) for i in range(size)])  19.8 us
    ppermute x9, starting transfers between devices, shifted(): return lax.ppermute(block, axis, route)  14.7 us
    ppermute x3, waiting for transfers between devices, hub_sum(): total = total + lax.ppermute(value, axis, route)  13.7 us
    all_to_all x1, blocking collectives, iterate(): gathered = lax.all_to_all(spread, ('sub', 'grp'), 0, 0, tiled=True)  11.7 us
    ppermute x9, starting transfers between devices, group_sum(): lax.ppermute(value, axis, [(i ^ hop, i) for i in range(size)])  10 us
    ppermute x2, waiting for transfers between devices, hub_sum(): others = [lax.ppermute(total, axis, [(hub, i)]) for i in range(hub - 1)]  9.96 us
    pallas_call x2, Pallas kernels, iterate(): call(functools.partial(first_image, lo * LANES, n, groups, share), [ANY,...  6.68 us
  transfers between devices with their start and end apart: 23, of which 12 were waited for; matrix products, arithmetic and copies ran while one was open for 0% of the time, Pallas kernels for 14%

profile of v3, /device:TPU:0, one launch (start us, length us, event | category | flops | bytes accessed | tf_op | source)
XLA Modules:
  0.0 146.4 jit_solution(13374833118899367481)
XLA Ops:
  0.0 2.1 %shard_map.64 = (f32[4,1024,128]{2,1,0:T(8,128)S(1)}, bf16[4,8,128,128]{3,2,1,0:T(8,128)(2,1)S(1)}, bf16[16,128,128]{2,1,0:T(8,128)(2,1)S(1)}, f32[8,128]{1,0:T(8,128)S(1)}, f32[128,128]{1,0:T(8,128)S(1)}) custom-call(s32[4,4]{1,0:T(4,128)} %partner_hbm.9, s32[4,8]{1,0:T(4,128)} %cmap_hbm.9, f32[4,1024,384]{2,1,0:T(8,128)} %load_hbm.7, ...), custom_call_target="tpu_custom_call" | custom-call | tf_op jit(solution)/shard_map/pallas_call | solution.py:381
  2.2 2.1 %shard_map.65 = (f32[4,1024,128]{2,1,0:T(8,128)S(1)}, bf16[16,128,128]{2,1,0:T(8,128)(2,1)S(1)}, bf16[16,128,128]{2,1,0:T(8,128)(2,1)S(1)}, f32[8,128]{1,0:T(8,128)S(1)}, f32[128,128]{1,0:T(8,128)S(1)}) custom-call(s32[4,4]{1,0:T(4,128)} %partner_hbm.9, s32[4,8]{1,0:T(4,128)} %cmap_hbm.9, f32[4,1024,384]{2,1,0:T(8,128)} %load_hbm.7, ...), custom_call_target="tpu_custom_call" | custom-call | tf_op jit(solution)/shard_map/pallas_call | solution.py:381
  4.2 2.1 %shard_map.66 = (f32[4,1024,128]{2,1,0:T(8,128)S(1)}, bf16[16,128,128]{2,1,0:T(8,128)(2,1)S(1)}, bf16[16,128,128]{2,1,0:T(8,128)(2,1)S(1)}, f32[8,128]{1,0:T(8,128)S(1)}, f32[128,128]{1,0:T(8,128)S(1)}) custom-call(s32[4,4]{1,0:T(4,128)} %partner_hbm.9, s32[4,8]{1,0:T(4,128)} %cmap_hbm.9, f32[4,1024,384]{2,1,0:T(8,128)} %load_hbm.7, ...), custom_call_target="tpu_custom_call" | custom-call | tf_op jit(solution)/shard_map/pallas_call | solution.py:381
  6.4 0.6 collective-permute-start
  6.9 4.6 %collective-permute-start.4 = (bf16[16,128,128]{2,1,0:T(8,128)(2,1)S(1)}, bf16[16,128,128]{2,1,0:T(8,128)(2,1)S(1)}, u32[]{:S(2)}, u32[]{:S(2)}) collective-permute-start(bf16[16,128,128]{2,1,0:T(8,128)(2,1)S(1)} %get-tuple-element.55.refs_7_), channel_id=1, source_target_pairs={{8,0},{16,8},{24,16},{0,24},{9,1},{17,9},{25,17},{1,25},{10,2},{18... | collective-permute-start | bytes 1572872 | tf_op jit(solution)/shard_map/ppermute | solution.py:19
  11.6 0.0 collective-permute-start.6
  11.6 0.0 collective-permute-start.5
  11.6 1.8 %shard_map.68.refs_6_ = bf16[16,128,128]{2,1,0:T(8,128)(2,1)S(1)} custom-call(f32[4,1024,384]{2,1,0:T(8,128)} %load_hbm.7, bf16[4,8,128,128]{3,2,1,0:T(8,128)(2,1)} %mortar_hbm.1), custom_call_target="tpu_custom_call" | custom-call | tf_op jit(solution)/shard_map/pallas_call | solution.py:370
  13.4 3.9 %collective-permute-start.3 = (bf16[16,128,128]{2,1,0:T(8,128)(2,1)S(1)}, bf16[16,128,128]{2,1,0:T(8,128)(2,1)S(1)}, u32[]{:S(2)}, u32[]{:S(2)}) collective-permute-start(bf16[16,128,128]{2,1,0:T(8,128)(2,1)S(1)} %shard_map.68.refs_6_), channel_id=1, source_target_pairs={{8,0},{16,8},{24,16},{0,24},{9,1},{17,9},{25,17},{1,25},{10,2},{18... | collective-permute-start | bytes 1572872 | tf_op jit(solution)/shard_map/ppermute | solution.py:19
  17.3 1.6 %collective-permute-start.1 = (f32[128,384]{1,0:T(8,128)S(1)}, f32[128,384]{1,0:T(8,128)S(1)}, u32[]{:S(2)}, u32[]{:S(2)}) collective-permute-start(f32[128,384]{1,0:T(8,128)S(1)} %add.36), channel_id=1, source_target_pairs={{2,0},{3,1},{0,2},{1,3},{6,4},{7,5},{4,6},{5,7},{10,8},{11,9},{8,1... | collective-permute-start | bytes 589832 | tf_op jit(solution)/shard_map/ppermute | solution.py:26
  18.8 4.9 %collective-permute-done.1 = f32[128,384]{1,0:T(8,128)S(1)} collective-permute-done((f32[128,384]{1,0:T(8,128)S(1)}, f32[128,384]{1,0:T(8,128)S(1)}, u32[]{:S(2)}, u32[]{:S(2)}) %collective-permute-start.1) | collective-permute-done | bytes 196640 | tf_op jit(solution)/shard_map/ppermute | solution.py:26
  23.8 1.6 %collective-permute-start.2 = (f32[128,384]{1,0:T(8,128)S(1)}, f32[128,384]{1,0:T(8,128)S(1)}, u32[]{:S(2)}, u32[]{:S(2)}) collective-permute-start(f32[128,384]{1,0:T(8,128)S(1)} %add.37), channel_id=1, source_target_pairs={{4,0},{5,1},{6,2},{7,3},{0,4},{1,5},{2,6},{3,7},{12,8},{13,9},{14,... | collective-permute-start | bytes 589832 | tf_op jit(solution)/shard_map/ppermute | solution.py:26
  25.4 2.8 %collective-permute-start.10 = (bf16[16,128,128]{2,1,0:T(8,128)(2,1)S(1)}, bf16[16,128,128]{2,1,0:T(8,128)(2,1)S(1)}, u32[]{:S(2)}, u32[]{:S(2)}) collective-permute-start(bf16[16,128,128]{2,1,0:T(8,128)(2,1)S(1)} %get-tuple-element.60.refs_3_), channel_id=1, source_target_pairs={{8,0},{16,8},{24,16},{0,24},{9,1},{17,9},{25,17},{1,25},{10,2},{18... | collective-permute-start | bytes 1572872 | tf_op jit(solution)/shard_map/ppermute | solution.py:19
  28.2 1.3 collective-permute-done.2
  29.5 0.0 collective-permute-start.11
  29.5 6.7 %shard_map.67 = (f32[4,1024,256]{2,1,0:T(8,128)S(1)}, f32[4,1024,128]{2,1,0:T(8,128)S(1)}, bf16[4,1024,1024]{2,1,0:T(8,128)(2,1)S(1)}, bf16[4,8,128,128]{3,2,1,0:T(8,128)(2,1)S(1)}) custom-call(bf16[4,1024,1024]{2,1,0:T(8,128)(2,1)} %schur_hbm.1, bf16[4,8,128,128]{3,2,1,0:T(8,128)(2,1)S(1)} %get-tuple-element.41.mortar_in.mortar, ...), custom_call_target="tpu_custom_call" | custom-call | tf_op jit(solution)/shard_map/pallas_call | solution.py:399
  36.2 0.0 collective-permute-done.6.refs_11_
  36.2 11.1 %collective-permute-done.5.refs_10_ = bf16[16,128,128]{2,1,0:T(8,128)(2,1)S(1)} collective-permute-done((bf16[16,128,128]{2,1,0:T(8,128)(2,1)S(1)}, bf16[16,128,128]{2,1,0:T(8,128)(2,1)S(1)}, u32[]{:S(2)}, u32[]{:S(2)}) %collective-permute-start.5) | collective-permute-done | bytes 524320 | tf_op jit(solution)/shard_map/ppermute | solution.py:19
  47.3 10.4 %collective-permute-done.3.refs_8_ = bf16[16,128,128]{2,1,0:T(8,128)(2,1)S(1)} collective-permute-done((bf16[16,128,128]{2,1,0:T(8,128)(2,1)S(1)}, bf16[16,128,128]{2,1,0:T(8,128)(2,1)S(1)}, u32[]{:S(2)}, u32[]{:S(2)}) %collective-permute-start.3) | collective-permute-done | bytes 524320 | tf_op jit(solution)/shard_map/ppermute | solution.py:19
  57.7 3.9 %shard_map.69 = (f32[4,1024,256]{2,1,0:T(8,128)S(1)}, bf16[14,128,256]{2,1,0:T(8,128)(2,1)S(1)}, bf16[2,128,256]{2,1,0:T(8,128)(2,1)S(1)}, bf16[16,128,256]{2,1,...) custom-call(s32[4,4]{1,0:T(4,128)} %partner_hbm.9, ...), custom_call_target="tpu_custom_call", output_to_operand_aliasing={{0}: (4, {})} | custom-call | tf_op jit(solution)/shard_map/pallas_call | solution.py:414
  61.6 0.4 collective-permute-start.20
  62.0 0.0 collective-permute-start.7
  62.0 1.4 collective-permute-done.7
  63.4 1.5 %collective-permute-start.8 = (f32[136,256]{1,0:T(8,128)S(1)}, f32[136,256]{1,0:T(8,128)S(1)}, u32[]{:S(2)}, u32[]{:S(2)}) collective-permute-start(f32[136,256]{1,0:T(8,128)S(1)} %add.39), channel_id=1, source_target_pairs={{2,0},{3,1},{0,2},{1,3},{6,4},{7,5},{4,6},{5,7},{10,8},{11,9},{8,1... | collective-permute-start | bytes 417800 | tf_op jit(solution)/shard_map/ppermute | solution.py:26
  64.9 4.3 %collective-permute-done.8 = f32[136,256]{1,0:T(8,128)S(1)} collective-permute-done((f32[136,256]{1,0:T(8,128)S(1)}, f32[136,256]{1,0:T(8,128)S(1)}, u32[]{:S(2)}, u32[]{:S(2)}) %collective-permute-start.8) | collective-permute-done | bytes 139296 | tf_op jit(solution)/shard_map/ppermute | solution.py:26
  69.2 1.6 %collective-permute-start.9 = (f32[136,256]{1,0:T(8,128)S(1)}, f32[136,256]{1,0:T(8,128)S(1)}, u32[]{:S(2)}, u32[]{:S(2)}) collective-permute-start(f32[136,256]{1,0:T(8,128)S(1)} %add.40), channel_id=1, source_target_pairs={{4,0},{5,1},{6,2},{7,3},{0,4},{1,5},{2,6},{3,7},{12,8},{13,9},{14,... | collective-permute-start | bytes 417800 | tf_op jit(solution)/shard_map/ppermute | solution.py:26
  70.8 3.5 %collective-permute-done.9 = f32[136,256]{1,0:T(8,128)S(1)} collective-permute-done((f32[136,256]{1,0:T(8,128)S(1)}, f32[136,256]{1,0:T(8,128)S(1)}, u32[]{:S(2)}, u32[]{:S(2)}) %collective-permute-start.9) | collective-permute-done | bytes 139296 | tf_op jit(solution)/shard_map/ppermute | solution.py:26
  74.3 0.0 collective-permute-done.10.refs_4_
  74.4 6.7 %collective-permute-done.11.refs_5_ = bf16[16,128,128]{2,1,0:T(8,128)(2,1)S(1)} collective-permute-done((bf16[16,128,128]{2,1,0:T(8,128)(2,1)S(1)}, bf16[16,128,128]{2,1,0:T(8,128)(2,1)S(1)}, u32[]{:S(2)}, u32[]{:S(2)}) %collective-permute-start.11) | collective-permute-done | bytes 524320 | tf_op jit(solution)/shard_map/ppermute | solution.py:19
  81.0 2.8 %shard_map.70 = (f32[4,1024,128]{2,1,0:T(8,128)S(1)}, bf16[8,128,128]{2,1,0:T(8,128)(2,1)S(1)}, bf16[12,128,128]{2,1,0:T(8,128)(2,1)S(1)}, bf16[16,128,128]{2,1,...) custom-call(s32[4,4]{1,0:T(4,128)} %partner_hbm.9, ...), custom_call_target="tpu_custom_call", output_to_operand_aliasing={{0}: (4, {})} | custom-call | tf_op jit(solution)/shard_map/pallas_call | solution.py:414
  83.8 0.1 collective-permute-start.12
  83.9 1.7 %collective-permute-start.22 = (bf16[12,128,128]{2,1,0:T(8,128)(2,1)S(1)}, bf16[12,128,128]{2,1,0:T(8,128)(2,1)S(1)}, u32[]{:S(2)}, u32[]{:S(2)}) collective-permute-start(bf16[12,128,128]{2,1,0:T(8,128)(2,1)S(1)} %get-tuple-element.76), channel_id=1, source_target_pairs={{24,0},{0,8},{8,16},{16,24},{25,1},{1,9},{9,17},{17,25},{26,2},{2,... | collective-permute-start | bytes 1179656 | tf_op jit(solution)/shard_map/ppermute | solution.py:19
  85.6 1.6 %collective-permute-start.13 = (f32[136,128]{1,0:T(8,128)S(1)}, f32[136,128]{1,0:T(8,128)S(1)}, u32[]{:S(2)}, u32[]{:S(2)}) collective-permute-start(f32[136,128]{1,0:T(8,128)S(1)} %add.42), channel_id=1, source_target_pairs={{2,0},{3,1},{0,2},{1,3},{6,4},{7,5},{4,6},{5,7},{10,8},{11,9},{8,1... | collective-permute-start | bytes 208904 | tf_op jit(solution)/shard_map/ppermute | solution.py:26
  87.2 2.8 %collective-permute-done.13 = f32[136,128]{1,0:T(8,128)S(1)} collective-permute-done((f32[136,128]{1,0:T(8,128)S(1)}, f32[136,128]{1,0:T(8,128)S(1)}, u32[]{:S(2)}, u32[]{:S(2)}) %collective-permute-start.13) | collective-permute-done | bytes 69664 | tf_op jit(solution)/shard_map/ppermute | solution.py:26
  90.0 1.6 %collective-permute-start.14 = (f32[136,128]{1,0:T(8,128)S(1)}, f32[136,128]{1,0:T(8,128)S(1)}, u32[]{:S(2)}, u32[]{:S(2)}) collective-permute-start(f32[136,128]{1,0:T(8,128)S(1)} %add.43), channel_id=1, source_target_pairs={{4,0},{5,1},{6,2},{7,3},{0,4},{1,5},{2,6},{3,7},{12,8},{13,9},{14,... | collective-permute-start | bytes 208904 | tf_op jit(solution)/shard_map/ppermute | solution.py:26
  91.6 1.2 collective-permute-start.21
  92.8 1.6 %collective-permute-done.14 = f32[136,128]{1,0:T(8,128)S(1)} collective-permute-done((f32[136,128]{1,0:T(8,128)S(1)}, f32[136,128]{1,0:T(8,128)S(1)}, u32[]{:S(2)}, u32[]{:S(2)}) %collective-permute-start.14) | collective-permute-done | bytes 69664 | tf_op jit(solution)/shard_map/ppermute | solution.py:26
  94.4 4.1 %collective-permute-start.15 = (f32[8,128]{1,0:T(8,128)S(1)}, f32[8,128]{1,0:T(8,128)S(1)}, u32[]{:S(2)}, u32[]{:S(2)}) collective-permute-start(f32[8,128]{1,0:T(8,128)S(1)} %slice.4), channel_id=1, source_target_pairs={{0,24},{24,16},{1,25},{25,17},{2,26},{26,18},{3,27},{27,19},{4,28}... | collective-permute-start | bytes 12296 | tf_op jit(solution)/shard_map/ppermute | solution.py:37
  98.5 1.3 collective-permute-start.16
  99.8 13.7 %collective-permute-done.15 = f32[8,128]{1,0:T(8,128)S(1)} collective-permute-done((f32[8,128]{1,0:T(8,128)S(1)}, f32[8,128]{1,0:T(8,128)S(1)}, u32[]{:S(2)}, u32[]{:S(2)}) %collective-permute-start.15) | collective-permute-done | bytes 4128 | tf_op jit(solution)/shard_map/ppermute | solution.py:37
  113.5 0.6 collective-permute-start.17
  114.2 1.3 collective-permute-start.18
  115.5 0.7 collective-permute-start.19
  116.1 10.0 %collective-permute-done.18.refs_1_ = f32[8,128]{1,0:T(8,128)S(1)} collective-permute-done((f32[8,128]{1,0:T(8,128)S(1)}, f32[8,128]{1,0:T(8,128)S(1)}, u32[]{:S(2)}, u32[]{:S(2)}) %collective-permute-start.18) | collective-permute-done | bytes 4128 | tf_op jit(solution)/shard_map/ppermute | solution.py:38
  126.1 5.2 %shard_map.71 = (f32[8,384]{1,0:T(8,128)S(1)}, f32[8,384]{1,0:T(8,128)S(1)}, f32[8,384]{1,0:T(8,128)S(1)}) custom-call(f32[8,128]{1,0:T(8,128)S(1)} %add_add_fusion.refs_0_, f32[8,128]{1,0:T(8,128)S(1)} %collective-permute-done.18.refs_1_, f32[8,128]{1,0:T(8,128)S(1)} %collective-permute-done.19.refs_2_, ...), custom_call_target="tpu_custom_call" | custom-call | tf_op jit(solution)/shard_map/pallas_call | solution.py:438
  131.4 0.4 shard_map.72
  131.8 11.7 %all_to_all.5.gathered = f32[32,2,384]{2,1,0:T(2,128)S(1)} all-to-all(f32[32,2,384]{2,1,0:T(2,128)S(1)} %shard_map.72), channel_id=1, replica_groups=mesh['sub'=4,'grp'=8] {'sub','grp'}, dimensions={0} | all-to-all | bytes 196608 | tf_op jit(solution)/shard_map/all_to_all | solution.py:448
  143.5 2.9 %shard_map.73 = f32[4,1024,384]{2,1,0:T(8,128)} custom-call(f32[8,384]{1,0:T(8,128)S(1)} %get-tuple-element.71.total, f32[32,2,384]{2,1,0:T(2,128)S(1)} %all_to_all.5.gathered, f32[4,1024,128]{2,1,0:T(8,128)S(1)} %get-tuple-element.42.refs_0_.refs_10_, f32[4,1024,128]{2,1,0:T(8,128)S(1)} %get-tuple-element.43.refs_1_.refs_11_, ...), custom_call_target="tpu_custom_call" | custom-call | tf_op jit(solution)/shard_map/pallas_call | solution.py:450
  (25 shorter events, 0.2 us)
Async XLA Ops:
  6.4 10.9 %collective-permute-start = (f32[128,384]{1,0:T(8,128)S(1)}, f32[128,384]{1,0:T(8,128)S(1)}, u32[]{:S(2)}, u32[]{:S(2)}) collective-permute-start(f32[128,384]{1,0:T(8,128)S(1)} %constant_dynamic-update-slice_fusion), channel_id=1, source_target_pairs={{1,0},{0,1},{3,2},{2,3},{5,4},{4,5},{7,6},{6,7},{9,8},{8,9},{11,10... | collective-permute-start | bytes 589832 | tf_op jit(solution)/shard_map/ppermute | solution.py:26
  6.9 18.4 %collective-permute-start.4 = (bf16[16,128,128]{2,1,0:T(8,128)(2,1)S(1)}, bf16[16,128,128]{2,1,0:T(8,128)(2,1)S(1)}, u32[]{:S(2)}, u32[]{:S(2)}) collective-permute-start(bf16[16,128,128]{2,1,0:T(8,128)(2,1)S(1)} %get-tuple-element.55.refs_7_), channel_id=1, source_target_pairs={{8,0},{16,8},{24,16},{0,24},{9,1},{17,9},{25,17},{1,25},{10,2},{18... | collective-permute-start | bytes 1572872 | tf_op jit(solution)/shard_map/ppermute | solution.py:19
  11.6 24.6 %collective-permute-start.6 = (bf16[16,128,128]{2,1,0:T(8,128)(2,1)S(1)}, bf16[16,128,128]{2,1,0:T(8,128)(2,1)S(1)}, u32[]{:S(2)}, u32[]{:S(2)}) collective-permute-start(bf16[16,128,128]{2,1,0:T(8,128)(2,1)S(1)} %get-tuple-element.54.refs_5_), channel_id=1, source_target_pairs={{24,0},{0,8},{8,16},{16,24},{25,1},{1,9},{9,17},{17,25},{26,2},{2,... | collective-permute-start | bytes 1572872 | tf_op jit(solution)/shard_map/ppermute | solution.py:19
  11.6 35.7 %collective-permute-start.5 = (bf16[16,128,128]{2,1,0:T(8,128)(2,1)S(1)}, bf16[16,128,128]{2,1,0:T(8,128)(2,1)S(1)}, u32[]{:S(2)}, u32[]{:S(2)}) collective-permute-start(bf16[16,128,128]{2,1,0:T(8,128)(2,1)S(1)} %get-tuple-element.53.refs_4_), channel_id=1, source_target_pairs={{24,0},{0,8},{8,16},{16,24},{25,1},{1,9},{9,17},{17,25},{26,2},{2,... | collective-permute-start | bytes 1572872 | tf_op jit(solution)/shard_map/ppermute | solution.py:19
  13.4 44.3 %collective-permute-start.3 = (bf16[16,128,128]{2,1,0:T(8,128)(2,1)S(1)}, bf16[16,128,128]{2,1,0:T(8,128)(2,1)S(1)}, u32[]{:S(2)}, u32[]{:S(2)}) collective-permute-start(bf16[16,128,128]{2,1,0:T(8,128)(2,1)S(1)} %shard_map.68.refs_6_), channel_id=1, source_target_pairs={{8,0},{16,8},{24,16},{0,24},{9,1},{17,9},{25,17},{1,25},{10,2},{18... | collective-permute-start | bytes 1572872 | tf_op jit(solution)/shard_map/ppermute | solution.py:19
  17.3 6.5 %collective-permute-start.1 = (f32[128,384]{1,0:T(8,128)S(1)}, f32[128,384]{1,0:T(8,128)S(1)}, u32[]{:S(2)}, u32[]{:S(2)}) collective-permute-start(f32[128,384]{1,0:T(8,128)S(1)} %add.36), channel_id=1, source_target_pairs={{2,0},{3,1},{0,2},{1,3},{6,4},{7,5},{4,6},{5,7},{10,8},{11,9},{8,1... | collective-permute-start | bytes 589832 | tf_op jit(solution)/shard_map/ppermute | solution.py:26
  23.8 5.7 %collective-permute-start.2 = (f32[128,384]{1,0:T(8,128)S(1)}, f32[128,384]{1,0:T(8,128)S(1)}, u32[]{:S(2)}, u32[]{:S(2)}) collective-permute-start(f32[128,384]{1,0:T(8,128)S(1)} %add.37), channel_id=1, source_target_pairs={{4,0},{5,1},{6,2},{7,3},{0,4},{1,5},{2,6},{3,7},{12,8},{13,9},{14,... | collective-permute-start | bytes 589832 | tf_op jit(solution)/shard_map/ppermute | solution.py:26
  25.4 49.0 %collective-permute-start.10 = (bf16[16,128,128]{2,1,0:T(8,128)(2,1)S(1)}, bf16[16,128,128]{2,1,0:T(8,128)(2,1)S(1)}, u32[]{:S(2)}, u32[]{:S(2)}) collective-permute-start(bf16[16,128,128]{2,1,0:T(8,128)(2,1)S(1)} %get-tuple-element.60.refs_3_), channel_id=1, source_target_pairs={{8,0},{16,8},{24,16},{0,24},{9,1},{17,9},{25,17},{1,25},{10,2},{18... | collective-permute-start | bytes 1572872 | tf_op jit(solution)/shard_map/ppermute | solution.py:19
  29.5 51.5 %collective-permute-start.11 = (bf16[16,128,128]{2,1,0:T(8,128)(2,1)S(1)}, bf16[16,128,128]{2,1,0:T(8,128)(2,1)S(1)}, u32[]{:S(2)}, u32[]{:S(2)}) collective-permute-start(bf16[16,128,128]{2,1,0:T(8,128)(2,1)S(1)} %get-tuple-element.59.refs_2_), channel_id=1, source_target_pairs={{24,0},{0,8},{8,16},{16,24},{25,1},{1,9},{9,17},{17,25},{26,2},{2,... | collective-permute-start | bytes 1572872 | tf_op jit(solution)/shard_map/ppermute | solution.py:19
  29.5 28.2 %copy-start = (f32[1,128,128]{2,1,0:T(8,128)S(1)}, f32[1,128,128]{2,1,0:T(8,128)}, u32[]{:S(2)}) copy-start(f32[1,128,128]{2,1,0:T(8,128)} %refs_5_.1) | copy-start | bytes 196612
  61.6 64.5 %collective-permute-start.20 = (bf16[14,128,256]{2,1,0:T(8,128)(2,1)S(1)}, bf16[14,128,256]{2,1,0:T(8,128)(2,1)S(1)}, u32[]{:S(2)}, u32[]{:S(2)}) collective-permute-start(bf16[14,128,256]{2,1,0:T(8,128)(2,1)S(1)} %get-tuple-element.69), channel_id=1, source_target_pairs={{24,0},{0,8},{8,16},{16,24},{25,1},{1,9},{9,17},{17,25},{26,2},{2,... | collective-permute-start | bytes 2752520 | tf_op jit(solution)/shard_map/ppermute | solution.py:19
  62.0 1.4 collective-permute-start.7
  63.4 5.8 %collective-permute-start.8 = (f32[136,256]{1,0:T(8,128)S(1)}, f32[136,256]{1,0:T(8,128)S(1)}, u32[]{:S(2)}, u32[]{:S(2)}) collective-permute-start(f32[136,256]{1,0:T(8,128)S(1)} %add.39), channel_id=1, source_target_pairs={{2,0},{3,1},{0,2},{1,3},{6,4},{7,5},{4,6},{5,7},{10,8},{11,9},{8,1... | collective-permute-start | bytes 417800 | tf_op jit(solution)/shard_map/ppermute | solution.py:26
  69.2 5.1 %collective-permute-start.9 = (f32[136,256]{1,0:T(8,128)S(1)}, f32[136,256]{1,0:T(8,128)S(1)}, u32[]{:S(2)}, u32[]{:S(2)}) collective-permute-start(f32[136,256]{1,0:T(8,128)S(1)} %add.40), channel_id=1, source_target_pairs={{4,0},{5,1},{6,2},{7,3},{0,4},{1,5},{2,6},{3,7},{12,8},{13,9},{14,... | collective-permute-start | bytes 417800 | tf_op jit(solution)/shard_map/ppermute | solution.py:26
  83.8 1.7 %collective-permute-start.12 = (f32[136,128]{1,0:T(8,128)S(1)}, f32[136,128]{1,0:T(8,128)S(1)}, u32[]{:S(2)}, u32[]{:S(2)}) collective-permute-start(f32[136,128]{1,0:T(8,128)S(1)} %get-tuple-element.63), channel_id=1, source_target_pairs={{1,0},{0,1},{3,2},{2,3},{5,4},{4,5},{7,6},{6,7},{9,8},{8,9},{11,10... | collective-permute-start | bytes 208904 | tf_op jit(solution)/shard_map/ppermute | solution.py:26
  83.9 47.5 %collective-permute-start.22 = (bf16[12,128,128]{2,1,0:T(8,128)(2,1)S(1)}, bf16[12,128,128]{2,1,0:T(8,128)(2,1)S(1)}, u32[]{:S(2)}, u32[]{:S(2)}) collective-permute-start(bf16[12,128,128]{2,1,0:T(8,128)(2,1)S(1)} %get-tuple-element.76), channel_id=1, source_target_pairs={{24,0},{0,8},{8,16},{16,24},{25,1},{1,9},{9,17},{17,25},{26,2},{2,... | collective-permute-start | bytes 1179656 | tf_op jit(solution)/shard_map/ppermute | solution.py:19
  85.6 4.4 %collective-permute-start.13 = (f32[136,128]{1,0:T(8,128)S(1)}, f32[136,128]{1,0:T(8,128)S(1)}, u32[]{:S(2)}, u32[]{:S(2)}) collective-permute-start(f32[136,128]{1,0:T(8,128)S(1)} %add.42), channel_id=1, source_target_pairs={{2,0},{3,1},{0,2},{1,3},{6,4},{7,5},{4,6},{5,7},{10,8},{11,9},{8,1... | collective-permute-start | bytes 208904 | tf_op jit(solution)/shard_map/ppermute | solution.py:26
  90.0 4.4 %collective-permute-start.14 = (f32[136,128]{1,0:T(8,128)S(1)}, f32[136,128]{1,0:T(8,128)S(1)}, u32[]{:S(2)}, u32[]{:S(2)}) collective-permute-start(f32[136,128]{1,0:T(8,128)S(1)} %add.43), channel_id=1, source_target_pairs={{4,0},{5,1},{6,2},{7,3},{0,4},{1,5},{2,6},{3,7},{12,8},{13,9},{14,... | collective-permute-start | bytes 208904 | tf_op jit(solution)/shard_map/ppermute | solution.py:26
  91.6 34.5 %collective-permute-start.21 = (bf16[8,128,128]{2,1,0:T(8,128)(2,1)S(1)}, bf16[8,128,128]{2,1,0:T(8,128)(2,1)S(1)}, u32[]{:S(2)}, u32[]{:S(2)}) collective-permute-start(bf16[8,128,128]{2,1,0:T(8,128)(2,1)S(1)} %get-tuple-element.70), channel_id=1, source_target_pairs={{24,0},{0,8},{8,16},{16,24},{25,1},{1,9},{9,17},{17,25},{26,2},{2,... | collective-permute-start | bytes 786440 | tf_op jit(solution)/shard_map/ppermute | solution.py:19
  94.4 19.1 %collective-permute-start.15 = (f32[8,128]{1,0:T(8,128)S(1)}, f32[8,128]{1,0:T(8,128)S(1)}, u32[]{:S(2)}, u32[]{:S(2)}) collective-permute-start(f32[8,128]{1,0:T(8,128)S(1)} %slice.4), channel_id=1, source_target_pairs={{0,24},{24,16},{1,25},{25,17},{2,26},{26,18},{3,27},{27,19},{4,28}... | collective-permute-start | bytes 12296 | tf_op jit(solution)/shard_map/ppermute | solution.py:37
  98.5 15.6 %collective-permute-start.16 = (f32[8,128]{1,0:T(8,128)S(1)}, f32[8,128]{1,0:T(8,128)S(1)}, u32[]{:S(2)}, u32[]{:S(2)}) collective-permute-start(f32[8,128]{1,0:T(8,128)S(1)} %slice.4), channel_id=1, source_target_pairs={{0,16},{8,24},{1,17},{9,25},{2,18},{10,26},{3,19},{11,27},{4,20},{... | collective-permute-start | bytes 12296 | tf_op jit(solution)/shard_map/ppermute | solution.py:37
  113.5 0.7 collective-permute-start.17
  114.2 11.9 %collective-permute-start.18 = (f32[8,128]{1,0:T(8,128)S(1)}, f32[8,128]{1,0:T(8,128)S(1)}, u32[]{:S(2)}, u32[]{:S(2)}) collective-permute-start(f32[8,128]{1,0:T(8,128)S(1)} %add_add_fusion.refs_0_), channel_id=1, source_target_pairs={{24,0},{25,1},{26,2},{27,3},{28,4},{29,5},{30,6},{31,7}} | collective-permute-start | bytes 12296 | tf_op jit(solution)/shard_map/ppermute | solution.py:38
  115.5 10.6 %collective-permute-start.19 = (f32[8,128]{1,0:T(8,128)S(1)}, f32[8,128]{1,0:T(8,128)S(1)}, u32[]{:S(2)}, u32[]{:S(2)}) collective-permute-start(f32[8,128]{1,0:T(8,128)S(1)} %add_add_fusion.refs_0_), channel_id=1, source_target_pairs={{24,8},{25,9},{26,10},{27,11},{28,12},{29,13},{30,14},{31,15}} | collective-permute-start | bytes 12296 | tf_op jit(solution)/shard_map/ppermute | solution.py:38

commit v4 on v3

--- a/solution.py
+++ b/solution.py
@@ -35,7 +35,7 @@
     for d in range(hub, 0, -1):
         route = [(i, (i + d) % size) for i in range(size) if (i + d) % size >= hub - 1]
         total = total + lax.ppermute(value, axis, route)
-    others = [lax.ppermute(total, axis, [(hub, i)]) for i in range(hub - 1)]
+    others = [lax.ppermute(total, axis, [(hub, i)]) for i in reversed(range(hub - 1))]
     return [total] + others
 
 
@@ -254,7 +254,8 @@
     norm[...] = jnp.zeros_like(norm)
     energy[...] = share * fold_rows(change * field)
 
-    slots, subs = low.shape[0], schur.shape[0]
+    slots, subs, order = low.shape[0], schur.shape[0], schur.shape[1]
+    tile = min(256, order)
 
     def received(k, j):
         whole, mixed = recvs
@@ -269,7 +270,14 @@
             resid[:, cols] = load[s] - step[:, cols] * image[s, :, own]
         r = resid[...]
         norm[...] += fold_rows(r * r)
-        energy[...] += fold_rows(r * jnp.dot(schur[s], r.astype(BF16), preferred_element_type=F32))
+        half = r.astype(BF16)
+        for i in range(0, order, tile):
+            rows = slice(i, i + tile)
+            beyond = half[rows, :]
+            if i + tile < order:
+                beyond = jnp.concatenate([beyond, half[i + tile :, :] * BF16(2.0)], axis=0)
+            product = jnp.dot(schur[s, rows, i:], beyond, preferred_element_type=F32)
+            energy[...] += fold_rows(r[rows, :] * product)
         for j in range(groups - 1):
             cols = group_cols(j)
             acc = energy[:, cols]
@@ -406,7 +414,7 @@
     bounds = ((0, groups - 1), (groups - 1, groups))
     share = 1.0 / lax.axis_size("grp")
     images, jumps, low2s, recvs, csum2s, tails = [], [], [], [], [], []
-    tail, lead_slots = 2 * slots // 16, 4 * slots // 16
+    tail, lead_slots = slots // 16, 6 * slots // 16
     cuts = ((slots - tail, tail), ((groups - 1) * tail + lead_slots, slots - lead_slots))
     for k, (lo, hi) in enumerate(bounds):
         n, w = hi - lo, (hi - lo) * LANES

time: 147 us -> 161 us (1.095)
  waiting for transfers between devices: 71.5 us -> 91.2 us
  starting transfers between devices: 32.7 us -> 30.5 us
  blocking collectives: 11.7 us -> 9.5 us
    ppermute x9, waiting for transfers between devices: 28.1 us -> 56.6 us  [shifted(): return lax.ppermute(block, axis, route)]
    ppermute x3, waiting for transfers between devices: 13.7 us -> 0.91 us  [hub_sum(): total = total + lax.ppermute(value, axis, route)]
    ppermute x2, waiting for transfers between devices: 9.96 us -> 12.7 us  [hub_sum(): lax.ppermute(total, axis, [(hub, i)])]
    all_to_all x1, blocking collectives: 11.7 us -> 9.5 us  [iterate(): gathered = lax.all_to_all(spread, ('sub', 'grp'), 0, 0, tiled=True)]
    ppermute x9, starting transfers between devices: 14.7 us -> 12.9 us  [shifted(): return lax.ppermute(block, axis, route)]
  transfers between devices with their start and end apart: 23 -> 23, of which waited for: 12 -> 14; matrix products, arithmetic and copies ran while one was open for 0% -> 0% of each run, Pallas kernels for 14% -> 10%
where the time goes in v4:
time: 161 us; the launch traced here: 160 us
  waiting for transfers between devices  91.2 us (57%)
  starting transfers between devices  30.5 us (19%)
  Pallas kernels  28.8 us (18%)
  blocking collectives  9.5 us (6%)
    ppermute x9, waiting for transfers between devices, shifted(): return lax.ppermute(block, axis, route)  56.6 us
    ppermute x9, waiting for transfers between devices, group_sum(): lax.ppermute(value, axis, [(i ^ hop, i) for i in range(size)])  20.9 us
    ppermute x9, starting transfers between devices, shifted(): return lax.ppermute(block, axis, route)  12.9 us
    ppermute x2, waiting for transfers between devices, hub_sum(): lax.ppermute(total, axis, [(hub, i)])  12.7 us
    ppermute x9, starting transfers between devices, group_sum(): lax.ppermute(value, axis, [(i ^ hop, i) for i in range(size)])  10.1 us
    all_to_all x1, blocking collectives, iterate(): gathered = lax.all_to_all(spread, ('sub', 'grp'), 0, 0, tiled=True)  9.5 us
    pallas_call x1, Pallas kernels, iterate(): call(stiff_product, [ANY] + [VMEM] * (1 + groups), [pltpu.VMEM((subs, ord...  6.65 us
    pallas_call x2, Pallas kernels, iterate(): call(functools.partial(first_image, lo * LANES, n, groups, share), [ANY,...  6.64 us
  transfers between devices with their start and end apart: 23, of which 14 were waited for; matrix products, arithmetic and copies ran while one was open for 0% of the time, Pallas kernels for 10%

profile of v4, /device:TPU:0, one launch (start us, length us, event | category | flops | bytes accessed | tf_op | source)
XLA Modules:
  0.0 160.5 jit_solution(12261831171576638650)
XLA Ops:
  0.0 2.1 %shard_map.64 = (f32[4,1024,128]{2,1,0:T(8,128)S(1)}, bf16[4,8,128,128]{3,2,1,0:T(8,128)(2,1)S(1)}, bf16[16,128,128]{2,1,0:T(8,128)(2,1)S(1)}, f32[8,128]{1,0:T(8,128)S(1)}, f32[128,128]{1,0:T(8,128)S(1)}) custom-call(s32[4,4]{1,0:T(4,128)} %partner_hbm.9, s32[4,8]{1,0:T(4,128)} %cmap_hbm.9, f32[4,1024,384]{2,1,0:T(8,128)} %load_hbm.7, ...), custom_call_target="tpu_custom_call" | custom-call | tf_op jit(solution)/shard_map/pallas_call | solution.py:389
  2.2 2.1 %shard_map.65 = (f32[4,1024,128]{2,1,0:T(8,128)S(1)}, bf16[16,128,128]{2,1,0:T(8,128)(2,1)S(1)}, bf16[16,128,128]{2,1,0:T(8,128)(2,1)S(1)}, f32[8,128]{1,0:T(8,128)S(1)}, f32[128,128]{1,0:T(8,128)S(1)}) custom-call(s32[4,4]{1,0:T(4,128)} %partner_hbm.9, s32[4,8]{1,0:T(4,128)} %cmap_hbm.9, f32[4,1024,384]{2,1,0:T(8,128)} %load_hbm.7, ...), custom_call_target="tpu_custom_call" | custom-call | tf_op jit(solution)/shard_map/pallas_call | solution.py:389
  4.2 2.1 %shard_map.66 = (f32[4,1024,128]{2,1,0:T(8,128)S(1)}, bf16[16,128,128]{2,1,0:T(8,128)(2,1)S(1)}, bf16[16,128,128]{2,1,0:T(8,128)(2,1)S(1)}, f32[8,128]{1,0:T(8,128)S(1)}, f32[128,128]{1,0:T(8,128)S(1)}) custom-call(s32[4,4]{1,0:T(4,128)} %partner_hbm.9, s32[4,8]{1,0:T(4,128)} %cmap_hbm.9, f32[4,1024,384]{2,1,0:T(8,128)} %load_hbm.7, ...), custom_call_target="tpu_custom_call" | custom-call | tf_op jit(solution)/shard_map/pallas_call | solution.py:389
  6.4 0.6 collective-permute-start
  6.9 4.6 %collective-permute-start.4 = (bf16[16,128,128]{2,1,0:T(8,128)(2,1)S(1)}, bf16[16,128,128]{2,1,0:T(8,128)(2,1)S(1)}, u32[]{:S(2)}, u32[]{:S(2)}) collective-permute-start(bf16[16,128,128]{2,1,0:T(8,128)(2,1)S(1)} %get-tuple-element.55.refs_7_), channel_id=1, source_target_pairs={{8,0},{16,8},{24,16},{0,24},{9,1},{17,9},{25,17},{1,25},{10,2},{18... | collective-permute-start | bytes 1572872 | tf_op jit(solution)/shard_map/ppermute | solution.py:19
  11.6 0.0 collective-permute-start.6
  11.6 0.0 collective-permute-start.5
  11.6 1.8 %shard_map.68.refs_6_ = bf16[16,128,128]{2,1,0:T(8,128)(2,1)S(1)} custom-call(f32[4,1024,384]{2,1,0:T(8,128)} %load_hbm.7, bf16[4,8,128,128]{3,2,1,0:T(8,128)(2,1)} %mortar_hbm.1), custom_call_target="tpu_custom_call" | custom-call | tf_op jit(solution)/shard_map/pallas_call | solution.py:378
  13.4 3.9 %collective-permute-start.3 = (bf16[16,128,128]{2,1,0:T(8,128)(2,1)S(1)}, bf16[16,128,128]{2,1,0:T(8,128)(2,1)S(1)}, u32[]{:S(2)}, u32[]{:S(2)}) collective-permute-start(bf16[16,128,128]{2,1,0:T(8,128)(2,1)S(1)} %shard_map.68.refs_6_), channel_id=1, source_target_pairs={{8,0},{16,8},{24,16},{0,24},{9,1},{17,9},{25,17},{1,25},{10,2},{18... | collective-permute-start | bytes 1572872 | tf_op jit(solution)/shard_map/ppermute | solution.py:19
  17.3 1.6 collective-permute-start.1
  18.8 4.9 %collective-permute-done.1 = f32[128,384]{1,0:T(8,128)S(1)} collective-permute-done((f32[128,384]{1,0:T(8,128)S(1)}, f32[128,384]{1,0:T(8,128)S(1)}, u32[]{:S(2)}, u32[]{:S(2)}) %collective-permute-start.1) | collective-permute-done | bytes 196640 | tf_op jit(solution)/shard_map/ppermute | solution.py:26
  23.8 1.6 collective-permute-start.2
  25.4 6.7 %shard_map.67 = (f32[4,1024,256]{2,1,0:T(8,128)S(1)}, f32[4,1024,128]{2,1,0:T(8,128)S(1)}, bf16[4,1024,1024]{2,1,0:T(8,128)(2,1)S(1)}, bf16[4,8,128,128]{3,2,1,0:T(8,128)(2,1)S(1)}) custom-call(bf16[4,1024,1024]{2,1,0:T(8,128)(2,1)} %schur_hbm.1, bf16[4,8,128,128]{3,2,1,0:T(8,128)(2,1)S(1)} %get-tuple-element.41.mortar_in.mortar, ...), custom_call_target="tpu_custom_call" | custom-call | tf_op jit(solution)/shard_map/pallas_call | solution.py:407
  32.1 0.0 collective-permute-done.2
  32.1 0.0 collective-permute-done.4.refs_9_
  32.1 4.0 %collective-permute-done.6.refs_11_ = bf16[16,128,128]{2,1,0:T(8,128)(2,1)S(1)} collective-permute-done((bf16[16,128,128]{2,1,0:T(8,128)(2,1)S(1)}, bf16[16,128,128]{2,1,0:T(8,128)(2,1)S(1)}, u32[]{:S(2)}, u32[]{:S(2)}) %collective-permute-start.6) | collective-permute-done | bytes 524320 | tf_op jit(solution)/shard_map/ppermute | solution.py:19
  36.1 11.2 %collective-permute-done.5.refs_10_ = bf16[16,128,128]{2,1,0:T(8,128)(2,1)S(1)} collective-permute-done((bf16[16,128,128]{2,1,0:T(8,128)(2,1)S(1)}, bf16[16,128,128]{2,1,0:T(8,128)(2,1)S(1)}, u32[]{:S(2)}, u32[]{:S(2)}) %collective-permute-start.5) | collective-permute-done | bytes 524320 | tf_op jit(solution)/shard_map/ppermute | solution.py:19
  47.3 9.8 %collective-permute-done.3.refs_8_ = bf16[16,128,128]{2,1,0:T(8,128)(2,1)S(1)} collective-permute-done((bf16[16,128,128]{2,1,0:T(8,128)(2,1)S(1)}, bf16[16,128,128]{2,1,0:T(8,128)(2,1)S(1)}, u32[]{:S(2)}, u32[]{:S(2)}) %collective-permute-start.3) | collective-permute-done | bytes 524320 | tf_op jit(solution)/shard_map/ppermute | solution.py:19
  57.1 3.9 %shard_map.69 = (f32[4,1024,256]{2,1,0:T(8,128)S(1)}, bf16[15,128,256]{2,1,0:T(8,128)(2,1)S(1)}, bf16[1,128,256]{2,1,0:T(8,128)(2,1)S(1)}, bf16[16,128,256]{2,1,...) custom-call(s32[4,4]{1,0:T(4,128)} %partner_hbm.9, ...), custom_call_target="tpu_custom_call", output_to_operand_aliasing={{0}: (4, {})} | custom-call | tf_op jit(solution)/shard_map/pallas_call | solution.py:422
  61.0 0.5 collective-permute-start.20
  61.5 3.9 %collective-permute-start.10 = (bf16[16,128,128]{2,1,0:T(8,128)(2,1)S(1)}, bf16[16,128,128]{2,1,0:T(8,128)(2,1)S(1)}, u32[]{:S(2)}, u32[]{:S(2)}) collective-permute-start(bf16[16,128,128]{2,1,0:T(8,128)(2,1)S(1)} %get-tuple-element.60.refs_3_), channel_id=1, source_target_pairs={{8,0},{16,8},{24,16},{0,24},{9,1},{17,9},{25,17},{1,25},{10,2},{18... | collective-permute-start | bytes 1572872 | tf_op jit(solution)/shard_map/ppermute | solution.py:19
  65.4 0.0 collective-permute-start.11
  65.4 0.0 collective-permute-start.7
  65.4 1.4 collective-permute-done.7
  66.8 1.6 collective-permute-start.8
  68.3 4.2 %collective-permute-done.8 = f32[136,256]{1,0:T(8,128)S(1)} collective-permute-done((f32[136,256]{1,0:T(8,128)S(1)}, f32[136,256]{1,0:T(8,128)S(1)}, u32[]{:S(2)}, u32[]{:S(2)}) %collective-permute-start.8) | collective-permute-done | bytes 139296 | tf_op jit(solution)/shard_map/ppermute | solution.py:26
  72.6 1.6 collective-permute-start.9
  74.2 3.5 %collective-permute-done.9 = f32[136,256]{1,0:T(8,128)S(1)} collective-permute-done((f32[136,256]{1,0:T(8,128)S(1)}, f32[136,256]{1,0:T(8,128)S(1)}, u32[]{:S(2)}, u32[]{:S(2)}) %collective-permute-start.9) | collective-permute-done | bytes 139296 | tf_op jit(solution)/shard_map/ppermute | solution.py:26
  77.7 17.9 %collective-permute-done.10.refs_4_ = bf16[16,128,128]{2,1,0:T(8,128)(2,1)S(1)} collective-permute-done((bf16[16,128,128]{2,1,0:T(8,128)(2,1)S(1)}, bf16[16,128,128]{2,1,0:T(8,128)(2,1)S(1)}, u32[]{:S(2)}, u32[]{:S(2)}) %collective-permute-start.10) | collective-permute-done | bytes 524320 | tf_op jit(solution)/shard_map/ppermute | solution.py:19
  95.7 13.7 %collective-permute-done.11.refs_5_ = bf16[16,128,128]{2,1,0:T(8,128)(2,1)S(1)} collective-permute-done((bf16[16,128,128]{2,1,0:T(8,128)(2,1)S(1)}, bf16[16,128,128]{2,1,0:T(8,128)(2,1)S(1)}, u32[]{:S(2)}, u32[]{:S(2)}) %collective-permute-start.11) | collective-permute-done | bytes 524320 | tf_op jit(solution)/shard_map/ppermute | solution.py:19
  109.3 2.8 %shard_map.70 = (f32[4,1024,128]{2,1,0:T(8,128)S(1)}, bf16[8,128,128]{2,1,0:T(8,128)(2,1)S(1)}, bf16[10,128,128]{2,1,0:T(8,128)(2,1)S(1)}, bf16[16,128,128]{2,1,...) custom-call(s32[4,4]{1,0:T(4,128)} %partner_hbm.9, ...), custom_call_target="tpu_custom_call", output_to_operand_aliasing={{0}: (4, {})} | custom-call | tf_op jit(solution)/shard_map/pallas_call | solution.py:422
  112.1 0.1 collective-permute-start.12
  112.2 1.2 collective-permute-done.12
  113.5 1.5 collective-permute-start.13
  115.0 2.8 %collective-permute-done.13 = f32[136,128]{1,0:T(8,128)S(1)} collective-permute-done((f32[136,128]{1,0:T(8,128)S(1)}, f32[136,128]{1,0:T(8,128)S(1)}, u32[]{:S(2)}, u32[]{:S(2)}) %collective-permute-start.13) | collective-permute-done | bytes 69664 | tf_op jit(solution)/shard_map/ppermute | solution.py:26
  117.9 1.6 collective-permute-start.14
  119.5 2.8 %collective-permute-done.14 = f32[136,128]{1,0:T(8,128)S(1)} collective-permute-done((f32[136,128]{1,0:T(8,128)S(1)}, f32[136,128]{1,0:T(8,128)S(1)}, u32[]{:S(2)}, u32[]{:S(2)}) %collective-permute-start.14) | collective-permute-done | bytes 69664 | tf_op jit(solution)/shard_map/ppermute | solution.py:26
  122.3 3.6 %collective-permute-start.15 = (f32[8,128]{1,0:T(8,128)S(1)}, f32[8,128]{1,0:T(8,128)S(1)}, u32[]{:S(2)}, u32[]{:S(2)}) collective-permute-start(f32[8,128]{1,0:T(8,128)S(1)} %slice.4), channel_id=1, source_target_pairs={{0,24},{24,16},{1,25},{25,17},{2,26},{26,18},{3,27},{27,19},{4,28}... | collective-permute-start | bytes 12296 | tf_op jit(solution)/shard_map/ppermute | solution.py:37
  125.9 1.3 collective-permute-start.16
  127.2 0.9 collective-permute-done.15
  128.1 0.6 collective-permute-start.17
  128.8 0.7 collective-permute-start.18
  129.4 1.3 collective-permute-start.19
  130.7 12.7 %collective-permute-done.19.refs_2_ = f32[8,128]{1,0:T(8,128)S(1)} collective-permute-done((f32[8,128]{1,0:T(8,128)S(1)}, f32[8,128]{1,0:T(8,128)S(1)}, u32[]{:S(2)}, u32[]{:S(2)}) %collective-permute-start.19) | collective-permute-done | bytes 4128 | tf_op jit(solution)/shard_map/ppermute | solution.py:38
  143.5 4.2 %shard_map.71 = (f32[8,384]{1,0:T(8,128)S(1)}, f32[8,384]{1,0:T(8,128)S(1)}, f32[8,384]{1,0:T(8,128)S(1)}) custom-call(f32[8,128]{1,0:T(8,128)S(1)} %add_add_fusion.refs_0_, f32[8,128]{1,0:T(8,128)S(1)} %collective-permute-done.18.refs_1_, f32[8,128]{1,0:T(8,128)S(1)} %collective-permute-done.19.refs_2_, ...), custom_call_target="tpu_custom_call" | custom-call | tf_op jit(solution)/shard_map/pallas_call | solution.py:446
  147.7 0.4 shard_map.72
  148.1 9.5 %all_to_all.5.gathered = f32[32,2,384]{2,1,0:T(2,128)S(1)} all-to-all(f32[32,2,384]{2,1,0:T(2,128)S(1)} %shard_map.72), channel_id=1, replica_groups=mesh['sub'=4,'grp'=8] {'sub','grp'}, dimensions={0} | all-to-all | bytes 196608 | tf_op jit(solution)/shard_map/all_to_all | solution.py:456
  157.6 2.9 %shard_map.73 = f32[4,1024,384]{2,1,0:T(8,128)} custom-call(f32[8,384]{1,0:T(8,128)S(1)} %get-tuple-element.71.total, f32[32,2,384]{2,1,0:T(2,128)S(1)} %all_to_all.5.gathered, f32[4,1024,128]{2,1,0:T(8,128)S(1)} %get-tuple-element.42.refs_0_.refs_10_, f32[4,1024,128]{2,1,0:T(8,128)S(1)} %get-tuple-element.43.refs_1_.refs_11_, ...), custom_call_target="tpu_custom_call" | custom-call | tf_op jit(solution)/shard_map/pallas_call | solution.py:458
  (25 shorter events, 0.2 us)
Async XLA Ops:
  6.4 10.9 %collective-permute-start = (f32[128,384]{1,0:T(8,128)S(1)}, f32[128,384]{1,0:T(8,128)S(1)}, u32[]{:S(2)}, u32[]{:S(2)}) collective-permute-start(f32[128,384]{1,0:T(8,128)S(1)} %constant_dynamic-update-slice_fusion), channel_id=1, source_target_pairs={{1,0},{0,1},{3,2},{2,3},{5,4},{4,5},{7,6},{6,7},{9,8},{8,9},{11,10... | collective-permute-start | bytes 589832 | tf_op jit(solution)/shard_map/ppermute | solution.py:26
  6.9 25.2 %collective-permute-start.4 = (bf16[16,128,128]{2,1,0:T(8,128)(2,1)S(1)}, bf16[16,128,128]{2,1,0:T(8,128)(2,1)S(1)}, u32[]{:S(2)}, u32[]{:S(2)}) collective-permute-start(bf16[16,128,128]{2,1,0:T(8,128)(2,1)S(1)} %get-tuple-element.55.refs_7_), channel_id=1, source_target_pairs={{8,0},{16,8},{24,16},{0,24},{9,1},{17,9},{25,17},{1,25},{10,2},{18... | collective-permute-start | bytes 1572872 | tf_op jit(solution)/shard_map/ppermute | solution.py:19
  11.6 24.5 %collective-permute-start.6 = (bf16[16,128,128]{2,1,0:T(8,128)(2,1)S(1)}, bf16[16,128,128]{2,1,0:T(8,128)(2,1)S(1)}, u32[]{:S(2)}, u32[]{:S(2)}) collective-permute-start(bf16[16,128,128]{2,1,0:T(8,128)(2,1)S(1)} %get-tuple-element.54.refs_5_), channel_id=1, source_target_pairs={{24,0},{0,8},{8,16},{16,24},{25,1},{1,9},{9,17},{17,25},{26,2},{2,... | collective-permute-start | bytes 1572872 | tf_op jit(solution)/shard_map/ppermute | solution.py:19
  11.6 35.7 %collective-permute-start.5 = (bf16[16,128,128]{2,1,0:T(8,128)(2,1)S(1)}, bf16[16,128,128]{2,1,0:T(8,128)(2,1)S(1)}, u32[]{:S(2)}, u32[]{:S(2)}) collective-permute-start(bf16[16,128,128]{2,1,0:T(8,128)(2,1)S(1)} %get-tuple-element.53.refs_4_), channel_id=1, source_target_pairs={{24,0},{0,8},{8,16},{16,24},{25,1},{1,9},{9,17},{17,25},{26,2},{2,... | collective-permute-start | bytes 1572872 | tf_op jit(solution)/shard_map/ppermute | solution.py:19
  13.4 43.8 %collective-permute-start.3 = (bf16[16,128,128]{2,1,0:T(8,128)(2,1)S(1)}, bf16[16,128,128]{2,1,0:T(8,128)(2,1)S(1)}, u32[]{:S(2)}, u32[]{:S(2)}) collective-permute-start(bf16[16,128,128]{2,1,0:T(8,128)(2,1)S(1)} %shard_map.68.refs_6_), channel_id=1, source_target_pairs={{8,0},{16,8},{24,16},{0,24},{9,1},{17,9},{25,17},{1,25},{10,2},{18... | collective-permute-start | bytes 1572872 | tf_op jit(solution)/shard_map/ppermute | solution.py:19
  17.3 6.5 %collective-permute-start.1 = (f32[128,384]{1,0:T(8,128)S(1)}, f32[128,384]{1,0:T(8,128)S(1)}, u32[]{:S(2)}, u32[]{:S(2)}) collective-permute-start(f32[128,384]{1,0:T(8,128)S(1)} %add.36), channel_id=1, source_target_pairs={{2,0},{3,1},{0,2},{1,3},{6,4},{7,5},{4,6},{5,7},{10,8},{11,9},{8,1... | collective-permute-start | bytes 589832 | tf_op jit(solution)/shard_map/ppermute | solution.py:26
  23.8 8.3 %collective-permute-start.2 = (f32[128,384]{1,0:T(8,128)S(1)}, f32[128,384]{1,0:T(8,128)S(1)}, u32[]{:S(2)}, u32[]{:S(2)}) collective-permute-start(f32[128,384]{1,0:T(8,128)S(1)} %add.37), channel_id=1, source_target_pairs={{4,0},{5,1},{6,2},{7,3},{0,4},{1,5},{2,6},{3,7},{12,8},{13,9},{14,... | collective-permute-start | bytes 589832 | tf_op jit(solution)/shard_map/ppermute | solution.py:26
  25.4 31.7 %copy-start = (f32[1,128,128]{2,1,0:T(8,128)S(1)}, f32[1,128,128]{2,1,0:T(8,128)}, u32[]{:S(2)}) copy-start(f32[1,128,128]{2,1,0:T(8,128)} %refs_5_.1) | copy-start | bytes 196612
  61.0 82.5 %collective-permute-start.20 = (bf16[15,128,256]{2,1,0:T(8,128)(2,1)S(1)}, bf16[15,128,256]{2,1,0:T(8,128)(2,1)S(1)}, u32[]{:S(2)}, u32[]{:S(2)}) collective-permute-start(bf16[15,128,256]{2,1,0:T(8,128)(2,1)S(1)} %get-tuple-element.69), channel_id=1, source_target_pairs={{24,0},{0,8},{8,16},{16,24},{25,1},{1,9},{9,17},{17,25},{26,2},{2,... | collective-permute-start | bytes 2949128 | tf_op jit(solution)/shard_map/ppermute | solution.py:19
  61.5 34.2 %collective-permute-start.10 = (bf16[16,128,128]{2,1,0:T(8,128)(2,1)S(1)}, bf16[16,128,128]{2,1,0:T(8,128)(2,1)S(1)}, u32[]{:S(2)}, u32[]{:S(2)}) collective-permute-start(bf16[16,128,128]{2,1,0:T(8,128)(2,1)S(1)} %get-tuple-element.60.refs_3_), channel_id=1, source_target_pairs={{8,0},{16,8},{24,16},{0,24},{9,1},{17,9},{25,17},{1,25},{10,2},{18... | collective-permute-start | bytes 1572872 | tf_op jit(solution)/shard_map/ppermute | solution.py:19
  65.4 44.0 %collective-permute-start.11 = (bf16[16,128,128]{2,1,0:T(8,128)(2,1)S(1)}, bf16[16,128,128]{2,1,0:T(8,128)(2,1)S(1)}, u32[]{:S(2)}, u32[]{:S(2)}) collective-permute-start(bf16[16,128,128]{2,1,0:T(8,128)(2,1)S(1)} %get-tuple-element.59.refs_2_), channel_id=1, source_target_pairs={{24,0},{0,8},{8,16},{16,24},{25,1},{1,9},{9,17},{17,25},{26,2},{2,... | collective-permute-start | bytes 1572872 | tf_op jit(solution)/shard_map/ppermute | solution.py:19
  65.4 1.4 collective-permute-start.7
  66.8 5.8 %collective-permute-start.8 = (f32[136,256]{1,0:T(8,128)S(1)}, f32[136,256]{1,0:T(8,128)S(1)}, u32[]{:S(2)}, u32[]{:S(2)}) collective-permute-start(f32[136,256]{1,0:T(8,128)S(1)} %add.39), channel_id=1, source_target_pairs={{2,0},{3,1},{0,2},{1,3},{6,4},{7,5},{4,6},{5,7},{10,8},{11,9},{8,1... | collective-permute-start | bytes 417800 | tf_op jit(solution)/shard_map/ppermute | solution.py:26
  72.6 5.1 %collective-permute-start.9 = (f32[136,256]{1,0:T(8,128)S(1)}, f32[136,256]{1,0:T(8,128)S(1)}, u32[]{:S(2)}, u32[]{:S(2)}) collective-permute-start(f32[136,256]{1,0:T(8,128)S(1)} %add.40), channel_id=1, source_target_pairs={{4,0},{5,1},{6,2},{7,3},{0,4},{1,5},{2,6},{3,7},{12,8},{13,9},{14,... | collective-permute-start | bytes 417800 | tf_op jit(solution)/shard_map/ppermute | solution.py:26
  112.1 1.3 collective-permute-start.12
  113.5 4.4 %collective-permute-start.13 = (f32[136,128]{1,0:T(8,128)S(1)}, f32[136,128]{1,0:T(8,128)S(1)}, u32[]{:S(2)}, u32[]{:S(2)}) collective-permute-start(f32[136,128]{1,0:T(8,128)S(1)} %add.42), channel_id=1, source_target_pairs={{2,0},{3,1},{0,2},{1,3},{6,4},{7,5},{4,6},{5,7},{10,8},{11,9},{8,1... | collective-permute-start | bytes 208904 | tf_op jit(solution)/shard_map/ppermute | solution.py:26
  115.0 32.7 %collective-permute-start.22 = (bf16[10,128,128]{2,1,0:T(8,128)(2,1)S(1)}, bf16[10,128,128]{2,1,0:T(8,128)(2,1)S(1)}, u32[]{:S(2)}, u32[]{:S(2)}) collective-permute-start(bf16[10,128,128]{2,1,0:T(8,128)(2,1)S(1)} %get-tuple-element.76), channel_id=1, source_target_pairs={{24,0},{0,8},{8,16},{16,24},{25,1},{1,9},{9,17},{17,25},{26,2},{2,... | collective-permute-start | bytes 983048 | tf_op jit(solution)/shard_map/ppermute | solution.py:19
  117.9 4.4 %collective-permute-start.14 = (f32[136,128]{1,0:T(8,128)S(1)}, f32[136,128]{1,0:T(8,128)S(1)}, u32[]{:S(2)}, u32[]{:S(2)}) collective-permute-start(f32[136,128]{1,0:T(8,128)S(1)} %add.43), channel_id=1, source_target_pairs={{4,0},{5,1},{6,2},{7,3},{0,4},{1,5},{2,6},{3,7},{12,8},{13,9},{14,... | collective-permute-start | bytes 208904 | tf_op jit(solution)/shard_map/ppermute | solution.py:26
  119.5 24.0 %collective-permute-start.21 = (bf16[8,128,128]{2,1,0:T(8,128)(2,1)S(1)}, bf16[8,128,128]{2,1,0:T(8,128)(2,1)S(1)}, u32[]{:S(2)}, u32[]{:S(2)}) collective-permute-start(bf16[8,128,128]{2,1,0:T(8,128)(2,1)S(1)} %get-tuple-element.70), channel_id=1, source_target_pairs={{24,0},{0,8},{8,16},{16,24},{25,1},{1,9},{9,17},{17,25},{26,2},{2,... | collective-permute-start | bytes 786440 | tf_op jit(solution)/shard_map/ppermute | solution.py:19
  122.3 5.8 %collective-permute-start.15 = (f32[8,128]{1,0:T(8,128)S(1)}, f32[8,128]{1,0:T(8,128)S(1)}, u32[]{:S(2)}, u32[]{:S(2)}) collective-permute-start(f32[8,128]{1,0:T(8,128)S(1)} %slice.4), channel_id=1, source_target_pairs={{0,24},{24,16},{1,25},{25,17},{2,26},{26,18},{3,27},{27,19},{4,28}... | collective-permute-start | bytes 12296 | tf_op jit(solution)/shard_map/ppermute | solution.py:37
  125.9 2.9 %collective-permute-start.16 = (f32[8,128]{1,0:T(8,128)S(1)}, f32[8,128]{1,0:T(8,128)S(1)}, u32[]{:S(2)}, u32[]{:S(2)}) collective-permute-start(f32[8,128]{1,0:T(8,128)S(1)} %slice.4), channel_id=1, source_target_pairs={{0,16},{8,24},{1,17},{9,25},{2,18},{10,26},{3,19},{11,27},{4,20},{... | collective-permute-start | bytes 12296 | tf_op jit(solution)/shard_map/ppermute | solution.py:37
  128.1 0.7 collective-permute-start.17
  128.8 2.0 %collective-permute-start.18 = (f32[8,128]{1,0:T(8,128)S(1)}, f32[8,128]{1,0:T(8,128)S(1)}, u32[]{:S(2)}, u32[]{:S(2)}) collective-permute-start(f32[8,128]{1,0:T(8,128)S(1)} %add_add_fusion.refs_0_), channel_id=1, source_target_pairs={{24,8},{25,9},{26,10},{27,11},{28,12},{29,13},{30,14},{31,15}} | collective-permute-start | bytes 12296 | tf_op jit(solution)/shard_map/ppermute | solution.py:38
  129.4 14.1 %collective-permute-start.19 = (f32[8,128]{1,0:T(8,128)S(1)}, f32[8,128]{1,0:T(8,128)S(1)}, u32[]{:S(2)}, u32[]{:S(2)}) collective-permute-start(f32[8,128]{1,0:T(8,128)S(1)} %add_add_fusion.refs_0_), channel_id=1, source_target_pairs={{24,0},{25,1},{26,2},{27,3},{28,4},{29,5},{30,6},{31,7}} | collective-permute-start | bytes 12296 | tf_op jit(solution)/shard_map/ppermute | solution.py:38

commit v5 on v4

--- a/solution.py
+++ b/solution.py
@@ -94,7 +94,7 @@
 
 def first_traces(lo, copies, partner_hbm, cmap_hbm, load_hbm, mortar_in, *refs):
     if copies:
-        load, mortar, up, norm, csum, partner, cmap, sems = refs
+        load, mortar, up, low, norm, csum, partner, cmap, sems = refs
     else:
         load, up, low, norm, csum, partner, cmap, sems = refs
         mortar = mortar_in
@@ -126,13 +126,13 @@
         for f in range(faces):
             rows = load[s, f * block : (f + 1) * block, :]
             norm[...] += fold_rows(rows * rows)
-            if copies and f >= half:
+            if copies and (f >= half and s < subs // 2):
                 continue
             trace = jnp.dot(mortar[s, f], rows.astype(BF16), preferred_element_type=F32).astype(BF16)
             if f < half:
                 up[partner[s, f]] = trace
             else:
-                low[s * half + f - half] = trace
+                low[(s - subs // 2 if copies else s) * half + f - half] = trace
         for c in range(corners):
             row = pl.ds(cmap[s, c], 1)
             csum[row, :] += load[s, c * stride : c * stride + 1, :]
@@ -164,6 +164,7 @@
 def first_image(lo, pieces, groups, share, partner_hbm, cmap_hbm, mortar, flipped, stiff, csum, cinv, *refs):
     ins, earlier, refs = refs[: 6 * pieces], refs[6 * pieces], refs[6 * pieces + 1 :]
     loads, norms, ups, lows, aboves, belows = (ins[i * pieces : (i + 1) * pieces] for i in range(6))
+    refs, joined = refs[:-2], refs[-2:]
     tail_in, (send, rest), refs = refs[:-11], refs[-10:-8], refs[-11:-10] + refs[-8:]
     image, low_out, jump_out, sums, cval, up_out, partner, cmap, sems = refs
     subs, order, width = image.shape
@@ -173,6 +174,11 @@
     coarse = csum.shape[0]
     stride = order // corners
     cols = slice(lo, lo + width)
+    if not lo:
+        for whole, start, more in zip(joined, (lows[0], aboves[0]), tail_in):
+            whole[: start.shape[0]] = start[...]
+            whole[start.shape[0] :] = more[...]
+        lows, aboves = joined[:1] + lows[1:], joined[1:] + aboves[1:]
     tables = fetch_tables(partner_hbm, cmap_hbm, partner, cmap, sems)
     for move in tables:
         move.start()
@@ -374,18 +380,19 @@
         return pltpu.VMEM((slots, block, width), BF16)
 
     loads, norms, ups, lows, csums, aboves, belows = [], [], [], [], [], [], []
+    half_traces = pltpu.VMEM((slots // 2, block, LANES), BF16)
     held_mortar = hbm(mortar)
     lead = call(
-        lead_traces, [ANY, ANY], [traces_of(LANES)],
-        [pltpu.VMEM((subs, half * block, LANES), F32), pltpu.VMEM((subs, half, block, block), BF16),
-         dma((2, subs))],
+        lead_traces, [ANY, ANY], [half_traces],
+        [pltpu.VMEM((subs // 2, half * block, LANES), F32),
+         pltpu.VMEM((subs // 2, half, block, block), BF16), dma((2, subs))],
     )(hbm(load), held_mortar)[0]
     aboves.append(vmem(shifted(lead, "sub", -1)))
     for j in range(groups):
         outs = [pltpu.VMEM((subs, order, LANES), F32)]
         if j == 0:
             outs.append(pltpu.VMEM(mortar.shape, BF16))
-        outs += [traces_of(LANES)] * (1 + (j > 0)) + [pltpu.VMEM((8, LANES), F32), pltpu.VMEM((coarse, LANES), F32)]
+        outs += [traces_of(LANES), traces_of(LANES) if j else half_traces] + [pltpu.VMEM((8, LANES), F32), pltpu.VMEM((coarse, LANES), F32)]
         got = list(call(
             functools.partial(first_traces, j * LANES, j == 0),
             [ANY, ANY, ANY, ANY if j == 0 else VMEM], outs, table_scratch + [dma((3, max(subs, 2)))],
@@ -393,11 +400,12 @@
         loads.append(vmem(got.pop(0)))
         if j == 0:
             held_mortar = vmem(got.pop(0))
-        if j == 0:
-            got.insert(1, lead)
+        above = vmem(shifted(got[1], "sub", -1))
         belows.append(vmem(shifted(got[0], "sub", 1)))
         if j:
-            aboves.append(vmem(shifted(got[1], "sub", -1)))
+            aboves.append(above)
+        else:
+            others, got[1] = [vmem(got[1]), above], lead
         ups.append(vmem(got[0]))
         lows.append(vmem(got[1]))
         norms.append(vmem(got[2]))
@@ -421,12 +429,13 @@
         pick = [x[lo:hi] for x in (loads, norms, ups, lows, aboves, belows)]
         got = call(
             functools.partial(first_image, lo * LANES, n, groups, share),
-            [ANY, ANY] + [VMEM] * (6 + 6 * n + k),
+            [ANY, ANY] + [VMEM] * (8 + 6 * n - k),
             [pltpu.VMEM((subs, order, w), F32)]
             + [pltpu.VMEM((size, block, w), BF16) for size in cuts[k]]
             + [traces_of(w)] * 2 + [pltpu.VMEM((coarse + 8, w), F32)],
-            [pltpu.VMEM((coarse, w), F32), traces_of(w)] + table_scratch + [dma((2,))], alias={4: 0},
-        )(*tables, held_mortar, flipped, vmem(stiff[k]), csum, coarse_inv, *sum(pick, []), csum2s[0] if k else csum, *tails)
+            [pltpu.VMEM((coarse, w), F32), traces_of(w)] + table_scratch + [dma((2,))]
+            + [traces_of(LANES)] * 2, alias={4: 0},
+        )(*tables, held_mortar, flipped, vmem(stiff[k]), csum, coarse_inv, *sum(pick, []), csum2s[0] if k else csum, *(tails if k else others))
         image, *up2, low2, jump, sums = got
         images.append(vmem(image))
         low2s.append(vmem(low2))

time: 161 us -> 163 us (1.012)
    ppermute x9 -> x10, starting transfers between devices: 12.9 us -> 14.8 us  [shifted(): return lax.ppermute(block, axis, route)]
    ppermute x9 -> x10, waiting for transfers between devices: 56.6 us -> 57.7 us  [shifted(): return lax.ppermute(block, axis, route)]
  transfers between devices with their start and end apart: 23 -> 24, of which waited for: 14 -> 14; matrix products, arithmetic and copies ran while one was open for 0% -> 0% of each run, Pallas kernels for 10% -> 9%
where the time goes in v5:
time: 163 us; the launch traced here: 162 us
  waiting for transfers between devices  90.9 us (56%)
  starting transfers between devices  32.1 us (20%)
  Pallas kernels  28.5 us (17%)
  blocking collectives  10.4 us (6%)
    ppermute x10, waiting for transfers between devices, shifted(): return lax.ppermute(block, axis, route)  57.7 us
    ppermute x9, waiting for transfers between devices, group_sum(): lax.ppermute(value, axis, [(i ^ hop, i) for i in range(size)])  20.5 us
    ppermute x10, starting transfers between devices, shifted(): return lax.ppermute(block, axis, route)  14.8 us
    ppermute x2, waiting for transfers between devices, hub_sum(): lax.ppermute(total, axis, [(hub, i)])  12.1 us
    all_to_all x1, blocking collectives, iterate(): gathered = lax.all_to_all(spread, ('sub', 'grp'), 0, 0, tiled=True)  10.4 us
    ppermute x9, starting transfers between devices, group_sum(): lax.ppermute(value, axis, [(i ^ hop, i) for i in range(size)])  9.81 us
    pallas_call x1, Pallas kernels, iterate(): call(stiff_product, [ANY] + [VMEM] * (1 + groups), [pltpu.VMEM((subs, ord...  6.66 us
    pallas_call x2, Pallas kernels, iterate(): call(functools.partial(first_image, lo * LANES, n, groups, share), [ANY,...  6.65 us
  transfers between devices with their start and end apart: 24, of which 14 were waited for; matrix products, arithmetic and copies ran while one was open for 0% of the time, Pallas kernels for 9%

profile of v5, /device:TPU:0, one launch (start us, length us, event | category | flops | bytes accessed | tf_op | source)
XLA Modules:
  0.0 162.4 jit_solution(13037684897115882905)
XLA Ops:
  0.0 2.2 %shard_map.64 = (f32[4,1024,128]{2,1,0:T(8,128)S(1)}, bf16[4,8,128,128]{3,2,1,0:T(8,128)(2,1)S(1)}, bf16[16,128,128]{2,1,0:T(8,128)(2,1)S(1)}, bf16[8,128,128]{2...) custom-call(s32[4,4]{1,0:T(4,128)} %partner_hbm.9, s32[4,8]{1,0:T(4,128)} %cmap_hbm.9, ...), custom_call_target="tpu_custom_call" | custom-call | tf_op jit(solution)/shard_map/pallas_call | solution.py:396
  2.2 2.1 %shard_map.65 = (f32[4,1024,128]{2,1,0:T(8,128)S(1)}, bf16[16,128,128]{2,1,0:T(8,128)(2,1)S(1)}, bf16[16,128,128]{2,1,0:T(8,128)(2,1)S(1)}, f32[8,128]{1,0:T(8,128)S(1)}, f32[128,128]{1,0:T(8,128)S(1)}) custom-call(s32[4,4]{1,0:T(4,128)} %partner_hbm.9, s32[4,8]{1,0:T(4,128)} %cmap_hbm.9, f32[4,1024,384]{2,1,0:T(8,128)} %load_hbm.7, ...), custom_call_target="tpu_custom_call" | custom-call | tf_op jit(solution)/shard_map/pallas_call | solution.py:396
  4.3 2.1 %shard_map.66 = (f32[4,1024,128]{2,1,0:T(8,128)S(1)}, bf16[16,128,128]{2,1,0:T(8,128)(2,1)S(1)}, bf16[16,128,128]{2,1,0:T(8,128)(2,1)S(1)}, f32[8,128]{1,0:T(8,128)S(1)}, f32[128,128]{1,0:T(8,128)S(1)}) custom-call(s32[4,4]{1,0:T(4,128)} %partner_hbm.9, s32[4,8]{1,0:T(4,128)} %cmap_hbm.9, f32[4,1024,384]{2,1,0:T(8,128)} %load_hbm.7, ...), custom_call_target="tpu_custom_call" | custom-call | tf_op jit(solution)/shard_map/pallas_call | solution.py:396
  6.4 0.6 collective-permute-start
  7.0 1.1 collective-permute-done
  8.1 2.9 %collective-permute-start.1 = (f32[128,384]{1,0:T(8,128)S(1)}, f32[128,384]{1,0:T(8,128)S(1)}, u32[]{:S(2)}, u32[]{:S(2)}) collective-permute-start(f32[128,384]{1,0:T(8,128)S(1)} %add.36), channel_id=1, source_target_pairs={{2,0},{3,1},{0,2},{1,3},{6,4},{7,5},{4,6},{5,7},{10,8},{11,9},{8,1... | collective-permute-start | bytes 589832 | tf_op jit(solution)/shard_map/ppermute | solution.py:26
  11.0 3.6 %collective-permute-start.4 = (bf16[16,128,128]{2,1,0:T(8,128)(2,1)S(1)}, bf16[16,128,128]{2,1,0:T(8,128)(2,1)S(1)}, u32[]{:S(2)}, u32[]{:S(2)}) collective-permute-start(bf16[16,128,128]{2,1,0:T(8,128)(2,1)S(1)} %get-tuple-element.56.refs_7_), channel_id=1, source_target_pairs={{8,0},{16,8},{24,16},{0,24},{9,1},{17,9},{25,17},{1,25},{10,2},{18... | collective-permute-start | bytes 1572872 | tf_op jit(solution)/shard_map/ppermute | solution.py:19
  14.6 0.0 collective-permute-start.5
  14.6 1.6 collective-permute-done.1
  16.2 1.8 %collective-permute-start.2 = (f32[128,384]{1,0:T(8,128)S(1)}, f32[128,384]{1,0:T(8,128)S(1)}, u32[]{:S(2)}, u32[]{:S(2)}) collective-permute-start(f32[128,384]{1,0:T(8,128)S(1)} %add.37), channel_id=1, source_target_pairs={{4,0},{5,1},{6,2},{7,3},{0,4},{1,5},{2,6},{3,7},{12,8},{13,9},{14,... | collective-permute-start | bytes 589832 | tf_op jit(solution)/shard_map/ppermute | solution.py:26
  18.0 3.6 %collective-permute-start.7 = (bf16[8,128,128]{2,1,0:T(8,128)(2,1)S(1)}, bf16[8,128,128]{2,1,0:T(8,128)(2,1)S(1)}, u32[]{:S(2)}, u32[]{:S(2)}) collective-permute-start(bf16[8,128,128]{2,1,0:T(8,128)(2,1)S(1)} %get-tuple-element.57.refs_13_), channel_id=1, source_target_pairs={{8,0},{16,8},{24,16},{0,24},{9,1},{17,9},{25,17},{1,25},{10,2},{18... | collective-permute-start | bytes 786440 | tf_op jit(solution)/shard_map/ppermute | solution.py:19
  21.7 1.4 shard_map.68.refs_6_
  23.1 0.0 collective-permute-done.2
  23.1 3.1 %collective-permute-start.3 = (bf16[8,128,128]{2,1,0:T(8,128)(2,1)S(1)}, bf16[8,128,128]{2,1,0:T(8,128)(2,1)S(1)}, u32[]{:S(2)}, u32[]{:S(2)}) collective-permute-start(bf16[8,128,128]{2,1,0:T(8,128)(2,1)S(1)} %shard_map.68.refs_6_), channel_id=1, source_target_pairs={{8,0},{16,8},{24,16},{0,24},{9,1},{17,9},{25,17},{1,25},{10,2},{18... | collective-permute-start | bytes 786440 | tf_op jit(solution)/shard_map/ppermute | solution.py:19
  26.2 6.7 %shard_map.67 = (f32[4,1024,256]{2,1,0:T(8,128)S(1)}, f32[4,1024,128]{2,1,0:T(8,128)S(1)}, bf16[4,1024,1024]{2,1,0:T(8,128)(2,1)S(1)}, bf16[4,8,128,128]{3,2,1,0:T(8,128)(2,1)S(1)}) custom-call(bf16[4,1024,1024]{2,1,0:T(8,128)(2,1)} %schur_hbm.1, bf16[4,8,128,128]{3,2,1,0:T(8,128)(2,1)S(1)} %get-tuple-element.42.mortar_in.mortar, ...), custom_call_target="tpu_custom_call" | custom-call | tf_op jit(solution)/shard_map/pallas_call | solution.py:415
  32.9 22.1 %collective-permute-done.7.refs_14_ = bf16[8,128,128]{2,1,0:T(8,128)(2,1)S(1)} collective-permute-done((bf16[8,128,128]{2,1,0:T(8,128)(2,1)S(1)}, bf16[8,128,128]{2,1,0:T(8,128)(2,1)S(1)}, u32[]{:S(2)}, u32[]{:S(2)}) %collective-permute-start.7) | collective-permute-done | bytes 262176 | tf_op jit(solution)/shard_map/ppermute | solution.py:19
  55.0 4.6 %collective-permute-done.3.refs_8_ = bf16[8,128,128]{2,1,0:T(8,128)(2,1)S(1)} collective-permute-done((bf16[8,128,128]{2,1,0:T(8,128)(2,1)S(1)}, bf16[8,128,128]{2,1,0:T(8,128)(2,1)S(1)}, u32[]{:S(2)}, u32[]{:S(2)}) %collective-permute-start.3) | collective-permute-done | bytes 262176 | tf_op jit(solution)/shard_map/ppermute | solution.py:19
  59.5 0.0 collective-permute-done.4.refs_9_
  59.5 0.0 collective-permute-done.6.refs_11_
  59.5 3.8 %shard_map.69 = (f32[4,1024,256]{2,1,0:T(8,128)S(1)}, bf16[15,128,256]{2,1,0:T(8,128)(2,1)S(1)}, bf16[1,128,256]{2,1,0:T(8,128)(2,1)S(1)}, bf16[16,128,256]{2,1,...) custom-call(s32[4,4]{1,0:T(4,128)} %partner_hbm.9, ...), custom_call_target="tpu_custom_call", output_to_operand_aliasing={{0}: (4, {})} | custom-call | tf_op jit(solution)/shard_map/pallas_call | solution.py:430
  63.4 0.5 collective-permute-start.21
  63.9 3.9 %collective-permute-start.11 = (bf16[16,128,128]{2,1,0:T(8,128)(2,1)S(1)}, bf16[16,128,128]{2,1,0:T(8,128)(2,1)S(1)}, u32[]{:S(2)}, u32[]{:S(2)}) collective-permute-start(bf16[16,128,128]{2,1,0:T(8,128)(2,1)S(1)} %get-tuple-element.62.refs_3_), channel_id=1, source_target_pairs={{8,0},{16,8},{24,16},{0,24},{9,1},{17,9},{25,17},{1,25},{10,2},{18... | collective-permute-start | bytes 1572872 | tf_op jit(solution)/shard_map/ppermute | solution.py:19
  67.8 1.4 collective-permute-done.8
  69.2 0.6 collective-permute-start.9
  69.8 5.2 %collective-permute-done.9 = f32[136,256]{1,0:T(8,128)S(1)} collective-permute-done((f32[136,256]{1,0:T(8,128)S(1)}, f32[136,256]{1,0:T(8,128)S(1)}, u32[]{:S(2)}, u32[]{:S(2)}) %collective-permute-start.9) | collective-permute-done | bytes 139296 | tf_op jit(solution)/shard_map/ppermute | solution.py:26
  75.0 1.6 collective-permute-start.10
  76.6 3.5 %collective-permute-done.10 = f32[136,256]{1,0:T(8,128)S(1)} collective-permute-done((f32[136,256]{1,0:T(8,128)S(1)}, f32[136,256]{1,0:T(8,128)S(1)}, u32[]{:S(2)}, u32[]{:S(2)}) %collective-permute-start.10) | collective-permute-done | bytes 139296 | tf_op jit(solution)/shard_map/ppermute | solution.py:26
  80.2 17.3 %collective-permute-done.11.refs_4_ = bf16[16,128,128]{2,1,0:T(8,128)(2,1)S(1)} collective-permute-done((bf16[16,128,128]{2,1,0:T(8,128)(2,1)S(1)}, bf16[16,128,128]{2,1,0:T(8,128)(2,1)S(1)}, u32[]{:S(2)}, u32[]{:S(2)}) %collective-permute-start.11) | collective-permute-done | bytes 524320 | tf_op jit(solution)/shard_map/ppermute | solution.py:19
  97.5 13.7 %collective-permute-done.12.refs_5_ = bf16[16,128,128]{2,1,0:T(8,128)(2,1)S(1)} collective-permute-done((bf16[16,128,128]{2,1,0:T(8,128)(2,1)S(1)}, bf16[16,128,128]{2,1,0:T(8,128)(2,1)S(1)}, u32[]{:S(2)}, u32[]{:S(2)}) %collective-permute-start.12) | collective-permute-done | bytes 524320 | tf_op jit(solution)/shard_map/ppermute | solution.py:19
  111.2 2.8 %shard_map.70 = (f32[4,1024,128]{2,1,0:T(8,128)S(1)}, bf16[8,128,128]{2,1,0:T(8,128)(2,1)S(1)}, bf16[10,128,128]{2,1,0:T(8,128)(2,1)S(1)}, bf16[16,128,128]{2,1,...) custom-call(s32[4,4]{1,0:T(4,128)} %partner_hbm.9, ...), custom_call_target="tpu_custom_call", output_to_operand_aliasing={{0}: (4, {})} | custom-call | tf_op jit(solution)/shard_map/pallas_call | solution.py:430
  114.0 0.1 collective-permute-start.13
  114.1 1.2 collective-permute-done.13
  115.4 0.6 collective-permute-start.14
  116.0 3.8 %collective-permute-done.14 = f32[136,128]{1,0:T(8,128)S(1)} collective-permute-done((f32[136,128]{1,0:T(8,128)S(1)}, f32[136,128]{1,0:T(8,128)S(1)}, u32[]{:S(2)}, u32[]{:S(2)}) %collective-permute-start.14) | collective-permute-done | bytes 69664 | tf_op jit(solution)/shard_map/ppermute | solution.py:26
  119.8 1.6 collective-permute-start.15
  121.4 2.8 %collective-permute-done.15 = f32[136,128]{1,0:T(8,128)S(1)} collective-permute-done((f32[136,128]{1,0:T(8,128)S(1)}, f32[136,128]{1,0:T(8,128)S(1)}, u32[]{:S(2)}, u32[]{:S(2)}) %collective-permute-start.15) | collective-permute-done | bytes 69664 | tf_op jit(solution)/shard_map/ppermute | solution.py:26
  124.2 3.6 %collective-permute-start.16 = (f32[8,128]{1,0:T(8,128)S(1)}, f32[8,128]{1,0:T(8,128)S(1)}, u32[]{:S(2)}, u32[]{:S(2)}) collective-permute-start(f32[8,128]{1,0:T(8,128)S(1)} %slice.4), channel_id=1, source_target_pairs={{0,24},{24,16},{1,25},{25,17},{2,26},{26,18},{3,27},{27,19},{4,28}... | collective-permute-start | bytes 12296 | tf_op jit(solution)/shard_map/ppermute | solution.py:37
  127.8 1.3 collective-permute-start.17
  129.1 0.0 collective-permute-done.16
  129.1 0.7 collective-permute-start.18
  129.8 0.6 collective-permute-done.17
  130.4 0.7 collective-permute-start.19
  131.1 1.3 collective-permute-start.20
  132.4 12.1 %collective-permute-done.20.refs_2_ = f32[8,128]{1,0:T(8,128)S(1)} collective-permute-done((f32[8,128]{1,0:T(8,128)S(1)}, f32[8,128]{1,0:T(8,128)S(1)}, u32[]{:S(2)}, u32[]{:S(2)}) %collective-permute-start.20) | collective-permute-done | bytes 4128 | tf_op jit(solution)/shard_map/ppermute | solution.py:38
  144.5 4.2 %shard_map.71 = (f32[8,384]{1,0:T(8,128)S(1)}, f32[8,384]{1,0:T(8,128)S(1)}, f32[8,384]{1,0:T(8,128)S(1)}) custom-call(f32[8,128]{1,0:T(8,128)S(1)} %add_add_fusion.refs_0_, f32[8,128]{1,0:T(8,128)S(1)} %collective-permute-done.19.refs_1_, f32[8,128]{1,0:T(8,128)S(1)} %collective-permute-done.20.refs_2_, ...), custom_call_target="tpu_custom_call" | custom-call | tf_op jit(solution)/shard_map/pallas_call | solution.py:455
  148.7 0.4 shard_map.72
  149.1 10.4 %all_to_all.5.gathered = f32[32,2,384]{2,1,0:T(2,128)S(1)} all-to-all(f32[32,2,384]{2,1,0:T(2,128)S(1)} %shard_map.72), channel_id=1, replica_groups=mesh['sub'=4,'grp'=8] {'sub','grp'}, dimensions={0} | all-to-all | bytes 196608 | tf_op jit(solution)/shard_map/all_to_all | solution.py:465
  159.5 2.9 %shard_map.73 = f32[4,1024,384]{2,1,0:T(8,128)} custom-call(f32[8,384]{1,0:T(8,128)S(1)} %get-tuple-element.73.total, f32[32,2,384]{2,1,0:T(2,128)S(1)} %all_to_all.5.gathered, f32[4,1024,128]{2,1,0:T(8,128)S(1)} %get-tuple-element.43.refs_0_.refs_10_, f32[4,1024,128]{2,1,0:T(8,128)S(1)} %get-tuple-element.44.refs_1_.refs_11_, ...), custom_call_target="tpu_custom_call" | custom-call | tf_op jit(solution)/shard_map/pallas_call | solution.py:467
  (27 shorter events, 0.2 us)
Async XLA Ops:
  6.4 1.6 %collective-permute-start = (f32[128,384]{1,0:T(8,128)S(1)}, f32[128,384]{1,0:T(8,128)S(1)}, u32[]{:S(2)}, u32[]{:S(2)}) collective-permute-start(f32[128,384]{1,0:T(8,128)S(1)} %constant_dynamic-update-slice_fusion), channel_id=1, source_target_pairs={{1,0},{0,1},{3,2},{2,3},{5,4},{4,5},{7,6},{6,7},{9,8},{8,9},{11,10... | collective-permute-start | bytes 589832 | tf_op jit(solution)/shard_map/ppermute | solution.py:26
  8.1 8.1 %collective-permute-start.1 = (f32[128,384]{1,0:T(8,128)S(1)}, f32[128,384]{1,0:T(8,128)S(1)}, u32[]{:S(2)}, u32[]{:S(2)}) collective-permute-start(f32[128,384]{1,0:T(8,128)S(1)} %add.36), channel_id=1, source_target_pairs={{2,0},{3,1},{0,2},{1,3},{6,4},{7,5},{4,6},{5,7},{10,8},{11,9},{8,1... | collective-permute-start | bytes 589832 | tf_op jit(solution)/shard_map/ppermute | solution.py:26
  11.0 48.5 %collective-permute-start.4 = (bf16[16,128,128]{2,1,0:T(8,128)(2,1)S(1)}, bf16[16,128,128]{2,1,0:T(8,128)(2,1)S(1)}, u32[]{:S(2)}, u32[]{:S(2)}) collective-permute-start(bf16[16,128,128]{2,1,0:T(8,128)(2,1)S(1)} %get-tuple-element.56.refs_7_), channel_id=1, source_target_pairs={{8,0},{16,8},{24,16},{0,24},{9,1},{17,9},{25,17},{1,25},{10,2},{18... | collective-permute-start | bytes 1572872 | tf_op jit(solution)/shard_map/ppermute | solution.py:19
  14.6 45.0 %collective-permute-start.6 = (bf16[16,128,128]{2,1,0:T(8,128)(2,1)S(1)}, bf16[16,128,128]{2,1,0:T(8,128)(2,1)S(1)}, u32[]{:S(2)}, u32[]{:S(2)}) collective-permute-start(bf16[16,128,128]{2,1,0:T(8,128)(2,1)S(1)} %get-tuple-element.55.refs_5_), channel_id=1, source_target_pairs={{24,0},{0,8},{8,16},{16,24},{25,1},{1,9},{9,17},{17,25},{26,2},{2,... | collective-permute-start | bytes 1572872 | tf_op jit(solution)/shard_map/ppermute | solution.py:19
  14.6 45.0 %collective-permute-start.5 = (bf16[16,128,128]{2,1,0:T(8,128)(2,1)S(1)}, bf16[16,128,128]{2,1,0:T(8,128)(2,1)S(1)}, u32[]{:S(2)}, u32[]{:S(2)}) collective-permute-start(bf16[16,128,128]{2,1,0:T(8,128)(2,1)S(1)} %get-tuple-element.54.refs_4_), channel_id=1, source_target_pairs={{24,0},{0,8},{8,16},{16,24},{25,1},{1,9},{9,17},{17,25},{26,2},{2,... | collective-permute-start | bytes 1572872 | tf_op jit(solution)/shard_map/ppermute | solution.py:19
  16.2 6.9 %collective-permute-start.2 = (f32[128,384]{1,0:T(8,128)S(1)}, f32[128,384]{1,0:T(8,128)S(1)}, u32[]{:S(2)}, u32[]{:S(2)}) collective-permute-start(f32[128,384]{1,0:T(8,128)S(1)} %add.37), channel_id=1, source_target_pairs={{4,0},{5,1},{6,2},{7,3},{0,4},{1,5},{2,6},{3,7},{12,8},{13,9},{14,... | collective-permute-start | bytes 589832 | tf_op jit(solution)/shard_map/ppermute | solution.py:26
  18.0 36.9 %collective-permute-start.7 = (bf16[8,128,128]{2,1,0:T(8,128)(2,1)S(1)}, bf16[8,128,128]{2,1,0:T(8,128)(2,1)S(1)}, u32[]{:S(2)}, u32[]{:S(2)}) collective-permute-start(bf16[8,128,128]{2,1,0:T(8,128)(2,1)S(1)} %get-tuple-element.57.refs_13_), channel_id=1, source_target_pairs={{8,0},{16,8},{24,16},{0,24},{9,1},{17,9},{25,17},{1,25},{10,2},{18... | collective-permute-start | bytes 786440 | tf_op jit(solution)/shard_map/ppermute | solution.py:19
  23.1 36.4 %collective-permute-start.3 = (bf16[8,128,128]{2,1,0:T(8,128)(2,1)S(1)}, bf16[8,128,128]{2,1,0:T(8,128)(2,1)S(1)}, u32[]{:S(2)}, u32[]{:S(2)}) collective-permute-start(bf16[8,128,128]{2,1,0:T(8,128)(2,1)S(1)} %shard_map.68.refs_6_), channel_id=1, source_target_pairs={{8,0},{16,8},{24,16},{0,24},{9,1},{17,9},{25,17},{1,25},{10,2},{18... | collective-permute-start | bytes 786440 | tf_op jit(solution)/shard_map/ppermute | solution.py:19
  26.2 33.3 %copy-start = (f32[1,128,128]{2,1,0:T(8,128)S(1)}, f32[1,128,128]{2,1,0:T(8,128)}, u32[]{:S(2)}) copy-start(f32[1,128,128]{2,1,0:T(8,128)} %refs_5_.1) | copy-start | bytes 196612
  63.4 81.1 %collective-permute-start.21 = (bf16[15,128,256]{2,1,0:T(8,128)(2,1)S(1)}, bf16[15,128,256]{2,1,0:T(8,128)(2,1)S(1)}, u32[]{:S(2)}, u32[]{:S(2)}) collective-permute-start(bf16[15,128,256]{2,1,0:T(8,128)(2,1)S(1)} %get-tuple-element.71), channel_id=1, source_target_pairs={{24,0},{0,8},{8,16},{16,24},{25,1},{1,9},{9,17},{17,25},{26,2},{2,... | collective-permute-start | bytes 2949128 | tf_op jit(solution)/shard_map/ppermute | solution.py:19
  63.9 33.6 %collective-permute-start.11 = (bf16[16,128,128]{2,1,0:T(8,128)(2,1)S(1)}, bf16[16,128,128]{2,1,0:T(8,128)(2,1)S(1)}, u32[]{:S(2)}, u32[]{:S(2)}) collective-permute-start(bf16[16,128,128]{2,1,0:T(8,128)(2,1)S(1)} %get-tuple-element.62.refs_3_), channel_id=1, source_target_pairs={{8,0},{16,8},{24,16},{0,24},{9,1},{17,9},{25,17},{1,25},{10,2},{18... | collective-permute-start | bytes 1572872 | tf_op jit(solution)/shard_map/ppermute | solution.py:19
  67.8 43.4 %collective-permute-start.12 = (bf16[16,128,128]{2,1,0:T(8,128)(2,1)S(1)}, bf16[16,128,128]{2,1,0:T(8,128)(2,1)S(1)}, u32[]{:S(2)}, u32[]{:S(2)}) collective-permute-start(bf16[16,128,128]{2,1,0:T(8,128)(2,1)S(1)} %get-tuple-element.61.refs_2_), channel_id=1, source_target_pairs={{24,0},{0,8},{8,16},{16,24},{25,1},{1,9},{9,17},{17,25},{26,2},{2,... | collective-permute-start | bytes 1572872 | tf_op jit(solution)/shard_map/ppermute | solution.py:19
  67.8 1.4 collective-permute-start.8
  69.2 5.8 %collective-permute-start.9 = (f32[136,256]{1,0:T(8,128)S(1)}, f32[136,256]{1,0:T(8,128)S(1)}, u32[]{:S(2)}, u32[]{:S(2)}) collective-permute-start(f32[136,256]{1,0:T(8,128)S(1)} %add.39), channel_id=1, source_target_pairs={{2,0},{3,1},{0,2},{1,3},{6,4},{7,5},{4,6},{5,7},{10,8},{11,9},{8,1... | collective-permute-start | bytes 417800 | tf_op jit(solution)/shard_map/ppermute | solution.py:26
  75.0 5.1 %collective-permute-start.10 = (f32[136,256]{1,0:T(8,128)S(1)}, f32[136,256]{1,0:T(8,128)S(1)}, u32[]{:S(2)}, u32[]{:S(2)}) collective-permute-start(f32[136,256]{1,0:T(8,128)S(1)} %add.40), channel_id=1, source_target_pairs={{4,0},{5,1},{6,2},{7,3},{0,4},{1,5},{2,6},{3,7},{12,8},{13,9},{14,... | collective-permute-start | bytes 417800 | tf_op jit(solution)/shard_map/ppermute | solution.py:26
  114.0 1.3 collective-permute-start.13
  115.4 4.4 %collective-permute-start.14 = (f32[136,128]{1,0:T(8,128)S(1)}, f32[136,128]{1,0:T(8,128)S(1)}, u32[]{:S(2)}, u32[]{:S(2)}) collective-permute-start(f32[136,128]{1,0:T(8,128)S(1)} %add.42), channel_id=1, source_target_pairs={{2,0},{3,1},{0,2},{1,3},{6,4},{7,5},{4,6},{5,7},{10,8},{11,9},{8,1... | collective-permute-start | bytes 208904 | tf_op jit(solution)/shard_map/ppermute | solution.py:26
  116.0 32.7 %collective-permute-start.23 = (bf16[10,128,128]{2,1,0:T(8,128)(2,1)S(1)}, bf16[10,128,128]{2,1,0:T(8,128)(2,1)S(1)}, u32[]{:S(2)}, u32[]{:S(2)}) collective-permute-start(bf16[10,128,128]{2,1,0:T(8,128)(2,1)S(1)} %get-tuple-element.78), channel_id=1, source_target_pairs={{24,0},{0,8},{8,16},{16,24},{25,1},{1,9},{9,17},{17,25},{26,2},{2,... | collective-permute-start | bytes 983048 | tf_op jit(solution)/shard_map/ppermute | solution.py:19
  119.8 4.4 %collective-permute-start.15 = (f32[136,128]{1,0:T(8,128)S(1)}, f32[136,128]{1,0:T(8,128)S(1)}, u32[]{:S(2)}, u32[]{:S(2)}) collective-permute-start(f32[136,128]{1,0:T(8,128)S(1)} %add.43), channel_id=1, source_target_pairs={{4,0},{5,1},{6,2},{7,3},{0,4},{1,5},{2,6},{3,7},{12,8},{13,9},{14,... | collective-permute-start | bytes 208904 | tf_op jit(solution)/shard_map/ppermute | solution.py:26
  121.4 23.1 %collective-permute-start.22 = (bf16[8,128,128]{2,1,0:T(8,128)(2,1)S(1)}, bf16[8,128,128]{2,1,0:T(8,128)(2,1)S(1)}, u32[]{:S(2)}, u32[]{:S(2)}) collective-permute-start(bf16[8,128,128]{2,1,0:T(8,128)(2,1)S(1)} %get-tuple-element.72), channel_id=1, source_target_pairs={{24,0},{0,8},{8,16},{16,24},{25,1},{1,9},{9,17},{17,25},{26,2},{2,... | collective-permute-start | bytes 786440 | tf_op jit(solution)/shard_map/ppermute | solution.py:19
  124.2 4.9 %collective-permute-start.16 = (f32[8,128]{1,0:T(8,128)S(1)}, f32[8,128]{1,0:T(8,128)S(1)}, u32[]{:S(2)}, u32[]{:S(2)}) collective-permute-start(f32[8,128]{1,0:T(8,128)S(1)} %slice.4), channel_id=1, source_target_pairs={{0,24},{24,16},{1,25},{25,17},{2,26},{26,18},{3,27},{27,19},{4,28}... | collective-permute-start | bytes 12296 | tf_op jit(solution)/shard_map/ppermute | solution.py:37
  127.8 2.6 %collective-permute-start.17 = (f32[8,128]{1,0:T(8,128)S(1)}, f32[8,128]{1,0:T(8,128)S(1)}, u32[]{:S(2)}, u32[]{:S(2)}) collective-permute-start(f32[8,128]{1,0:T(8,128)S(1)} %slice.4), channel_id=1, source_target_pairs={{0,16},{8,24},{1,17},{9,25},{2,18},{10,26},{3,19},{11,27},{4,20},{... | collective-permute-start | bytes 12296 | tf_op jit(solution)/shard_map/ppermute | solution.py:37
  129.1 1.3 collective-permute-start.18
  130.4 2.0 %collective-permute-start.19 = (f32[8,128]{1,0:T(8,128)S(1)}, f32[8,128]{1,0:T(8,128)S(1)}, u32[]{:S(2)}, u32[]{:S(2)}) collective-permute-start(f32[8,128]{1,0:T(8,128)S(1)} %add_add_fusion.refs_0_), channel_id=1, source_target_pairs={{24,8},{25,9},{26,10},{27,11},{28,12},{29,13},{30,14},{31,15}} | collective-permute-start | bytes 12296 | tf_op jit(solution)/shard_map/ppermute | solution.py:38
  131.1 13.4 %collective-permute-start.20 = (f32[8,128]{1,0:T(8,128)S(1)}, f32[8,128]{1,0:T(8,128)S(1)}, u32[]{:S(2)}, u32[]{:S(2)}) collective-permute-start(f32[8,128]{1,0:T(8,128)S(1)} %add_add_fusion.refs_0_), channel_id=1, source_target_pairs={{24,0},{25,1},{26,2},{27,3},{28,4},{29,5},{30,6},{31,7}} | collective-permute-start | bytes 12296 | tf_op jit(solution)/shard_map/ppermute | solution.py:38

commit v6 on v5

--- a/solution.py
+++ b/solution.py
@@ -303,7 +303,7 @@
             value = jump[start + k, :, cols].astype(F32) - step * delta
             return acc + fold_rows(value * value)
 
-        acc = lax.fori_loop(max(-start, 0), recv.shape[0], one, acc, unroll=2)
+        acc = lax.fori_loop(max(-start, 0), recv.shape[0], one, acc, unroll=True)
         start += recv.shape[0]
     return acc
 
@@ -314,10 +314,10 @@
     last = group_cols(groups - 1)
     step = total[0:1, last] / total[1:2, last]
     ending = row_sum(energy[:, last] + jump_squares(step, low, jump, recvs, group_cols(0)))
+    sums = jnp.concatenate([row_sum(energy[:, : last.start]), ending], axis=1)
+    rows = jnp.concatenate([row_sum(norm[...]), sums], axis=0)
     for d in range(out.shape[0]):
-        out[d, 0:1, :] = row_sum(norm[...])
-        out[d, 1:2, :] = row_sum(energy[...])
-        out[d, 1:2, last] = ending
+        out[d] = rows
 
 
 def finish(total, gathered, *refs):
@@ -422,7 +422,7 @@
     bounds = ((0, groups - 1), (groups - 1, groups))
     share = 1.0 / lax.axis_size("grp")
     images, jumps, low2s, recvs, csum2s, tails = [], [], [], [], [], []
-    tail, lead_slots = slots // 16, 6 * slots // 16
+    tail, lead_slots = slots // 16, 7 * slots // 16
     cuts = ((slots - tail, tail), ((groups - 1) * tail + lead_slots, slots - lead_slots))
     for k, (lo, hi) in enumerate(bounds):
         n, w = hi - lo, (hi - lo) * LANES

time: 163 us -> 166 us (1.018)
  waiting for transfers between devices: 90.9 us -> 94.8 us
    ppermute x3, waiting for transfers between devices: 0.65 us -> 4.19 us  [hub_sum(): total = total + lax.ppermute(value, axis, route)]
where the time goes in v6:
time: 166 us
  waiting for transfers between devices  94.8 us (57%)
  starting transfers between devices  32.4 us (20%)
  Pallas kernels  28.5 us (17%)
  blocking collectives  9.48 us (6%)
    ppermute x10, waiting for transfers between devices, shifted(): return lax.ppermute(block, axis, route)  57.7 us
    ppermute x9, waiting for transfers between devices, group_sum(): lax.ppermute(value, axis, [(i ^ hop, i) for i in range(size)])  20.1 us
    ppermute x10, starting transfers between devices, shifted(): return lax.ppermute(block, axis, route)  15.1 us
    ppermute x2, waiting for transfers between devices, hub_sum(): lax.ppermute(total, axis, [(hub, i)])  12.7 us
    ppermute x9, starting transfers between devices, group_sum(): lax.ppermute(value, axis, [(i ^ hop, i) for i in range(size)])  9.81 us
    all_to_all x1, blocking collectives, iterate(): gathered = lax.all_to_all(spread, ('sub', 'grp'), 0, 0, tiled=True)  9.48 us
    pallas_call x1, Pallas kernels, iterate(): call(stiff_product, [ANY] + [VMEM] * (1 + groups), [pltpu.VMEM((subs, ord...  6.66 us
    pallas_call x2, Pallas kernels, iterate(): call(functools.partial(first_image, lo * LANES, n, groups, share), [ANY,...  6.65 us
  transfers between devices with their start and end apart: 24, of which 14 were waited for; matrix products, arithmetic and copies ran while one was open for 0% of the time, Pallas kernels for 9%

profile of v6, /device:TPU:0, one launch (start us, length us, event | category | flops | bytes accessed | tf_op | source)
XLA Modules:
  0.0 165.6 jit_solution(6107609307335572653)
XLA Ops:
  0.0 2.2 %shard_map.64 = (f32[4,1024,128]{2,1,0:T(8,128)S(1)}, bf16[4,8,128,128]{3,2,1,0:T(8,128)(2,1)S(1)}, bf16[16,128,128]{2,1,0:T(8,128)(2,1)S(1)}, bf16[8,128,128]{2...) custom-call(s32[4,4]{1,0:T(4,128)} %partner_hbm.9, s32[4,8]{1,0:T(4,128)} %cmap_hbm.9, ...), custom_call_target="tpu_custom_call" | custom-call | tf_op jit(solution)/shard_map/pallas_call | solution.py:396
  2.2 2.1 %shard_map.65 = (f32[4,1024,128]{2,1,0:T(8,128)S(1)}, bf16[16,128,128]{2,1,0:T(8,128)(2,1)S(1)}, bf16[16,128,128]{2,1,0:T(8,128)(2,1)S(1)}, f32[8,128]{1,0:T(8,128)S(1)}, f32[128,128]{1,0:T(8,128)S(1)}) custom-call(s32[4,4]{1,0:T(4,128)} %partner_hbm.9, s32[4,8]{1,0:T(4,128)} %cmap_hbm.9, f32[4,1024,384]{2,1,0:T(8,128)} %load_hbm.7, ...), custom_call_target="tpu_custom_call" | custom-call | tf_op jit(solution)/shard_map/pallas_call | solution.py:396
  4.3 2.1 %shard_map.66 = (f32[4,1024,128]{2,1,0:T(8,128)S(1)}, bf16[16,128,128]{2,1,0:T(8,128)(2,1)S(1)}, bf16[16,128,128]{2,1,0:T(8,128)(2,1)S(1)}, f32[8,128]{1,0:T(8,128)S(1)}, f32[128,128]{1,0:T(8,128)S(1)}) custom-call(s32[4,4]{1,0:T(4,128)} %partner_hbm.9, s32[4,8]{1,0:T(4,128)} %cmap_hbm.9, f32[4,1024,384]{2,1,0:T(8,128)} %load_hbm.7, ...), custom_call_target="tpu_custom_call" | custom-call | tf_op jit(solution)/shard_map/pallas_call | solution.py:396
  6.4 0.6 collective-permute-start
  7.0 1.1 collective-permute-done
  8.1 2.9 %collective-permute-start.1 = (f32[128,384]{1,0:T(8,128)S(1)}, f32[128,384]{1,0:T(8,128)S(1)}, u32[]{:S(2)}, u32[]{:S(2)}) collective-permute-start(f32[128,384]{1,0:T(8,128)S(1)} %add.36), channel_id=1, source_target_pairs={{2,0},{3,1},{0,2},{1,3},{6,4},{7,5},{4,6},{5,7},{10,8},{11,9},{8,1... | collective-permute-start | bytes 589832 | tf_op jit(solution)/shard_map/ppermute | solution.py:26
  11.0 3.6 %collective-permute-start.4 = (bf16[16,128,128]{2,1,0:T(8,128)(2,1)S(1)}, bf16[16,128,128]{2,1,0:T(8,128)(2,1)S(1)}, u32[]{:S(2)}, u32[]{:S(2)}) collective-permute-start(bf16[16,128,128]{2,1,0:T(8,128)(2,1)S(1)} %get-tuple-element.56.refs_7_), channel_id=1, source_target_pairs={{8,0},{16,8},{24,16},{0,24},{9,1},{17,9},{25,17},{1,25},{10,2},{18... | collective-permute-start | bytes 1572872 | tf_op jit(solution)/shard_map/ppermute | solution.py:19
  14.6 0.0 collective-permute-start.5
  14.6 1.6 collective-permute-done.1
  16.2 1.8 %collective-permute-start.2 = (f32[128,384]{1,0:T(8,128)S(1)}, f32[128,384]{1,0:T(8,128)S(1)}, u32[]{:S(2)}, u32[]{:S(2)}) collective-permute-start(f32[128,384]{1,0:T(8,128)S(1)} %add.37), channel_id=1, source_target_pairs={{4,0},{5,1},{6,2},{7,3},{0,4},{1,5},{2,6},{3,7},{12,8},{13,9},{14,... | collective-permute-start | bytes 589832 | tf_op jit(solution)/shard_map/ppermute | solution.py:26
  18.0 3.6 %collective-permute-start.7 = (bf16[8,128,128]{2,1,0:T(8,128)(2,1)S(1)}, bf16[8,128,128]{2,1,0:T(8,128)(2,1)S(1)}, u32[]{:S(2)}, u32[]{:S(2)}) collective-permute-start(bf16[8,128,128]{2,1,0:T(8,128)(2,1)S(1)} %get-tuple-element.57.refs_13_), channel_id=1, source_target_pairs={{8,0},{16,8},{24,16},{0,24},{9,1},{17,9},{25,17},{1,25},{10,2},{18... | collective-permute-start | bytes 786440 | tf_op jit(solution)/shard_map/ppermute | solution.py:19
  21.7 1.4 shard_map.68.refs_6_
  23.1 0.0 collective-permute-done.2
  23.1 3.1 %collective-permute-start.3 = (bf16[8,128,128]{2,1,0:T(8,128)(2,1)S(1)}, bf16[8,128,128]{2,1,0:T(8,128)(2,1)S(1)}, u32[]{:S(2)}, u32[]{:S(2)}) collective-permute-start(bf16[8,128,128]{2,1,0:T(8,128)(2,1)S(1)} %shard_map.68.refs_6_), channel_id=1, source_target_pairs={{8,0},{16,8},{24,16},{0,24},{9,1},{17,9},{25,17},{1,25},{10,2},{18... | collective-permute-start | bytes 786440 | tf_op jit(solution)/shard_map/ppermute | solution.py:19
  26.2 6.7 %shard_map.67 = (f32[4,1024,256]{2,1,0:T(8,128)S(1)}, f32[4,1024,128]{2,1,0:T(8,128)S(1)}, bf16[4,1024,1024]{2,1,0:T(8,128)(2,1)S(1)}, bf16[4,8,128,128]{3,2,1,0:T(8,128)(2,1)S(1)}) custom-call(bf16[4,1024,1024]{2,1,0:T(8,128)(2,1)} %schur_hbm.1, bf16[4,8,128,128]{3,2,1,0:T(8,128)(2,1)S(1)} %get-tuple-element.42.mortar_in.mortar, ...), custom_call_target="tpu_custom_call" | custom-call | tf_op jit(solution)/shard_map/pallas_call | solution.py:415
  32.9 22.1 %collective-permute-done.7.refs_14_ = bf16[8,128,128]{2,1,0:T(8,128)(2,1)S(1)} collective-permute-done((bf16[8,128,128]{2,1,0:T(8,128)(2,1)S(1)}, bf16[8,128,128]{2,1,0:T(8,128)(2,1)S(1)}, u32[]{:S(2)}, u32[]{:S(2)}) %collective-permute-start.7) | collective-permute-done | bytes 262176 | tf_op jit(solution)/shard_map/ppermute | solution.py:19
  55.0 4.6 %collective-permute-done.3.refs_8_ = bf16[8,128,128]{2,1,0:T(8,128)(2,1)S(1)} collective-permute-done((bf16[8,128,128]{2,1,0:T(8,128)(2,1)S(1)}, bf16[8,128,128]{2,1,0:T(8,128)(2,1)S(1)}, u32[]{:S(2)}, u32[]{:S(2)}) %collective-permute-start.3) | collective-permute-done | bytes 262176 | tf_op jit(solution)/shard_map/ppermute | solution.py:19
  59.5 0.0 collective-permute-done.4.refs_9_
  59.5 0.0 collective-permute-done.6.refs_11_
  59.5 3.8 %shard_map.69 = (f32[4,1024,256]{2,1,0:T(8,128)S(1)}, bf16[15,128,256]{2,1,0:T(8,128)(2,1)S(1)}, bf16[1,128,256]{2,1,0:T(8,128)(2,1)S(1)}, bf16[16,128,256]{2,1,...) custom-call(s32[4,4]{1,0:T(4,128)} %partner_hbm.9, ...), custom_call_target="tpu_custom_call", output_to_operand_aliasing={{0}: (4, {})} | custom-call | tf_op jit(solution)/shard_map/pallas_call | solution.py:430
  63.4 0.5 collective-permute-start.21
  63.9 3.9 %collective-permute-start.11 = (bf16[16,128,128]{2,1,0:T(8,128)(2,1)S(1)}, bf16[16,128,128]{2,1,0:T(8,128)(2,1)S(1)}, u32[]{:S(2)}, u32[]{:S(2)}) collective-permute-start(bf16[16,128,128]{2,1,0:T(8,128)(2,1)S(1)} %get-tuple-element.62.refs_3_), channel_id=1, source_target_pairs={{8,0},{16,8},{24,16},{0,24},{9,1},{17,9},{25,17},{1,25},{10,2},{18... | collective-permute-start | bytes 1572872 | tf_op jit(solution)/shard_map/ppermute | solution.py:19
  67.8 1.4 collective-permute-done.8
  69.2 0.6 collective-permute-start.9
  69.8 5.2 %collective-permute-done.9 = f32[136,256]{1,0:T(8,128)S(1)} collective-permute-done((f32[136,256]{1,0:T(8,128)S(1)}, f32[136,256]{1,0:T(8,128)S(1)}, u32[]{:S(2)}, u32[]{:S(2)}) %collective-permute-start.9) | collective-permute-done | bytes 139296 | tf_op jit(solution)/shard_map/ppermute | solution.py:26
  75.0 1.6 collective-permute-start.10
  76.6 3.5 %collective-permute-done.10 = f32[136,256]{1,0:T(8,128)S(1)} collective-permute-done((f32[136,256]{1,0:T(8,128)S(1)}, f32[136,256]{1,0:T(8,128)S(1)}, u32[]{:S(2)}, u32[]{:S(2)}) %collective-permute-start.10) | collective-permute-done | bytes 139296 | tf_op jit(solution)/shard_map/ppermute | solution.py:26
  80.2 17.3 %collective-permute-done.11.refs_4_ = bf16[16,128,128]{2,1,0:T(8,128)(2,1)S(1)} collective-permute-done((bf16[16,128,128]{2,1,0:T(8,128)(2,1)S(1)}, bf16[16,128,128]{2,1,0:T(8,128)(2,1)S(1)}, u32[]{:S(2)}, u32[]{:S(2)}) %collective-permute-start.11) | collective-permute-done | bytes 524320 | tf_op jit(solution)/shard_map/ppermute | solution.py:19
  97.5 13.7 %collective-permute-done.12.refs_5_ = bf16[16,128,128]{2,1,0:T(8,128)(2,1)S(1)} collective-permute-done((bf16[16,128,128]{2,1,0:T(8,128)(2,1)S(1)}, bf16[16,128,128]{2,1,0:T(8,128)(2,1)S(1)}, u32[]{:S(2)}, u32[]{:S(2)}) %collective-permute-start.12) | collective-permute-done | bytes 524320 | tf_op jit(solution)/shard_map/ppermute | solution.py:19
  111.2 2.8 %shard_map.70 = (f32[4,1024,128]{2,1,0:T(8,128)S(1)}, bf16[9,128,128]{2,1,0:T(8,128)(2,1)S(1)}, bf16[9,128,128]{2,1,0:T(8,128)(2,1)S(1)}, bf16[16,128,128]{2,1,0...) custom-call(s32[4,4]{1,0:T(4,128)} %partner_hbm.9, ...), custom_call_target="tpu_custom_call", output_to_operand_aliasing={{0}: (4, {})} | custom-call | tf_op jit(solution)/shard_map/pallas_call | solution.py:430
  114.0 0.1 collective-permute-start.13
  114.1 1.2 collective-permute-done.13
  115.4 0.6 collective-permute-start.14
  116.0 3.8 %collective-permute-done.14 = f32[136,128]{1,0:T(8,128)S(1)} collective-permute-done((f32[136,128]{1,0:T(8,128)S(1)}, f32[136,128]{1,0:T(8,128)S(1)}, u32[]{:S(2)}, u32[]{:S(2)}) %collective-permute-start.14) | collective-permute-done | bytes 69664 | tf_op jit(solution)/shard_map/ppermute | solution.py:26
  119.8 1.6 collective-permute-start.15
  121.4 0.4 collective-permute-start.23
  121.7 2.4 %collective-permute-done.15 = f32[136,128]{1,0:T(8,128)S(1)} collective-permute-done((f32[136,128]{1,0:T(8,128)S(1)}, f32[136,128]{1,0:T(8,128)S(1)}, u32[]{:S(2)}, u32[]{:S(2)}) %collective-permute-start.15) | collective-permute-done | bytes 69664 | tf_op jit(solution)/shard_map/ppermute | solution.py:26
  124.2 3.6 %collective-permute-start.16 = (f32[8,128]{1,0:T(8,128)S(1)}, f32[8,128]{1,0:T(8,128)S(1)}, u32[]{:S(2)}, u32[]{:S(2)}) collective-permute-start(f32[8,128]{1,0:T(8,128)S(1)} %slice.4), channel_id=1, source_target_pairs={{0,24},{24,16},{1,25},{25,17},{2,26},{26,18},{3,27},{27,19},{4,28}... | collective-permute-start | bytes 12296 | tf_op jit(solution)/shard_map/ppermute | solution.py:37
  127.8 1.3 collective-permute-start.17
  129.1 4.2 %collective-permute-done.16 = f32[8,128]{1,0:T(8,128)S(1)} collective-permute-done((f32[8,128]{1,0:T(8,128)S(1)}, f32[8,128]{1,0:T(8,128)S(1)}, u32[]{:S(2)}, u32[]{:S(2)}) %collective-permute-start.16) | collective-permute-done | bytes 4128 | tf_op jit(solution)/shard_map/ppermute | solution.py:37
  133.3 0.6 collective-permute-start.18
  134.0 0.7 collective-permute-start.19
  134.6 1.3 collective-permute-start.20
  135.9 12.7 %collective-permute-done.20.refs_2_ = f32[8,128]{1,0:T(8,128)S(1)} collective-permute-done((f32[8,128]{1,0:T(8,128)S(1)}, f32[8,128]{1,0:T(8,128)S(1)}, u32[]{:S(2)}, u32[]{:S(2)}) %collective-permute-start.20) | collective-permute-done | bytes 4128 | tf_op jit(solution)/shard_map/ppermute | solution.py:38
  148.7 4.2 %shard_map.71 = (f32[8,384]{1,0:T(8,128)S(1)}, f32[8,384]{1,0:T(8,128)S(1)}, f32[8,384]{1,0:T(8,128)S(1)}) custom-call(f32[8,128]{1,0:T(8,128)S(1)} %add_add_fusion.refs_0_, f32[8,128]{1,0:T(8,128)S(1)} %collective-permute-done.19.refs_1_, f32[8,128]{1,0:T(8,128)S(1)} %collective-permute-done.20.refs_2_, ...), custom_call_target="tpu_custom_call" | custom-call | tf_op jit(solution)/shard_map/pallas_call | solution.py:455
  152.9 0.3 shard_map.72
  153.2 9.5 %all_to_all.5.gathered = f32[32,2,384]{2,1,0:T(2,128)S(1)} all-to-all(f32[32,2,384]{2,1,0:T(2,128)S(1)} %shard_map.72), channel_id=1, replica_groups=mesh['sub'=4,'grp'=8] {'sub','grp'}, dimensions={0} | all-to-all | bytes 196608 | tf_op jit(solution)/shard_map/all_to_all | solution.py:465
  162.7 2.9 %shard_map.73 = f32[4,1024,384]{2,1,0:T(8,128)} custom-call(f32[8,384]{1,0:T(8,128)S(1)} %get-tuple-element.73.total, f32[32,2,384]{2,1,0:T(2,128)S(1)} %all_to_all.5.gathered, f32[4,1024,128]{2,1,0:T(8,128)S(1)} %get-tuple-element.43.refs_0_.refs_10_, f32[4,1024,128]{2,1,0:T(8,128)S(1)} %get-tuple-element.44.refs_1_.refs_11_, ...), custom_call_target="tpu_custom_call" | custom-call | tf_op jit(solution)/shard_map/pallas_call | solution.py:467
  (27 shorter events, 0.2 us)
Async XLA Ops:
  6.4 1.6 collective-permute-start
  8.1 8.1 %collective-permute-start.1 = (f32[128,384]{1,0:T(8,128)S(1)}, f32[128,384]{1,0:T(8,128)S(1)}, u32[]{:S(2)}, u32[]{:S(2)}) collective-permute-start(f32[128,384]{1,0:T(8,128)S(1)} %add.36), channel_id=1, source_target_pairs={{2,0},{3,1},{0,2},{1,3},{6,4},{7,5},{4,6},{5,7},{10,8},{11,9},{8,1... | collective-permute-start | bytes 589832 | tf_op jit(solution)/shard_map/ppermute | solution.py:26
  11.0 48.5 %collective-permute-start.4 = (bf16[16,128,128]{2,1,0:T(8,128)(2,1)S(1)}, bf16[16,128,128]{2,1,0:T(8,128)(2,1)S(1)}, u32[]{:S(2)}, u32[]{:S(2)}) collective-permute-start(bf16[16,128,128]{2,1,0:T(8,128)(2,1)S(1)} %get-tuple-element.56.refs_7_), channel_id=1, source_target_pairs={{8,0},{16,8},{24,16},{0,24},{9,1},{17,9},{25,17},{1,25},{10,2},{18... | collective-permute-start | bytes 1572872 | tf_op jit(solution)/shard_map/ppermute | solution.py:19
  14.6 45.0 %collective-permute-start.6 = (bf16[16,128,128]{2,1,0:T(8,128)(2,1)S(1)}, bf16[16,128,128]{2,1,0:T(8,128)(2,1)S(1)}, u32[]{:S(2)}, u32[]{:S(2)}) collective-permute-start(bf16[16,128,128]{2,1,0:T(8,128)(2,1)S(1)} %get-tuple-element.55.refs_5_), channel_id=1, source_target_pairs={{24,0},{0,8},{8,16},{16,24},{25,1},{1,9},{9,17},{17,25},{26,2},{2,... | collective-permute-start | bytes 1572872 | tf_op jit(solution)/shard_map/ppermute | solution.py:19
  14.6 45.0 %collective-permute-start.5 = (bf16[16,128,128]{2,1,0:T(8,128)(2,1)S(1)}, bf16[16,128,128]{2,1,0:T(8,128)(2,1)S(1)}, u32[]{:S(2)}, u32[]{:S(2)}) collective-permute-start(bf16[16,128,128]{2,1,0:T(8,128)(2,1)S(1)} %get-tuple-element.54.refs_4_), channel_id=1, source_target_pairs={{24,0},{0,8},{8,16},{16,24},{25,1},{1,9},{9,17},{17,25},{26,2},{2,... | collective-permute-start | bytes 1572872 | tf_op jit(solution)/shard_map/ppermute | solution.py:19
  16.2 6.9 %collective-permute-start.2 = (f32[128,384]{1,0:T(8,128)S(1)}, f32[128,384]{1,0:T(8,128)S(1)}, u32[]{:S(2)}, u32[]{:S(2)}) collective-permute-start(f32[128,384]{1,0:T(8,128)S(1)} %add.37), channel_id=1, source_target_pairs={{4,0},{5,1},{6,2},{7,3},{0,4},{1,5},{2,6},{3,7},{12,8},{13,9},{14,... | collective-permute-start | bytes 589832 | tf_op jit(solution)/shard_map/ppermute | solution.py:26
  18.0 36.9 %collective-permute-start.7 = (bf16[8,128,128]{2,1,0:T(8,128)(2,1)S(1)}, bf16[8,128,128]{2,1,0:T(8,128)(2,1)S(1)}, u32[]{:S(2)}, u32[]{:S(2)}) collective-permute-start(bf16[8,128,128]{2,1,0:T(8,128)(2,1)S(1)} %get-tuple-element.57.refs_13_), channel_id=1, source_target_pairs={{8,0},{16,8},{24,16},{0,24},{9,1},{17,9},{25,17},{1,25},{10,2},{18... | collective-permute-start | bytes 786440 | tf_op jit(solution)/shard_map/ppermute | solution.py:19
  23.1 36.4 %collective-permute-start.3 = (bf16[8,128,128]{2,1,0:T(8,128)(2,1)S(1)}, bf16[8,128,128]{2,1,0:T(8,128)(2,1)S(1)}, u32[]{:S(2)}, u32[]{:S(2)}) collective-permute-start(bf16[8,128,128]{2,1,0:T(8,128)(2,1)S(1)} %shard_map.68.refs_6_), channel_id=1, source_target_pairs={{8,0},{16,8},{24,16},{0,24},{9,1},{17,9},{25,17},{1,25},{10,2},{18... | collective-permute-start | bytes 786440 | tf_op jit(solution)/shard_map/ppermute | solution.py:19
  26.2 33.3 %copy-start = (f32[1,128,128]{2,1,0:T(8,128)S(1)}, f32[1,128,128]{2,1,0:T(8,128)}, u32[]{:S(2)}) copy-start(f32[1,128,128]{2,1,0:T(8,128)} %refs_5_.1) | copy-start | bytes 196612
  63.4 85.3 %collective-permute-start.21 = (bf16[15,128,256]{2,1,0:T(8,128)(2,1)S(1)}, bf16[15,128,256]{2,1,0:T(8,128)(2,1)S(1)}, u32[]{:S(2)}, u32[]{:S(2)}) collective-permute-start(bf16[15,128,256]{2,1,0:T(8,128)(2,1)S(1)} %get-tuple-element.71), channel_id=1, source_target_pairs={{24,0},{0,8},{8,16},{16,24},{25,1},{1,9},{9,17},{17,25},{26,2},{2,... | collective-permute-start | bytes 2949128 | tf_op jit(solution)/shard_map/ppermute | solution.py:19
  63.9 33.6 %collective-permute-start.11 = (bf16[16,128,128]{2,1,0:T(8,128)(2,1)S(1)}, bf16[16,128,128]{2,1,0:T(8,128)(2,1)S(1)}, u32[]{:S(2)}, u32[]{:S(2)}) collective-permute-start(bf16[16,128,128]{2,1,0:T(8,128)(2,1)S(1)} %get-tuple-element.62.refs_3_), channel_id=1, source_target_pairs={{8,0},{16,8},{24,16},{0,24},{9,1},{17,9},{25,17},{1,25},{10,2},{18... | collective-permute-start | bytes 1572872 | tf_op jit(solution)/shard_map/ppermute | solution.py:19
  67.8 43.4 %collective-permute-start.12 = (bf16[16,128,128]{2,1,0:T(8,128)(2,1)S(1)}, bf16[16,128,128]{2,1,0:T(8,128)(2,1)S(1)}, u32[]{:S(2)}, u32[]{:S(2)}) collective-permute-start(bf16[16,128,128]{2,1,0:T(8,128)(2,1)S(1)} %get-tuple-element.61.refs_2_), channel_id=1, source_target_pairs={{24,0},{0,8},{8,16},{16,24},{25,1},{1,9},{9,17},{17,25},{26,2},{2,... | collective-permute-start | bytes 1572872 | tf_op jit(solution)/shard_map/ppermute | solution.py:19
  67.8 1.4 collective-permute-start.8
  69.2 5.8 %collective-permute-start.9 = (f32[136,256]{1,0:T(8,128)S(1)}, f32[136,256]{1,0:T(8,128)S(1)}, u32[]{:S(2)}, u32[]{:S(2)}) collective-permute-start(f32[136,256]{1,0:T(8,128)S(1)} %add.39), channel_id=1, source_target_pairs={{2,0},{3,1},{0,2},{1,3},{6,4},{7,5},{4,6},{5,7},{10,8},{11,9},{8,1... | collective-permute-start | bytes 417800 | tf_op jit(solution)/shard_map/ppermute | solution.py:26
  75.0 5.1 %collective-permute-start.10 = (f32[136,256]{1,0:T(8,128)S(1)}, f32[136,256]{1,0:T(8,128)S(1)}, u32[]{:S(2)}, u32[]{:S(2)}) collective-permute-start(f32[136,256]{1,0:T(8,128)S(1)} %add.40), channel_id=1, source_target_pairs={{4,0},{5,1},{6,2},{7,3},{0,4},{1,5},{2,6},{3,7},{12,8},{13,9},{14,... | collective-permute-start | bytes 417800 | tf_op jit(solution)/shard_map/ppermute | solution.py:26
  114.0 1.3 collective-permute-start.13
  115.4 4.4 %collective-permute-start.14 = (f32[136,128]{1,0:T(8,128)S(1)}, f32[136,128]{1,0:T(8,128)S(1)}, u32[]{:S(2)}, u32[]{:S(2)}) collective-permute-start(f32[136,128]{1,0:T(8,128)S(1)} %add.42), channel_id=1, source_target_pairs={{2,0},{3,1},{0,2},{1,3},{6,4},{7,5},{4,6},{5,7},{10,8},{11,9},{8,1... | collective-permute-start | bytes 208904 | tf_op jit(solution)/shard_map/ppermute | solution.py:26
  119.8 4.4 %collective-permute-start.15 = (f32[136,128]{1,0:T(8,128)S(1)}, f32[136,128]{1,0:T(8,128)S(1)}, u32[]{:S(2)}, u32[]{:S(2)}) collective-permute-start(f32[136,128]{1,0:T(8,128)S(1)} %add.43), channel_id=1, source_target_pairs={{4,0},{5,1},{6,2},{7,3},{0,4},{1,5},{2,6},{3,7},{12,8},{13,9},{14,... | collective-permute-start | bytes 208904 | tf_op jit(solution)/shard_map/ppermute | solution.py:26
  121.4 27.3 %collective-permute-start.22 = (bf16[9,128,128]{2,1,0:T(8,128)(2,1)S(1)}, bf16[9,128,128]{2,1,0:T(8,128)(2,1)S(1)}, u32[]{:S(2)}, u32[]{:S(2)}) collective-permute-start(bf16[9,128,128]{2,1,0:T(8,128)(2,1)S(1)} %get-tuple-element.72), channel_id=1, source_target_pairs={{24,0},{0,8},{8,16},{16,24},{25,1},{1,9},{9,17},{17,25},{26,2},{2,... | collective-permute-start | bytes 884744 | tf_op jit(solution)/shard_map/ppermute | solution.py:19
  121.4 31.5 %collective-permute-start.23 = (bf16[9,128,128]{2,1,0:T(8,128)(2,1)S(1)}, bf16[9,128,128]{2,1,0:T(8,128)(2,1)S(1)}, u32[]{:S(2)}, u32[]{:S(2)}) collective-permute-start(bf16[9,128,128]{2,1,0:T(8,128)(2,1)S(1)} %get-tuple-element.78), channel_id=1, source_target_pairs={{24,0},{0,8},{8,16},{16,24},{25,1},{1,9},{9,17},{17,25},{26,2},{2,... | collective-permute-start | bytes 884744 | tf_op jit(solution)/shard_map/ppermute | solution.py:19
  124.2 9.1 %collective-permute-start.16 = (f32[8,128]{1,0:T(8,128)S(1)}, f32[8,128]{1,0:T(8,128)S(1)}, u32[]{:S(2)}, u32[]{:S(2)}) collective-permute-start(f32[8,128]{1,0:T(8,128)S(1)} %slice.4), channel_id=1, source_target_pairs={{0,24},{24,16},{1,25},{25,17},{2,26},{26,18},{3,27},{27,19},{4,28}... | collective-permute-start | bytes 12296 | tf_op jit(solution)/shard_map/ppermute | solution.py:37
  127.8 6.1 %collective-permute-start.17 = (f32[8,128]{1,0:T(8,128)S(1)}, f32[8,128]{1,0:T(8,128)S(1)}, u32[]{:S(2)}, u32[]{:S(2)}) collective-permute-start(f32[8,128]{1,0:T(8,128)S(1)} %slice.4), channel_id=1, source_target_pairs={{0,16},{8,24},{1,17},{9,25},{2,18},{10,26},{3,19},{11,27},{4,20},{... | collective-permute-start | bytes 12296 | tf_op jit(solution)/shard_map/ppermute | solution.py:37
  133.3 0.7 collective-permute-start.18
  134.0 2.0 %collective-permute-start.19 = (f32[8,128]{1,0:T(8,128)S(1)}, f32[8,128]{1,0:T(8,128)S(1)}, u32[]{:S(2)}, u32[]{:S(2)}) collective-permute-start(f32[8,128]{1,0:T(8,128)S(1)} %add_add_fusion.refs_0_), channel_id=1, source_target_pairs={{24,8},{25,9},{26,10},{27,11},{28,12},{29,13},{30,14},{31,15}} | collective-permute-start | bytes 12296 | tf_op jit(solution)/shard_map/ppermute | solution.py:38
  134.6 14.1 %collective-permute-start.20 = (f32[8,128]{1,0:T(8,128)S(1)}, f32[8,128]{1,0:T(8,128)S(1)}, u32[]{:S(2)}, u32[]{:S(2)}) collective-permute-start(f32[8,128]{1,0:T(8,128)S(1)} %add_add_fusion.refs_0_), channel_id=1, source_target_pairs={{24,0},{25,1},{26,2},{27,3},{28,4},{29,5},{30,6},{31,7}} | collective-permute-start | bytes 12296 | tf_op jit(solution)/shard_map/ppermute | solution.py:38
